TPU v7x, 512 devices: a whole 4x8x8 slice. The times are simulated.
512 devices in a mesh: dp: 8 (over x, y_hi), ctx: 64 (over y_lo, z, core).
Axes of the slice: x: 4, y: 8 (y_hi: 2, y_lo: 4; y = y_hi * 4 + y_lo), z: 8, core: 2. Of those that a mesh axis runs over, the one named last changes fastest.
Arguments:
- tile_features: bfloat16 [8, 32768, 768], P('dp', 'ctx'), may hold values from -6 to 6
- flip_perm: int32 [8, 32768], P('dp', 'ctx'), may hold values from 0 to 32767, as said below
- head_offsets: int32 [6], replicated, may hold values from 0 to 15, as said below
- input_gain: float32 [768], replicated, may hold values from 0.1 to 1.9
- projection: bfloat16 [768, 1152], P('dp'), may hold values from -12 to 12
- output_gain: float32 [384], replicated, may hold values from 0.1 to 1.9
- output_weight: bfloat16 [384, 768], P('dp'), may hold values from -0.3125 to 0.3125
Outputs:
- plain_view: bfloat16 [8, 32768, 768], P('dp', 'ctx')
- flipped_view: bfloat16 [8, 32768, 768], P('dp', 'ctx')
Inputs may be any that keep to these rules, and one draw needn't show every extreme that they name: For each slide, flip_perm is a permutation of 0 to 32767; the positions b * 512 to (b + 1) * 512 - 1 hold the tiles of block 63 - b in an order drawn from the seed. `head_offsets`: the 6 offsets are distinct.
All inputs are finite; a program needn't handle non-finite values.
Results may differ from a plain program's by a relative error of at most 0.0083.
Values may be sent and summed in bfloat16 or wider, within the bound.
No kernel may reach another device: no remote copies, remote signals or barrier semaphores. Data moves between devices by JAX's collectives and lax.ppermute only.
A program may use at most 64 MiB of HBM per device.

v0:
```python
import jax
import jax.numpy as jnp
from jax import lax
from jax.sharding import PartitionSpec as P

HEADS = 6
HEAD_DIM = 64
INNER = 384
SEGMENT = 1024
RATIO = 16
TOK_DEV = 512


eps_norm = 1e-05


def swapped(block, axis, apart):
    count = lax.axis_size(axis)
    route = []
    for low in range(count):
        high = low | 1 << apart
        if high != low and high < count:
            route += [(low, high), (high, low)]
    return lax.ppermute(block, axis, route)


def layer_norm(values, scale_gain):
    average = jnp.mean(values, axis=-1, keepdims=True)
    centred = values - average
    variance = jnp.mean(centred * centred, axis=-1, keepdims=True)
    return centred * lax.rsqrt(variance + eps_norm) * scale_gain


def attend(queries, key_rows, value_rows):

    def one_head(packed):
        head_query, head_key, head_value = packed
        scores = jnp.einsum(
            "vqd,vkd->vqk", head_query, head_key, preferred_element_type=jnp.float32
        ) * HEAD_DIM ** (-0.5)
        row_max = jnp.max(scores, axis=-1)
        weights = jnp.exp(scores - row_max[..., None])
        row_total = jnp.sum(weights, axis=-1)
        summed = jnp.einsum(
            "vqk,vkd->vqd",
            weights.astype(jnp.bfloat16),
            head_value,
            preferred_element_type=jnp.float32,
        )
        return (row_max, row_total, summed)

    return lax.map(one_head, (queries, key_rows, value_rows))


def combine(near_max, near_total, near_sum, far_max, far_total, far_sum, picked_rows):
    head_ids = jnp.arange(near_max.shape[0], dtype=jnp.int32)[:, None]
    far_max_rows = near_max.at[head_ids, picked_rows].set(far_max)
    far_total_rows = jnp.zeros_like(near_total).at[head_ids, picked_rows].set(far_total)
    far_sum_rows = jnp.zeros_like(near_sum).at[head_ids, picked_rows].set(far_sum)
    joint_max = jnp.maximum(near_max, far_max_rows)
    near_scale = jnp.exp(near_max - joint_max)
    far_scale = jnp.exp(far_max_rows - joint_max)
    numerator = near_scale[..., None] * near_sum + far_scale[..., None] * far_sum_rows
    denominator = near_scale * near_total + far_scale * far_total_rows
    attended = numerator / denominator[..., None]
    return jnp.transpose(attended, (1, 0, 2)).reshape(attended.shape[1], -1)


def per_device(
    tile_features, flip_perm, head_offsets, input_gain, projection, output_gain, output_weight
):
    ctx_rank = lax.axis_index("ctx")
    ctx_count = lax.axis_size("ctx")
    ctx_bits = ctx_count.bit_length() - 1
    sparse_local = TOK_DEV // RATIO
    picked = head_offsets[:, None] + RATIO * jnp.arange(sparse_local, dtype=jnp.int32)[None, :]
    normed = layer_norm(tile_features[0].astype(jnp.float32), input_gain).astype(jnp.bfloat16)
    mirror_perm = flip_perm[0]
    for bit_index in range(ctx_bits):
        mirror_perm = swapped(mirror_perm, "ctx", bit_index)
    flip_rows = jnp.take(mirror_perm, picked) - ctx_rank * TOK_DEV
    columns = normed
    projected = jnp.dot(
        columns,
        lax.all_gather(projection, "dp", axis=0, tiled=True),
        preferred_element_type=jnp.float32,
    ).astype(jnp.bfloat16)
    heads_split = projected.reshape(TOK_DEV, 3, HEADS, HEAD_DIM)
    key_pairs = heads_split[:, 1:].reshape(1, TOK_DEV, 2 * INNER)
    bit_index = 0
    partner = swapped(key_pairs, "ctx", bit_index)
    key_pairs = jnp.concatenate([key_pairs, partner], axis=1)
    near_keys = jnp.transpose(key_pairs.reshape(1, SEGMENT, 2, HEADS, HEAD_DIM), (2, 3, 0, 1, 4))
    near_queries = jnp.transpose(heads_split[None, :, 0], (2, 0, 1, 3))
    near_max, near_total, near_sum = attend(near_queries, near_keys[0], near_keys[1])
    head_ids = jnp.arange(HEADS, dtype=jnp.int32)[None, :]
    plain_chosen = heads_split[picked.T, :, head_ids]
    flip_chosen = heads_split[flip_rows.T, :, head_ids]
    chosen = jnp.stack([plain_chosen, flip_chosen])
    sparse_pairs = chosen[:, :, :, 1:].reshape(2, sparse_local, HEADS, 2 * HEAD_DIM)
    gathered = lax.all_gather(sparse_pairs, "ctx", axis=1, tiled=True)
    far_keys = jnp.transpose(gathered.reshape(2, -1, HEADS, 2, HEAD_DIM), (3, 2, 0, 1, 4))
    far_queries = jnp.transpose(chosen[:, :, :, 0], (2, 0, 1, 3))
    far_max, far_total, far_sum = attend(far_queries, far_keys[0], far_keys[1])
    plain_attended = combine(
        near_max[:, 0],
        near_total[:, 0],
        near_sum[:, 0],
        far_max[:, 0],
        far_total[:, 0],
        far_sum[:, 0],
        picked,
    )
    flip_attended = combine(
        near_max[:, 0],
        near_total[:, 0],
        near_sum[:, 0],
        far_max[:, 1],
        far_total[:, 1],
        far_sum[:, 1],
        flip_rows,
    )
    mixed = layer_norm(
        jnp.concatenate([plain_attended, flip_attended], axis=0), output_gain
    ).astype(jnp.bfloat16)
    columns = mixed
    result = jnp.dot(
        columns,
        lax.all_gather(output_weight, "dp", axis=0, tiled=True),
        preferred_element_type=jnp.float32,
    ).astype(jnp.bfloat16)
    plain_view = result[:TOK_DEV]
    flipped_view = result[TOK_DEV:]
    return (plain_view[None], flipped_view[None])


def solution(mesh):
    placed = (P("dp", "ctx", None), P("dp", "ctx"), P(), P(), P("dp", None), P(), P("dp", None))
    return jax.shard_map(
        per_device,
        mesh=mesh,
        in_specs=placed,
        out_specs=(P("dp", "ctx", None), P("dp", "ctx", None)),
        check_vma=False,
    )
```

profile of v0, /device:TPU:1, one launch (start us, length us, event | category | flops | bytes accessed | tf_op | source)
XLA Modules:
  0.0 339.9 jit_solution(6781169139366244679)
XLA Ops:
  7.9 8.7 %collective-permute-start.1 = (s32[512]{0:T(512)}, s32[512]{0:T(512)S(1)}, u32[]{:S(2)}, u32[]{:S(2)}) collective-permute-start(s32[512]{0:T(512)} %bitcast.202), channel_id=1, source_target_pairs={{0,1},{1,0},{2,3},{3,2},{4,5},{5,4},{6,7},{7,6},{8,9},{9,8},{10,11... | collective-permute-start | bytes 6152 | tf_op jit(solution)/shard_map/ppermute | solution.py:24
  16.7 0.7 compare_select_fusion.4
  17.7 1.9 collective-permute-start.2
  19.6 1.3 convert_reduce_fusion
  20.9 1.1 collective-permute-done.2
  22.0 1.9 collective-permute-start.3
  24.0 3.3 collective-permute-done.3
  27.2 5.4 %collective-permute-start.4 = (s32[512]{0:T(512)S(1)}, s32[512]{0:T(512)S(1)}, u32[]{:S(2)}, u32[]{:S(2)}) collective-permute-start(s32[512]{0:T(512)S(1)} %collective-permute-done.3), channel_id=1, source_target_pairs={{0,8},{8,0},{1,9},{9,1},{2,10},{10,2},{3,11},{11,3},{4,12},{12,4},... | collective-permute-start | bytes 6152 | tf_op jit(solution)/shard_map/ppermute | solution.py:24
  32.6 1.5 fusion.31
  34.2 1.3 collective-permute-done.4
  35.5 1.9 collective-permute-start.5
  37.5 2.7 collective-permute-done.5
  40.2 3.1 collective-permute-start.6
  43.4 2.4 collective-permute-done.6
  45.8 1.6 gather_fusion.1
  48.0 38.4 %all-gather.3.cloned.1.call-done = bf16[768,1152]{1,0:T(8,128)(2,1)} async-done(((bf16[96,1152]{1,0:T(8,128)(2,1)}), bf16[768,1152]{1,0:T(8,128)(2,1)}) %all-gather.3.cloned.1.call-update) | async-done | bytes 1769488 | tf_op jit(solution)/shard_map/all_gather | solution.py:85
  86.4 2.8 convolution_convert_fusion
  89.8 3.8 %copy.34 = bf16[512,3,6,64]{3,1,2,0:T(4,128)(2,1)} copy(bf16[512,3,6,64]{0,3,2,1:T(8,128)(2,1)S(1)} %bitcast.185) | data formatting | bytes 2359296 | tf_op jit(solution)/shard_map/reshape | solution.py:88
  93.6 3.7 %gather_fusion = bf16[192,3,64]{2,1,0:T(4,128)(2,1)S(1)} fusion(bf16[512,3,6,64]{3,1,2,0:T(4,128)(2,1)} %copy.34, s32[192]{0:T(256)S(1)} %reshape.289), kind=kCustom, calls=%fused_computation | custom fusion | bytes 148992 | tf_op jit(solution)/shard_map/gather | solution.py:97
  97.4 3.7 %gather_fusion.2 = bf16[192,3,64]{2,1,0:T(4,128)(2,1)S(1)} fusion(bf16[512,3,6,64]{3,1,2,0:T(4,128)(2,1)} %copy.34, s32[192]{0:T(256)S(1)} %reshape.303), kind=kCustom, calls=%fused_computation.2 | custom fusion | bytes 148992 | tf_op jit(solution)/shard_map/gather | solution.py:98
  101.5 0.8 reshape.285
  102.3 1.0 slice_bitcast_fusion.8
  103.3 9.7 %collective-permute-start = (bf16[1,512,768]{1,2,0:T(8,128)(2,1)}, bf16[1,512,768]{1,2,0:T(8,128)(2,1)}, u32[]{:S(2)}, u32[]{:S(2)}) collective-permute-start(bf16[1,512,768]{1,2,0:T(8,128)(2,1)} %bitcast.17), channel_id=1, source_target_pairs={{0,1},{1,0},{2,3},{3,2},{4,5},{5,4},{6,7},{7,6},{8,9},{9,8},{10,11... | collective-permute-start | bytes 2359304 | tf_op jit(solution)/shard_map/ppermute | solution.py:24
  113.0 44.8 %all_gather.11 = bf16[384,768]{1,0:T(8,128)(2,1)} all-gather(bf16[48,768]{1,0:T(8,128)(2,1)S(1)} %copy-done.3), channel_id=1, replica_groups=mesh['dp'=8,'ctx'=64] {'dp'}, dimensions={0}, use_global_device_ids=true | all-gather | bytes 663552 | tf_op jit(solution)/shard_map/all_gather | solution.py:129
  158.2 1.3 maximum_bitcast_fusion
  159.7 10.8 %while.28 = (s32[]{:T(128)}, f32[6,1,512]{2,0,1:T(8,128)S(1)}, f32[6,1,512]{2,0,1:T(8,128)S(1)}, f32[6,1,512,64]{2,3,1,0:T(8,128)S(1)}, bf16[6,1,512,64]{2,3,0,1...) while((s32[]{:T(128)}, f32[6,1,512]{2,0,1:T(8,128)S(1)}, ...), condition=%wide.region_5.6_spmd, body=%wide.region_2.5_spmd.sunk | while | flops 138411008 | bytes 6768741 | solution.py:52
  170.5 1.7 copy.44
  172.1 62.7 %all-gather.5.cloned.1.call-done = bf16[2,2048,6,128]{3,1,2,0:T(8,128)(2,1)} async-done(((bf16[2,32,6,128]{3,1,2,0:T(8,128)(2,1)}), bf16[2,2048,6,128]{3,1,2,0:T(8,128)(2,1)}) %all-gather.5.cloned.1.call-update) | async-done | bytes 6291472 | tf_op jit(solution)/shard_map/all_gather | solution.py:101
  234.8 8.7 %copy.40 = bf16[2,2048,6,128]{1,3,2,0:T(8,128)(2,1)} copy(bf16[2,2048,6,128]{3,1,2,0:T(8,128)(2,1)} %all-gather.5.cloned.1.call-done) | data formatting | bytes 12582912 | tf_op jit(solution)/shard_map/all_gather | solution.py:101
  243.5 5.3 %slice_bitcast_fusion = (bf16[6,2,2048,64]{2,3,0,1:T(8,128)(2,1)S(1)}, bf16[6,2,2048,64]{2,3,0,1:T(8,128)(2,1)}) fusion(bf16[2,6,2,2048,64]{3,4,0,1,2:T(8,128)(2,1)} %bitcast.184), kind=kLoop, calls=%fused_computation.43 | loop fusion | bytes 12582912 | tf_op jit(solution)/shard_map/squeeze | solution.py:104
  248.9 11.7 %while.29 = (s32[]{:T(128)}, f32[6,2,32]{2,1,0:T(2,128)S(1)}, f32[6,2,32]{2,1,0:T(2,128)S(1)}, f32[6,2,32,64]{3,2,1,0:T(8,128)S(1)}, bf16[6,2,32,64]{3,2,1,0:T(8...) while((s32[]{:T(128)}, f32[6,2,32]{2,1,0:T(2,128)S(1)}, ...), condition=%wide.region_9.10_spmd, body=%wide.region_6.9_spmd.sunk | while | flops 34340736 | bytes 2678617 | solution.py:52
  248.9 1.3 fusion.99
  250.8 1.3 fusion.99
  252.7 1.3 fusion.99
  254.7 1.3 fusion.99
  256.6 1.3 fusion.99
  258.6 1.3 fusion.99
  260.9 9.9 %scatter_fusion.3 = f32[6,512]{1,0:T(8,128)S(1)} fusion(f32[6,512]{1,0:T(8,128)S(1)} %copy.101, s32[192]{0:T(256)S(1)} %reshape.327, f32[192]{0:T(256)S(1)} %reshape.329), kind=kCustom, calls=%fused_computation.6 | custom fusion | bytes 3840 | tf_op jit(solution)/shard_map/scatter | solution.py:57
  270.9 9.9 %scatter_fusion.5 = f32[6,512]{1,0:T(8,128)S(1)} fusion(f32[6,512]{1,0:T(8,128)S(1)} %broadcast.321.clone.1, s32[192]{0:T(256)S(1)} %reshape.327, f32[192]{0:T(256)S(1)} %reshape.341), kind=kCustom, calls=%fused_computation.8 | custom fusion | bytes 3840 | tf_op jit(solution)/shard_map/scatter | solution.py:58
  280.8 10.0 %scatter_fusion = f32[6,512]{1,0:T(8,128)S(1)} fusion(f32[6,512]{1,0:T(8,128)S(1)} %copy.99, s32[192]{0:T(256)S(1)} %reshape.309, f32[192]{0:T(256)S(1)} %reshape.311), kind=kCustom, calls=%fused_computation.3 | custom fusion | bytes 3840 | tf_op jit(solution)/shard_map/scatter | solution.py:57
  290.8 10.0 %scatter_fusion.2 = f32[6,512]{1,0:T(8,128)S(1)} fusion(f32[6,512]{1,0:T(8,128)S(1)} %broadcast.321.clone, s32[192]{0:T(256)S(1)} %reshape.309, f32[192]{0:T(256)S(1)} %reshape.323), kind=kCustom, calls=%fused_computation.5 | custom fusion | bytes 3840 | tf_op jit(solution)/shard_map/scatter | solution.py:58
  300.9 10.0 %scatter_fusion.4 = f32[6,512,64]{2,1,0:T(8,128)S(1)} fusion(f32[6,512,64]{2,1,0:T(8,128)S(1)} %broadcast.320.clone.1, s32[192]{0:T(256)S(1)} %reshape.327, f32[192,64]{1,0:T(8,128)S(1)} %bitcast.198), kind=kCustom, calls=%fused_computation.7 | custom fusion | bytes 148992 | tf_op jit(solution)/shard_map/scatter | solution.py:59
  311.1 10.0 %scatter_fusion.1 = f32[6,512,64]{2,1,0:T(8,128)S(1)} fusion(f32[6,512,64]{2,1,0:T(8,128)S(1)} %broadcast.320.clone, s32[192]{0:T(256)S(1)} %reshape.309, f32[192,64]{1,0:T(8,128)S(1)} %bitcast.197), kind=kCustom, calls=%fused_computation.4 | custom fusion | bytes 148992 | tf_op jit(solution)/shard_map/scatter | solution.py:59
  321.0 6.1 %fusion.36 = (f32[512,6,64]{2,0,1:T(8,128)}, f32[512,6,64]{2,0,1:T(8,128)}) fusion(f32[6,1,512,64]{3,2,0,1:T(8,128)} %copy.44, f32[6,512,64]{2,1,0:T(8,128)S(1)} %scatter_fusion.1, f32[6,512]{1,0:T(8,128)S(1)} %get-tuple-element.146, f32[6,512]{1,0:T(8,128)S(1)} %get-tuple-element.147, f32[6,512]{1,0:T(8,128)S(1)} %get-tuple-element.148, ...), kind=kLoop, calls=%fused_computation.61 | loop fusion | flops 1572864 | bytes 4005888 | tf_op jit(solution)/shard_map/transpose | solution.py:66
  327.2 2.0 copy.45
  330.0 0.7 copy-done.2
  330.7 1.1 convolution_convert_fusion.1
  331.8 1.2 slice_bitcast_fusion.2
  (115 shorter events, 18.7 us)
Async XLA Ops:
  7.2 79.2 %all-gather.3.cloned.1.call-start = ((), (), s32[]{:S(2)}) async-start(), calls=%async_computation | async-start | bytes 1990656 | tf_op jit(solution)/shard_map/all_gather | solution.py:85
  7.9 226.9 %all-gather.5.cloned.1.call-start = ((), (), s32[]{:S(2)}) async-start(), calls=%async_computation.1 | async-start | bytes 6389760 | tf_op jit(solution)/shard_map/all_gather | solution.py:101
  7.9 9.8 %collective-permute-start.1 = (s32[512]{0:T(512)}, s32[512]{0:T(512)S(1)}, u32[]{:S(2)}, u32[]{:S(2)}) collective-permute-start(s32[512]{0:T(512)} %bitcast.202), channel_id=1, source_target_pairs={{0,1},{1,0},{2,3},{3,2},{4,5},{5,4},{6,7},{7,6},{8,9},{9,8},{10,11... | collective-permute-start | bytes 6152 | tf_op jit(solution)/shard_map/ppermute | solution.py:24
  17.7 4.3 %collective-permute-start.2 = (s32[512]{0:T(512)S(1)}, s32[512]{0:T(512)S(1)}, u32[]{:S(2)}, u32[]{:S(2)}) collective-permute-start(s32[512]{0:T(512)S(1)} %collective-permute-done.1), channel_id=1, source_target_pairs={{0,2},{2,0},{1,3},{3,1},{4,6},{6,4},{5,7},{7,5},{8,10},{10,8},{9,1... | collective-permute-start | bytes 6152 | tf_op jit(solution)/shard_map/ppermute | solution.py:24
  22.0 5.2 %collective-permute-start.3 = (s32[512]{0:T(512)S(1)}, s32[512]{0:T(512)S(1)}, u32[]{:S(2)}, u32[]{:S(2)}) collective-permute-start(s32[512]{0:T(512)S(1)} %collective-permute-done.2), channel_id=1, source_target_pairs={{0,4},{4,0},{1,5},{5,1},{2,6},{6,2},{3,7},{7,3},{8,12},{12,8},{9,1... | collective-permute-start | bytes 6152 | tf_op jit(solution)/shard_map/ppermute | solution.py:24
  27.2 8.2 %collective-permute-start.4 = (s32[512]{0:T(512)S(1)}, s32[512]{0:T(512)S(1)}, u32[]{:S(2)}, u32[]{:S(2)}) collective-permute-start(s32[512]{0:T(512)S(1)} %collective-permute-done.3), channel_id=1, source_target_pairs={{0,8},{8,0},{1,9},{9,1},{2,10},{10,2},{3,11},{11,3},{4,12},{12,4},... | collective-permute-start | bytes 6152 | tf_op jit(solution)/shard_map/ppermute | solution.py:24
  35.5 4.7 %collective-permute-start.5 = (s32[512]{0:T(512)S(1)}, s32[512]{0:T(512)S(1)}, u32[]{:S(2)}, u32[]{:S(2)}) collective-permute-start(s32[512]{0:T(512)S(1)} %collective-permute-done.4), channel_id=1, source_target_pairs={{0,16},{16,0},{1,17},{17,1},{2,18},{18,2},{3,19},{19,3},{4,20},{20... | collective-permute-start | bytes 6152 | tf_op jit(solution)/shard_map/ppermute | solution.py:24
  40.2 5.6 %collective-permute-start.6 = (s32[512]{0:T(512)S(1)}, s32[512]{0:T(512)S(1)}, u32[]{:S(2)}, u32[]{:S(2)}) collective-permute-start(s32[512]{0:T(512)S(1)} %collective-permute-done.5), channel_id=1, source_target_pairs={{0,32},{32,0},{1,33},{33,1},{2,34},{34,2},{3,35},{35,3},{4,36},{36... | collective-permute-start | bytes 6152 | tf_op jit(solution)/shard_map/ppermute | solution.py:24
  43.3 4.2 %copy-start.4 = (s32[6]{0:T(128)S(1)}, s32[6]{0:T(128)}, u32[]{:S(2)}) copy-start(s32[6]{0:T(128)} %param.13) | copy-start | bytes 76
  43.3 43.0 %copy-start.1 = (bf16[1,512,768]{2,1,0:T(8,128)(2,1)S(1)}, bf16[1,512,768]{2,1,0:T(8,128)(2,1)}, u32[]{:S(2)}) copy-start(bf16[1,512,768]{2,1,0:T(8,128)(2,1)} %param.11) | copy-start | bytes 2359300
  43.4 43.0 %copy-start.5 = (f32[768]{0:T(1024)S(1)}, f32[768]{0:T(1024)}, u32[]{:S(2)}) copy-start(f32[768]{0:T(1024)} %param.14) | copy-start | bytes 9220
  101.2 11.8 %copy-start.3 = (bf16[48,768]{1,0:T(8,128)(2,1)S(1)}, bf16[48,768]{1,0:T(8,128)(2,1)}, u32[]{:S(2)}) copy-start(bf16[48,768]{1,0:T(8,128)(2,1)} %param.17) | copy-start | bytes 221188
  103.3 55.0 %collective-permute-start = (bf16[1,512,768]{1,2,0:T(8,128)(2,1)}, bf16[1,512,768]{1,2,0:T(8,128)(2,1)}, u32[]{:S(2)}, u32[]{:S(2)}) collective-permute-start(bf16[1,512,768]{1,2,0:T(8,128)(2,1)} %bitcast.17), channel_id=1, source_target_pairs={{0,1},{1,0},{2,3},{3,2},{4,5},{5,4},{6,7},{7,6},{8,9},{9,8},{10,11... | collective-permute-start | bytes 2359304 | tf_op jit(solution)/shard_map/ppermute | solution.py:24
  327.2 2.0 copy-start
  329.6 1.1 copy-start.2
  329.6 1.1 copy-start.6
Sparse Core Ops, SparseCore 0:
  11.2 75.1 all-gather.2
  102.4 132.3 all-gather.4
where the time goes:
time: 341 us; the launch traced here: 340 us
  waiting for transfers between devices  113 us (33%)
  local copies, waits for them, and re-layouts  97.8 us (29%)
  blocking collectives  44.8 us (13%)
  starting transfers between devices  32.8 us (10%)
  matrix products  20.8 us (6%)
  other arithmetic  16 us (5%)
  between operations  14.5 us (4%)
    all_gather x1, waiting for transfers between devices, per_device(): gathered = lax.all_gather(sparse_pairs, 'ctx', axis=1, tiled=True)  62.7 us
    all_gather x1, blocking collectives, per_device(): lax.all_gather(output_weight, 'dp', axis=0, tiled=True)  44.8 us
    all_gather x1, waiting for transfers between devices, per_device(): lax.all_gather(projection, 'dp', axis=0, tiled=True)  38.4 us
    ppermute x7, starting transfers between devices, swapped(): return lax.ppermute(block, axis, route)  32.7 us
    scatter x2, local copies, waits for them, and re-layouts, combine(): jnp.zeros_like(near_sum).at[head_ids, picked_rows].set(far_sum)  20 us
    scatter x2, local copies, waits for them, and re-layouts, combine(): far_max_rows = near_max.at[head_ids, picked_rows].set(far_max)  19.9 us
    scatter x2, local copies, waits for them, and re-layouts, combine(): jnp.zeros_like(near_total).at[head_ids, picked_rows].set(far_total)  19.9 us
    dot_general x12, matrix products, one_head(): jnp.einsum('vqd,vkd->vqk', head_query, head_key, preferred_element_type=j...  11.3 us
  transfers between devices with their start and end apart: 9, of which 8 were waited for; matrix products, arithmetic and copies ran while one was open for 6% of the time, Pallas kernels for 0%

commit v1 on v0

v1 whole, which is shorter than its diff:
```python
import functools

import jax
import jax.numpy as jnp
from jax import lax
from jax.experimental import pallas as pl
from jax.experimental.pallas import tpu as pltpu
from jax.sharding import Mesh, PartitionSpec as P

HEADS = 6
HEAD_DIM = 64
INNER = 384
D = 768
RATIO = 16
TOK = 512
SEG = 1024
HALF = 3
SPARSE = TOK // RATIO
POS = 32
INTERPRET = False

eps_norm = 1e-05
EXP_SCALE = HEAD_DIM ** (-0.5) * 1.4426950408889634
SCALE = HEAD_DIM ** (-0.5)

F32 = jnp.float32
BF16 = jnp.bfloat16
VMEM = pl.BlockSpec(memory_space=pltpu.VMEM)
SMEM = pl.BlockSpec(memory_space=pltpu.SMEM)


def call(kernel, out_shape, specs, scratch=(), flops=0, moved=0):
    single = not isinstance(out_shape, (list, tuple))
    return pl.pallas_call(
        kernel,
        out_shape=out_shape,
        in_specs=specs,
        out_specs=VMEM if single else [VMEM] * len(out_shape),
        scratch_shapes=list(scratch),
        cost_estimate=pl.CostEstimate(flops=flops, bytes_accessed=moved, transcendentals=0),
        interpret=INTERPRET,
    )


def shape_of(*dims, dtype=BF16):
    return jax.ShapeDtypeStruct(dims, dtype)


def swap_halves(block):
    return jnp.concatenate([block[:, HEAD_DIM:], block[:, :HEAD_DIM]], axis=1)


def parts3(value):
    high = value.astype(BF16)
    rest = value - high.astype(F32)
    middle = rest.astype(BF16)
    low = (rest - middle.astype(F32)).astype(BF16)
    return high, middle, low


def pack_kernel(core_ref, proj_ref, outw_ref, packed_ref):
    for core in range(2):

        @pl.when(core_ref[0] == core)
        def _():
            for head in range(HALF):
                col = (core * HALF + head) * HEAD_DIM
                lanes = slice(head * 128, head * 128 + 128)
                keys = proj_ref[:, INNER + col : INNER + col + HEAD_DIM].astype(F32)
                values = proj_ref[:, 2 * INNER + col : 2 * INNER + col + HEAD_DIM].astype(F32)
                queries = proj_ref[:, col : col + HEAD_DIM].astype(F32)
                pair = jnp.concatenate([keys, values], axis=1).astype(BF16)
                folded = jnp.concatenate([queries[:48], queries[48:]], axis=1).astype(BF16)
                for peer in range(packed_ref.shape[0]):
                    packed_ref[peer, 0:96, lanes] = pair
                    packed_ref[peer, 96:144, lanes] = folded
            half = outw_ref[:, core * INNER : (core + 1) * INNER]
            for peer in range(packed_ref.shape[0]):
                packed_ref[peer, 144:192, :] = half


def pack_weights(core, projection, output_weight, peers):
    return call(pack_kernel, shape_of(peers, 192, INNER), [SMEM, VMEM, VMEM])(
        core, projection, output_weight
    )


def gather_weights(core, projection, output_weight):
    packed = pack_weights(core, projection, output_weight, 8)
    return lax.all_to_all(packed, "dp", 0, 0, tiled=True)


def norm_kernel(x_ref, gain_ref, out_ref):
    for row in range(0, TOK, 128):
        values = x_ref[row : row + 128, :].astype(F32)
        average = jnp.mean(values, axis=-1, keepdims=True)
        centred = values - average
        variance = jnp.mean(centred * centred, axis=-1, keepdims=True)
        out_ref[row : row + 128, :] = (
            centred * lax.rsqrt(variance + eps_norm) * gain_ref[...]
        ).astype(BF16)


def one_hot(view, offset, base_ref, own_ref, other_ref):
    if view == 0:
        rows = lax.broadcasted_iota(jnp.int32, (SPARSE, 1), 0) * RATIO + offset
        index = jnp.concatenate([rows, rows + TOK], axis=0)
    else:
        lane = lax.broadcasted_iota(jnp.int32, (SPARSE, RATIO), 1)
        own = jnp.sum(jnp.where(lane == offset, own_ref[...], 0), axis=1, keepdims=True)
        other = jnp.sum(jnp.where(lane == offset, other_ref[...], 0), axis=1, keepdims=True)
        index = jnp.concatenate([own - base_ref[1], other - base_ref[2] + TOK], axis=0)
    token = lax.broadcasted_iota(jnp.int32, (2 * SPARSE, SEG), 1)
    return jnp.where(token == index, 1.0, 0.0).astype(BF16)


def project_kernel(
    base_ref, offset_ref, own_x, other_x, packed_ref, own_ref, other_ref,
    kv_ref, q_ref, send_ref, wkv_ref, wq_ref,
):
    lane = lax.broadcasted_iota(jnp.int32, (48, 128), 1)
    for shard in range(8):
        wkv_ref[shard * 96 : shard * 96 + 96, :] = packed_ref[shard, 0:96, :]
        for head in range(HALF):
            lanes = slice(head * 128, head * 128 + 128)
            folded = packed_ref[shard, 96:144, lanes].astype(F32)
            first = jnp.where(lane < HEAD_DIM, folded, 0.0)
            second = jnp.where(lane < HEAD_DIM, swap_halves(folded), 0.0)
            wq_ref[shard * 96 : shard * 96 + 48, lanes] = first.astype(BF16)
            wq_ref[shard * 96 + 48 : shard * 96 + 96, lanes] = second.astype(BF16)
    for part, x_ref in enumerate((own_x, other_x)):
        rows = slice(part * TOK, part * TOK + TOK)
        kv_ref[rows, :] = jnp.dot(
            x_ref[...], wkv_ref[...], preferred_element_type=F32
        ).astype(BF16)
        q_ref[rows, :] = jnp.dot(
            x_ref[...], wq_ref[...], preferred_element_type=F32
        ).astype(BF16)
    for view in range(2):
        for head in range(HALF):
            lanes = slice(head * 128, head * 128 + 128)
            offset = offset_ref[base_ref[0] * HALF + head]
            chosen = one_hot(view, offset, base_ref, own_ref, other_ref)
            far_kv = jnp.dot(chosen, kv_ref[:, lanes], preferred_element_type=F32).astype(BF16)
            far_q = jnp.dot(chosen, q_ref[:, lanes], preferred_element_type=F32)
            pair = (view * HALF + head) * 4
            for q_half in range(2):
                row = q_half * SPARSE
                folded = (
                    far_q[row : row + 16] + swap_halves(far_q[row + 16 : row + 32])
                ).astype(BF16)
                for k_half in range(2):
                    peer = pair + q_half * 2 + k_half
                    send_ref[peer, 0:32, :] = far_kv[k_half * SPARSE : k_half * SPARSE + 32]
                    send_ref[peer, 32:48, :] = folded
    for peer in range(4 * 2 * HALF, POS):
        send_ref[peer] = jnp.zeros((48, 128), BF16)


def near_kernel(q_ref, kv_ref, out_ref):
    keys = kv_ref[...]
    lane = lax.broadcasted_iota(jnp.int32, (SEG, 128), 1)
    values = jnp.where(lane < HEAD_DIM, swap_halves(keys.astype(F32)), 1.0).astype(BF16)
    scores = lax.dot_general(
        q_ref[...], keys, (((1,), (1,)), ((), ())), preferred_element_type=F32
    )
    row_max = jnp.max(scores, axis=1, keepdims=True)
    weights = jnp.exp2((scores - row_max) * EXP_SCALE).astype(BF16)
    summed = jnp.dot(weights, values, preferred_element_type=F32)
    swapped = swap_halves(summed)
    out_lane = lax.broadcasted_iota(jnp.int32, summed.shape, 1)
    out_ref[...] = jnp.where(
        out_lane < HEAD_DIM, summed / swapped, row_max * SCALE + jnp.log(summed)
    )


def near_level(queries, key_pairs):
    tile = 256
    return pl.pallas_call(
        near_kernel,
        out_shape=shape_of(SEG, HALF * 128, dtype=F32),
        grid=(HALF, SEG // tile),
        in_specs=[
            pl.BlockSpec((tile, 128), lambda h, i: (i, h)),
            pl.BlockSpec((SEG, 128), lambda h, i: (0, h)),
        ],
        out_specs=pl.BlockSpec((tile, 128), lambda h, i: (i, h)),
        cost_estimate=pl.CostEstimate(
            flops=4 * HALF * SEG * SEG * 128, bytes_accessed=3 << 20, transcendentals=HALF * SEG * SEG
        ),
        interpret=INTERPRET,
    )(queries, key_pairs)


def far_kernel(got_ref, back_ref):
    keys = got_ref[:, 0:32, :].reshape(POS * 32, 128)
    folded = got_ref[:, 32:48, :].reshape(POS * 16, 128)
    lane = lax.broadcasted_iota(jnp.int32, (POS * 32, 128), 1)
    turned = swap_halves(keys.astype(F32))
    lane_q = lax.broadcasted_iota(jnp.int32, (POS * 16, 128), 1)
    wide = folded.astype(F32)
    outputs, logs = [], []
    for part in range(2):
        queries = jnp.where(lane_q < HEAD_DIM, wide if part == 0 else swap_halves(wide), 0.0)
        scores = lax.dot_general(
            queries.astype(BF16), keys, (((1,), (1,)), ((), ())), preferred_element_type=F32
        )
        row_max = jnp.max(scores, axis=1, keepdims=True)
        weights = jnp.exp2((scores - row_max) * EXP_SCALE).astype(BF16)
        if part == 0:
            values = jnp.where(lane < HEAD_DIM, turned, 1.0).astype(BF16)
        else:
            values = jnp.where(lane < HEAD_DIM, 1.0, keys.astype(F32)).astype(BF16)
        summed = jnp.dot(weights, values, preferred_element_type=F32)
        swapped = swap_halves(summed)
        outputs.append(summed / swapped)
        logs.append(row_max * SCALE + jnp.log(swapped if part == 0 else summed))
    merged = jnp.where(lane_q < HEAD_DIM, outputs[0], outputs[1]).astype(BF16)
    back_ref[:, 0:16, :] = merged.reshape(POS, 16, 128)
    total = jnp.where(lane_q < HEAD_DIM, logs[0], swap_halves(logs[1]))
    high, middle, low = (part.astype(F32) for part in parts3(total))
    slot = jnp.bitwise_and(lane_q, HEAD_DIM - 1)
    stats = jnp.where(slot == 0, high, jnp.where(slot == 1, middle, low)).astype(BF16)
    back_ref[:, 16:32, :] = stats.reshape(POS, 16, 128)


def join_kernel(base_ref, offset_ref, near_ref, back_ref, own_ref, other_ref, keep_ref, give_ref):
    for view in range(2):
        for head in range(HALF):
            offset = offset_ref[base_ref[0] * HALF + head]
            chosen = one_hot(view, offset, base_ref, own_ref, other_ref)
            outs, logs = [], []
            for k_half in range(2):
                rows, stats = [], []
                for q_half in range(2):
                    peer = (view * HALF + head) * 4 + q_half * 2 + k_half
                    block = back_ref[peer, 0:16, :].astype(F32)
                    stat = back_ref[peer, 16:32, :].astype(F32)
                    rows += [block[:, :HEAD_DIM], block[:, HEAD_DIM:]]
                    for at in (0, HEAD_DIM):
                        stats.append(
                            stat[:, at : at + 1] + stat[:, at + 1 : at + 2] + stat[:, at + 2 : at + 3]
                        )
                outs.append(jnp.concatenate(rows, axis=0))
                logs.append(jnp.concatenate(stats, axis=0))
            top = jnp.maximum(logs[0], logs[1])
            weight0, weight1 = jnp.exp(logs[0] - top), jnp.exp(logs[1] - top)
            joint = weight0 + weight1
            far = (weight0 * outs[0] + weight1 * outs[1]) / joint
            far_log = jnp.broadcast_to(top + jnp.log(joint), (2 * SPARSE, HEAD_DIM))
            both = jnp.concatenate([far, far_log], axis=1)
            ones = jnp.ones((2 * SPARSE, 128), BF16)
            none = jnp.zeros((2 * SPARSE, 128), BF16)
            right = jnp.concatenate(
                [
                    jnp.concatenate([part, ones if i == 0 else none], axis=1)
                    for i, part in enumerate(parts3(both))
                ],
                axis=0,
            )
            left = jnp.concatenate([chosen, chosen, chosen], axis=0)
            spread = lax.dot_general(
                left, right, (((0,), (0,)), ((), ())), preferred_element_type=F32
            )
            near = near_ref[:, head * 128 : head * 128 + 128]
            gap = spread[:, :128] - near
            share = spread[:, 128:] / (1.0 + jnp.exp(-gap))
            attended = near + swap_halves(share) * gap
            cols = slice(head * HEAD_DIM, head * HEAD_DIM + HEAD_DIM)
            keep_ref[view * TOK : view * TOK + TOK, cols] = attended[:TOK, :HEAD_DIM]
            give_ref[view * TOK : view * TOK + TOK, cols] = attended[TOK:, :HEAD_DIM].astype(BF16)


def output_kernel(core_ref, keep_ref, got_ref, gain_ref, own_w, other_w, plain_ref, flip_ref):
    core = core_ref[0]
    width = HALF * HEAD_DIM
    for row in range(0, 2 * TOK, 256):
        first = keep_ref[row : row + 256, :]
        second = got_ref[row : row + 256, :].astype(F32)
        average = (
            jnp.sum(first, axis=-1, keepdims=True) + jnp.sum(second, axis=-1, keepdims=True)
        ) / INNER
        first, second = first - average, second - average
        variance = (
            jnp.sum(first * first, axis=-1, keepdims=True)
            + jnp.sum(second * second, axis=-1, keepdims=True)
        ) / INNER
        scale = lax.rsqrt(variance + eps_norm)
        first = (first * scale * gain_ref[pl.ds(core, 1), :]).astype(BF16)
        second = (second * scale * gain_ref[pl.ds(1 - core, 1), :]).astype(BF16)
        out_ref = plain_ref if row < TOK else flip_ref
        at = row % TOK
        own_rows = pl.ds(pl.multiple_of(core * width, width), width)
        other_rows = pl.ds(pl.multiple_of((1 - core) * width, width), width)
        for weights, place in ((own_w, core), (other_w, 1 - core)):
            result = jnp.dot(first, weights[own_rows, :], preferred_element_type=F32) + jnp.dot(
                second, weights[other_rows, :], preferred_element_type=F32
            )
            out_ref[at : at + 256, pl.ds(pl.multiple_of(place * INNER, 128), INNER)] = result.astype(
                BF16
            )


def core_swap(block):
    return lax.ppermute(block, "core", [(0, 1), (1, 0)])


def per_device(
    tile_features, flip_perm, head_offsets, input_gain, projection, output_gain, output_weight
):
    core = lax.axis_index("core").astype(jnp.int32)
    pos = lax.axis_index("pos").astype(jnp.int32)
    rank = pos * 2 + core
    core_id = core[None]
    base = jnp.stack([core, rank * TOK, (rank ^ 1) * TOK])

    perm = flip_perm.reshape(SPARSE, RATIO)
    last = 2 * POS - 1
    own_perm = lax.ppermute(perm, ("pos", "core"), [(last - r, r) for r in range(2 * POS)])
    other_perm = lax.ppermute(perm, ("pos", "core"), [(last - (r ^ 1), r) for r in range(2 * POS)])

    own_x = call(norm_kernel, shape_of(TOK, D), [VMEM, VMEM])(
        tile_features[0], input_gain[None, :]
    )
    other_x = core_swap(own_x)
    packed = gather_weights(core_id, projection, output_weight)

    key_pairs, queries, send = call(
        project_kernel,
        [shape_of(SEG, INNER), shape_of(SEG, INNER), shape_of(POS, 48, 128)],
        [SMEM, SMEM, VMEM, VMEM, VMEM, VMEM, VMEM],
        [pltpu.VMEM((D, INNER), BF16), pltpu.VMEM((D, INNER), BF16)],
        flops=2 * SEG * D * 768,
        moved=4 << 20,
    )(base, head_offsets, own_x, other_x, packed, own_perm, other_perm)

    own_w = packed[:, 144:192, :].reshape(INNER, INNER)
    other_w = core_swap(own_w)

    got = lax.all_to_all(send, "pos", 0, 0, tiled=True)
    near = near_level(queries, key_pairs)
    back = call(far_kernel, shape_of(POS, 32, 128), [VMEM], flops=4 * SEG * SEG * 128, moved=1 << 20)(
        got
    )
    back = lax.all_to_all(back, "pos", 0, 0, tiled=True)

    keep, give = call(
        join_kernel,
        [shape_of(2 * TOK, HALF * HEAD_DIM, dtype=F32), shape_of(2 * TOK, HALF * HEAD_DIM)],
        [SMEM, SMEM, VMEM, VMEM, VMEM, VMEM],
        flops=12 * SEG * 192 * 256,
        moved=3 << 20,
    )(base, head_offsets, near, back, own_perm, other_perm)
    taken = core_swap(give)

    plain_view, flipped_view = call(
        output_kernel,
        [shape_of(TOK, D), shape_of(TOK, D)],
        [SMEM, VMEM, VMEM, VMEM, VMEM, VMEM],
        flops=4 * SEG * INNER * D,
        moved=4 << 20,
    )(core_id, keep, taken, output_gain.reshape(2, HALF * HEAD_DIM), own_w, other_w)
    return (plain_view[None], flipped_view[None])


def solution(mesh):
    fine = Mesh(mesh.devices.reshape(mesh.shape["dp"], POS, 2), ("dp", "pos", "core"))
    ctx = ("pos", "core")
    placed = (
        P("dp", ctx, None), P("dp", ctx), P(), P(), P("dp", None), P(), P("dp", None),
    )
    return jax.shard_map(
        per_device,
        mesh=fine,
        in_specs=placed,
        out_specs=(P("dp", ctx, None), P("dp", ctx, None)),
        check_vma=False,
    )
```

time: 341 us -> 121 us (0.35)
  waiting for transfers between devices: 113 us -> 6.97 us
  local copies, waits for them, and re-layouts: 97.8 us -> 6.32 us
  Pallas kernels: 0 us -> 36.5 us
  matrix products: 20.8 us -> 0 us
  other arithmetic: 16 us -> 1.22 us
  blocking collectives: 44.8 us -> 30.4 us
  between operations: 14.5 us -> 0.76 us
  starting transfers between devices: 32.8 us -> 37.7 us
    all_gather x2 -> x0, waiting for transfers between devices: 101 us -> none  [the longest x1 62.7 us: per_device(): gathered = lax.all_gather(sparse_pairs, 'ctx', axis=1, tiled=True)]
    scatter x6 -> x0, local copies, waits for them, and re-layouts: 59.8 us -> none  [the longest x2 20 us: combine(): jnp.zeros_like(near_sum).at[head_ids, picked_rows].set(far_sum)]
    all_gather x1 -> x0, blocking collectives: 44.8 us -> none  [per_device(): lax.all_gather(output_weight, 'dp', axis=0, tiled=True)]
    pallas_call x0 -> x7, Pallas kernels: none -> 36.5 us  [the longest x1 11.6 us: near_level(): pl.pallas_call(near_kernel, out_shape=shape_of(SEG, HALF * 128, dtype=F32...]
    all_to_all x0 -> x1, blocking collectives: none -> 30.4 us  [per_device(): got = lax.all_to_all(send, 'pos', 0, 0, tiled=True)]
    dot_general x26 -> x0, matrix products: 20.8 us -> none  [the longest x12 11.3 us: one_head(): jnp.einsum('vqd,vkd->vqk', head_query, head_key, preferred_element_type=j...]
    all_to_all x0 -> x2, starting transfers between devices: none -> 16.7 us  [the longest x1 10.2 us: gather_weights(): return lax.all_to_all(packed, 'dp', 0, 0, tiled=True)]
    ppermute x7 -> x5, starting transfers between devices: 32.7 us -> 20.9 us  [the longest x1 10.9 us: per_device(): lax.ppermute(perm, ('pos', 'core'), [(last - r, r) for r in range(2 * POS)])]
  transfers between devices with their start and end apart: 9 -> 7, of which waited for: 8 -> 3; matrix products, arithmetic and copies ran while one was open for 6% -> 3% of each run, Pallas kernels for 0% -> 12%
where the time goes in v1:
time: 121 us; the launch traced here: 120 us
  starting transfers between devices  37.7 us (31%)
  Pallas kernels  36.5 us (30%)
  blocking collectives  30.4 us (25%)
  waiting for transfers between devices  6.97 us (6%)
  local copies, waits for them, and re-layouts  6.32 us (5%)
  other arithmetic  1.22 us (1%)
    all_to_all x1, blocking collectives, per_device(): got = lax.all_to_all(send, 'pos', 0, 0, tiled=True)  30.4 us
    pallas_call x1, Pallas kernels, near_level(): pl.pallas_call(near_kernel, out_shape=shape_of(SEG, HALF * 128, dtype=F32...  11.6 us
    ppermute x1, starting transfers between devices, per_device(): lax.ppermute(perm, ('pos', 'core'), [(last - r, r) for r in range(2 * POS)])  10.9 us
    all_to_all x1, starting transfers between devices, gather_weights(): return lax.all_to_all(packed, 'dp', 0, 0, tiled=True)  10.2 us
    ppermute x3, starting transfers between devices, core_swap(): return lax.ppermute(block, 'core', [(0, 1), (1, 0)])  8.02 us
    pallas_call x1, Pallas kernels, per_device(): call(join_kernel, [shape_of(2 * TOK, HALF * HEAD_DIM, dtype=F32), shape_o...  7.58 us
    all_to_all x1, starting transfers between devices, per_device(): back = lax.all_to_all(back, 'pos', 0, 0, tiled=True)  6.51 us
    pallas_call x1, Pallas kernels, per_device(): call(project_kernel, [shape_of(SEG, INNER), shape_of(SEG, INNER), shape_o...  4.97 us
  transfers between devices with their start and end apart: 7, of which 3 were waited for; matrix products, arithmetic and copies ran while one was open for 3% of the time, Pallas kernels for 12%

profile of v1, /device:TPU:1, one launch (start us, length us, event | category | flops | bytes accessed | tf_op | source)
XLA Modules:
  0.0 119.8 jit_solution(18023939795643116046)
XLA Ops:
  0.6 2.2 %shard_map.87 = bf16[8,192,384]{2,1,0:T(8,128)(2,1)} custom-call(s32[1]{0:T(128)} %bitcast.core_ref, bf16[96,1152]{1,0:T(8,128)(2,1)} %proj_ref.1, bf16[48,768]{1,0:T(8,128)(2,1)} %outw_ref.1), custom_call_target="tpu_custom_call" | custom-call | tf_op jit(solution)/shard_map/pallas_call | solution.py:83
  2.9 0.0 copy-start.3
  2.9 10.2 %all-to-all-start = ((bf16[8,192,384]{2,1,0:T(8,128)(2,1)}), bf16[8,192,384]{2,1,0:T(8,128)(2,1)S(1)}, u32[]{:S(2)}, u32[]{:S(2)}) async-start(bf16[8,192,384]{2,1,0:T(8,128)(2,1)} %shard_map.87), calls=%async_computation | async-start | bytes 2359296 | tf_op jit(solution)/shard_map/all_to_all | solution.py:90
  13.1 0.0 copy-done.3
  13.1 0.0 copy-start.4
  13.1 0.6 broadcast_in_dim.13.gain_ref
  13.7 2.5 %shard_map.86.own_x = bf16[512,768]{1,0:T(8,128)(2,1)} custom-call(bf16[512,768]{1,0:T(8,128)(2,1)} %bitcast.7, f32[1,768]{1,0:T(1,128)} %broadcast_in_dim.13.gain_ref), custom_call_target="tpu_custom_call" | custom-call | tf_op jit(solution)/shard_map/pallas_call | solution.py:322
  16.2 2.9 %collective-permute-start = (bf16[512,768]{1,0:T(8,128)(2,1)}, bf16[512,768]{1,0:T(8,128)(2,1)S(1)}, u32[]{:S(2)}, u32[]{:S(2)}) collective-permute-start(bf16[512,768]{1,0:T(8,128)(2,1)} %shard_map.86.own_x), channel_id=1, source_target_pairs={{0,1},{1,0},{2,3},{3,2},{4,5},{5,4},{6,7},{7,6},{8,9},{9,8},{10,11... | collective-permute-start | bytes 2359304 | tf_op jit(solution)/shard_map/ppermute | solution.py:305
  19.1 0.5 broadcast.3
  19.6 0.0 copy-done.4
  19.6 0.7 reduce.3
  20.3 0.1 reshape.13
  20.3 10.9 %collective-permute-start.1 = (s32[32,16]{1,0:T(8,128)S(1)}, s32[32,16]{1,0:T(8,128)S(1)}, u32[]{:S(2)}, u32[]{:S(2)}) collective-permute-start(s32[32,16]{1,0:T(8,128)S(1)} %reshape.13), channel_id=1, source_target_pairs={{63,0},{62,1},{61,2},{60,3},{59,4},{58,5},{57,6},{56,7},{55,8},{54... | collective-permute-start | bytes 6152 | tf_op jit(solution)/shard_map/ppermute | solution.py:319
  31.2 2.0 %collective-permute-start.2 = (s32[32,16]{1,0:T(8,128)S(1)}, s32[32,16]{1,0:T(8,128)S(1)}, u32[]{:S(2)}, u32[]{:S(2)}) collective-permute-start(s32[32,16]{1,0:T(8,128)S(1)} %reshape.13), channel_id=1, source_target_pairs={{62,0},{63,1},{60,2},{61,3},{58,4},{59,5},{56,6},{57,7},{54,8},{55... | collective-permute-start | bytes 6152 | tf_op jit(solution)/shard_map/ppermute | solution.py:320
  33.3 0.6 pad_add_fusion.base_ref
  33.8 3.4 %collective-permute-done.1.own_ref = s32[32,16]{1,0:T(8,128)S(1)} collective-permute-done((s32[32,16]{1,0:T(8,128)S(1)}, s32[32,16]{1,0:T(8,128)S(1)}, u32[]{:S(2)}, u32[]{:S(2)}) %collective-permute-start.1) | collective-permute-done | bytes 2080 | tf_op jit(solution)/shard_map/ppermute | solution.py:319
  37.2 0.0 copy-start.9
  37.2 2.7 %collective-permute-done.2.other_ref = s32[32,16]{1,0:T(8,128)S(1)} collective-permute-done((s32[32,16]{1,0:T(8,128)S(1)}, s32[32,16]{1,0:T(8,128)S(1)}, u32[]{:S(2)}, u32[]{:S(2)}) %collective-permute-start.2) | collective-permute-done | bytes 2080 | tf_op jit(solution)/shard_map/ppermute | solution.py:320
  39.9 0.0 collective-permute-done.other_x
  39.9 0.0 copy-start.6
  39.9 0.0 all-to-all-done.packed_ref
  39.9 0.0 copy-done.9
  40.0 0.6 copy-done.10
  40.5 0.3 copy-done.6
  40.8 0.0 copy-start
  40.8 1.0 copy-done
  41.8 5.0 %shard_map.88 = (bf16[1024,384]{1,0:T(8,128)(2,1)}, bf16[1024,384]{1,0:T(8,128)(2,1)}, bf16[32,48,128]{2,1,0:T(8,128)(2,1)}) custom-call(s32[3]{0:T(128)} %pad_add_fusion.base_ref, s32[6]{0:T(128)} %offset_ref.3, bf16[512,768]{1,0:T(8,128)(2,1)} %shard_map.86.own_x, bf16[512,768]{1,0:T(8,128)(2,1)} %copy-done.6, bf16[8,192,384]{2,1,0:T(8,128)(2,1)} %copy-done, ...), custom_call_target="tpu_custom_call" | custom-call | flops 1207959552 | bytes 4194304 | tf_op jit(solution)/shard_map/pallas_call | solution.py:328
  46.8 30.4 %all_to_all.15.got_ref = bf16[32,48,128]{2,1,0:T(8,128)(2,1)} all-to-all(bf16[32,48,128]{2,1,0:T(8,128)(2,1)} %get-tuple-element.11), channel_id=1, replica_groups=mesh['dp'=8,'pos'=32,'core'=2] {'pos'}, dimensions={0} | all-to-all | bytes 786432 | tf_op jit(solution)/shard_map/all_to_all | solution.py:340
  77.2 3.7 %shard_map.90 = bf16[32,32,128]{2,1,0:T(8,128)(2,1)} custom-call(bf16[32,48,128]{2,1,0:T(8,128)(2,1)} %all_to_all.15.got_ref), custom_call_target="tpu_custom_call" | custom-call | flops 536870912 | bytes 1048576 | tf_op jit(solution)/shard_map/pallas_call | solution.py:342
  81.0 6.5 %all-to-all-start.2 = ((bf16[32,32,128]{2,1,0:T(8,128)(2,1)}), bf16[32,32,128]{2,1,0:T(8,128)(2,1)S(1)}, u32[]{:S(2)}, u32[]{:S(2)}) async-start(bf16[32,32,128]{2,1,0:T(8,128)(2,1)} %shard_map.90), calls=%async_computation.2 | async-start | bytes 524288 | tf_op jit(solution)/shard_map/all_to_all | solution.py:345
  87.5 11.6 %shard_map.89.near_ref = f32[1024,384]{1,0:T(8,128)} custom-call(bf16[1024,384]{1,0:T(8,128)(2,1)} %get-tuple-element.9.q_ref, bf16[1024,384]{1,0:T(8,128)(2,1)} %get-tuple-element.10.kv_ref), custom_call_target="tpu_custom_call" | custom-call | flops 1610612736 | bytes 3145728 | tf_op jit(solution)/shard_map/pallas_call | solution.py:179
  99.0 0.0 copy-start.5
  99.0 0.0 all-to-all-done.2.back_ref
  99.0 0.0 copy-start.2
  99.1 0.7 copy-done.2
  99.7 7.6 %shard_map.91 = (f32[1024,192]{1,0:T(8,128)}, bf16[1024,192]{1,0:T(8,128)(2,1)}) custom-call(s32[3]{0:T(128)} %pad_add_fusion.base_ref, s32[6]{0:T(128)} %offset_ref.3, f32[1024,384]{1,0:T(8,128)} %shard_map.89.near_ref, bf16[32,32,128]{2,1,0:T(8,128)(2,1)} %copy-done.2, s32[32,16]{1,0:T(8,128)} %copy-done.9, s32[32,16]{1,0:T(8,128)} %copy-done.10), custom_call_target="tpu_custom_call" | custom-call | flops 603979776 | bytes 3145728 | tf_op jit(solution)/shard_map/pallas_call | solution.py:347
  107.3 3.2 %collective-permute-start.3 = (bf16[1024,192]{1,0:T(8,128)(2,1)}, bf16[1024,192]{1,0:T(8,128)(2,1)S(1)}, u32[]{:S(2)}, u32[]{:S(2)}) collective-permute-start(bf16[1024,192]{1,0:T(8,128)(2,1)} %get-tuple-element.13), channel_id=1, source_target_pairs={{0,1},{1,0},{2,3},{3,2},{4,5},{5,4},{6,7},{7,6},{8,9},{9,8},{10,11... | collective-permute-start | bytes 1179656 | tf_op jit(solution)/shard_map/ppermute | solution.py:305
  110.6 1.0 slice.4
  111.6 0.0 copy-start.1
  111.6 1.9 %collective-permute-start.4 = (bf16[384,384]{1,0:T(8,128)(2,1)S(1)}, bf16[384,384]{1,0:T(8,128)(2,1)S(1)}, u32[]{:S(2)}, u32[]{:S(2)}) collective-permute-start(bf16[384,384]{1,0:T(8,128)(2,1)S(1)} %bitcast.8), channel_id=1, source_target_pairs={{0,1},{1,0},{2,3},{3,2},{4,5},{5,4},{6,7},{7,6},{8,9},{9,8},{10,11... | collective-permute-start | bytes 884744 | tf_op jit(solution)/shard_map/ppermute | solution.py:305
  113.5 0.0 copy-done.5
  113.5 0.7 reshape.14.gain_ref
  114.2 0.9 collective-permute-done.4.other_w
  115.1 0.0 collective-permute-done.3.got_ref
  115.1 0.0 copy-done.1
  115.1 0.7 copy-done.8
  115.8 0.2 copy-done.7
  116.0 3.9 %shard_map.92 = (bf16[512,768]{1,0:T(8,128)(2,1)}, bf16[512,768]{1,0:T(8,128)(2,1)}) custom-call(s32[1]{0:T(128)} %bitcast.core_ref, f32[1024,192]{1,0:T(8,128)} %get-tuple-element.12.keep_ref, bf16[1024,192]{1,0:T(8,128)(2,1)} %copy-done.7, f32[2,192]{1,0:T(2,128)} %reshape.14.gain_ref, bf16[384,384]{1,0:T(8,128)(2,1)} %bitcast.9, bf16[384,384]{1,0:T(8,128)(2,1)} %copy-done.8), custom_call_target="tpu_custom_call" | custom-call | flops 1207959552 | bytes 4194304 | tf_op jit(solution)/shard_map/pallas_call | solution.py:356
  (3 shorter events, 0.0 us)
Async XLA Ops:
  2.9 10.2 %copy-start.3 = (f32[768]{0:T(1024)S(1)}, f32[768]{0:T(1024)}, u32[]{:S(2)}) copy-start(f32[768]{0:T(1024)} %param.10) | copy-start | bytes 9220
  2.9 37.1 %all-to-all-start = ((bf16[8,192,384]{2,1,0:T(8,128)(2,1)}), bf16[8,192,384]{2,1,0:T(8,128)(2,1)S(1)}, u32[]{:S(2)}, u32[]{:S(2)}) async-start(bf16[8,192,384]{2,1,0:T(8,128)(2,1)} %shard_map.87), calls=%async_computation | async-start | bytes 2359296 | tf_op jit(solution)/shard_map/all_to_all | solution.py:90
  13.1 6.5 %copy-start.4 = (s32[1,512]{1,0:T(1,128)S(1)}, s32[1,512]{1,0:T(1,128)}, u32[]{:S(2)}) copy-start(s32[1,512]{1,0:T(1,128)} %param.8) | copy-start | bytes 6148
  16.2 23.7 %collective-permute-start = (bf16[512,768]{1,0:T(8,128)(2,1)}, bf16[512,768]{1,0:T(8,128)(2,1)S(1)}, u32[]{:S(2)}, u32[]{:S(2)}) collective-permute-start(bf16[512,768]{1,0:T(8,128)(2,1)} %shard_map.86.own_x), channel_id=1, source_target_pairs={{0,1},{1,0},{2,3},{3,2},{4,5},{5,4},{6,7},{7,6},{8,9},{9,8},{10,11... | collective-permute-start | bytes 2359304 | tf_op jit(solution)/shard_map/ppermute | solution.py:305
  20.3 16.9 %collective-permute-start.1 = (s32[32,16]{1,0:T(8,128)S(1)}, s32[32,16]{1,0:T(8,128)S(1)}, u32[]{:S(2)}, u32[]{:S(2)}) collective-permute-start(s32[32,16]{1,0:T(8,128)S(1)} %reshape.13), channel_id=1, source_target_pairs={{63,0},{62,1},{61,2},{60,3},{59,4},{58,5},{57,6},{56,7},{55,8},{54... | collective-permute-start | bytes 6152 | tf_op jit(solution)/shard_map/ppermute | solution.py:319
  31.2 8.7 %collective-permute-start.2 = (s32[32,16]{1,0:T(8,128)S(1)}, s32[32,16]{1,0:T(8,128)S(1)}, u32[]{:S(2)}, u32[]{:S(2)}) collective-permute-start(s32[32,16]{1,0:T(8,128)S(1)} %reshape.13), channel_id=1, source_target_pairs={{62,0},{63,1},{60,2},{61,3},{58,4},{59,5},{56,6},{57,7},{54,8},{55... | collective-permute-start | bytes 6152 | tf_op jit(solution)/shard_map/ppermute | solution.py:320
  37.2 2.7 %copy-start.9 = (s32[32,16]{1,0:T(8,128)}, s32[32,16]{1,0:T(8,128)S(1)}, u32[]{:S(2)}) copy-start(s32[32,16]{1,0:T(8,128)S(1)} %collective-permute-done.1.own_ref) | copy-start | bytes 6148
  39.9 0.6 copy-start.10
  39.9 0.9 copy-start.6
  40.8 1.0 copy-start
  81.0 18.1 %all-to-all-start.2 = ((bf16[32,32,128]{2,1,0:T(8,128)(2,1)}), bf16[32,32,128]{2,1,0:T(8,128)(2,1)S(1)}, u32[]{:S(2)}, u32[]{:S(2)}) async-start(bf16[32,32,128]{2,1,0:T(8,128)(2,1)} %shard_map.90), calls=%async_computation.2 | async-start | bytes 524288 | tf_op jit(solution)/shard_map/all_to_all | solution.py:345
  99.0 14.5 %copy-start.5 = (f32[384]{0:T(512)S(1)}, f32[384]{0:T(512)}, u32[]{:S(2)}) copy-start(f32[384]{0:T(512)} %param.12) | copy-start | bytes 4612
  99.0 0.7 copy-start.2
  107.3 7.7 %collective-permute-start.3 = (bf16[1024,192]{1,0:T(8,128)(2,1)}, bf16[1024,192]{1,0:T(8,128)(2,1)S(1)}, u32[]{:S(2)}, u32[]{:S(2)}) collective-permute-start(bf16[1024,192]{1,0:T(8,128)(2,1)} %get-tuple-element.13), channel_id=1, source_target_pairs={{0,1},{1,0},{2,3},{3,2},{4,5},{5,4},{6,7},{7,6},{8,9},{9,8},{10,11... | collective-permute-start | bytes 1179656 | tf_op jit(solution)/shard_map/ppermute | solution.py:305
  111.6 3.5 %copy-start.1 = (bf16[8,48,384]{2,1,0:T(8,128)(2,1)}, bf16[8,48,384]{2,1,0:T(8,128)(2,1)S(1)}, u32[]{:S(2)}) copy-start(bf16[8,48,384]{2,1,0:T(8,128)(2,1)S(1)} %slice.4) | copy-start | bytes 884740
  111.6 3.5 %collective-permute-start.4 = (bf16[384,384]{1,0:T(8,128)(2,1)S(1)}, bf16[384,384]{1,0:T(8,128)(2,1)S(1)}, u32[]{:S(2)}, u32[]{:S(2)}) collective-permute-start(bf16[384,384]{1,0:T(8,128)(2,1)S(1)} %bitcast.8), channel_id=1, source_target_pairs={{0,1},{1,0},{2,3},{3,2},{4,5},{5,4},{6,7},{7,6},{8,9},{9,8},{10,11... | collective-permute-start | bytes 884744 | tf_op jit(solution)/shard_map/ppermute | solution.py:305
  115.1 0.7 copy-start.8
  115.1 0.9 copy-start.7

commit v2 on v1

v2 whole, which is shorter than its diff:
```python
import jax
import jax.numpy as jnp
from jax import lax
from jax.experimental import pallas as pl
from jax.experimental.pallas import tpu as pltpu
from jax.sharding import Mesh, PartitionSpec as P


HEADS = 6
HEAD_DIM = 64
INNER = 384
D = 768
RATIO = 16
TOK = 512
SEG = 1024
HALF = 3
SPARSE = TOK // RATIO
POS = 32
DP_X, DP_Y = 4, 2
INTERPRET = False
LIMITS = [60 * 1024 * 1024, 60 * 1024 * 1024, 24 << 20, 24 << 20, 24 << 20]

eps_norm = 1e-05
EXP_SCALE = HEAD_DIM ** (-0.5) * 1.4426950408889634
SCALE = HEAD_DIM ** (-0.5)

F32 = jnp.float32
BF16 = jnp.bfloat16
VMEM = pl.BlockSpec(memory_space=pltpu.VMEM)
SMEM = pl.BlockSpec(memory_space=pltpu.SMEM)
HBM = pl.BlockSpec(memory_space=pltpu.HBM)


def call(kernel, out_shape, specs, scratch=(), flops=0, moved=0, limit=24 << 20, outs=None):
    single = not isinstance(out_shape, (list, tuple))
    return pl.pallas_call(
        kernel,
        out_shape=out_shape,
        in_specs=specs,
        out_specs=outs or (VMEM if single else [VMEM] * len(out_shape)),
        scratch_shapes=list(scratch),
        cost_estimate=pl.CostEstimate(flops=flops, bytes_accessed=moved, transcendentals=0),
        compiler_params=pltpu.CompilerParams(vmem_limit_bytes=limit),
        interpret=INTERPRET,
    )


def shape_of(*dims, dtype=BF16):
    return jax.ShapeDtypeStruct(dims, dtype)


def swap_halves(block):
    return jnp.concatenate([block[:, HEAD_DIM:], block[:, :HEAD_DIM]], axis=1)


def parts3(value):
    high = value.astype(BF16)
    rest = value - high.astype(F32)
    middle = rest.astype(BF16)
    low = (rest - middle.astype(F32)).astype(BF16)
    return high, middle, low


def pack_kernel(core_ref, proj_ref, outw_ref, packed_ref):
    for core in range(2):

        @pl.when(core_ref[0] == core)
        def _():
            for head in range(HALF):
                col = (core * HALF + head) * HEAD_DIM
                lanes = slice(head * 128, head * 128 + 128)
                keys = proj_ref[:, INNER + col : INNER + col + HEAD_DIM].astype(F32)
                values = proj_ref[:, 2 * INNER + col : 2 * INNER + col + HEAD_DIM].astype(F32)
                queries = proj_ref[:, col : col + HEAD_DIM].astype(F32)
                packed_ref[0:96, lanes] = jnp.concatenate([keys, values], axis=1).astype(BF16)
                packed_ref[96:144, lanes] = jnp.concatenate(
                    [queries[:48], queries[48:]], axis=1
                ).astype(BF16)
            packed_ref[144:192, :] = outw_ref[:, core * INNER : (core + 1) * INNER]


def pack_weights(core, projection, output_weight):
    return call(pack_kernel, shape_of(192, INNER), [SMEM, VMEM, VMEM])(
        core, projection, output_weight
    )


def fan_kernel(own_ref, other_ref, both_ref):
    for peer in range(DP_X):
        both_ref[peer, 0] = own_ref[...]
        both_ref[peer, 1] = other_ref[...]


def gather_weights(core, projection, output_weight):
    packed = pack_weights(core, projection, output_weight)
    other = lax.ppermute(packed, "yh", [(0, 1), (1, 0)])
    both = call(fan_kernel, shape_of(DP_X, DP_Y, 192, INNER), [VMEM, VMEM])(packed, other)
    got = lax.all_to_all(both, "x", 0, 0, tiled=True)
    return got.reshape(DP_X * DP_Y, 192, INNER)


def norm_kernel(x_ref, gain_ref, out_ref):
    gain = gain_ref[...].reshape(1, D)
    for row in range(0, TOK, 128):
        values = x_ref[row : row + 128, :].astype(F32)
        average = jnp.mean(values, axis=-1, keepdims=True)
        centred = values - average
        variance = jnp.mean(centred * centred, axis=-1, keepdims=True)
        out_ref[row : row + 128, :] = (
            centred * lax.rsqrt(variance + eps_norm) * gain
        ).astype(BF16)


def chosen_rows(view, offset, first, perm_ref):
    rows = lax.broadcasted_iota(jnp.int32, (SPARSE, 1), 0) * RATIO + offset
    if view == 0:
        return rows
    lane = lax.broadcasted_iota(jnp.int32, (SPARSE, TOK), 1)
    tiles = jnp.broadcast_to(perm_ref[...], (SPARSE, TOK))
    return jnp.sum(jnp.where(lane == rows, tiles, 0), axis=1, keepdims=True) - first


def one_hot(index, width):
    token = lax.broadcasted_iota(jnp.int32, (index.shape[0], width), 1)
    return jnp.where(token == index, 1.0, 0.0).astype(BF16)


def project_kernel(
    base_ref, offset_ref, own_x, other_x, packed_ref, own_ref, other_ref,
    kv_out, q_out, send_ref, outw_ref, w_ref, kv_ref, q_ref, sems,
):
    flip = base_ref[3]
    lane = lax.broadcasted_iota(jnp.int32, (48, 128), 1)
    for entry in range(8):
        shard = (entry - entry % 2) + (entry % 2 ^ flip)
        row = pl.multiple_of(shard * 96, 16)
        w_ref[pl.ds(row, 96), 0:INNER] = packed_ref[entry, 0:96, :]
        outw_ref[pl.ds(pl.multiple_of(shard * 48, 16), 48), :] = packed_ref[entry, 144:192, :]
        first, second = [], []
        for head in range(HALF):
            folded = packed_ref[entry, 96:144, head * 128 : head * 128 + 128].astype(F32)
            first.append(folded[:, :HEAD_DIM])
            second.append(folded[:, HEAD_DIM:])
        for at, pieces in ((0, first), (48, second)):
            w_ref[pl.ds(pl.multiple_of(row + at, 16), 48), INNER : INNER + 192] = jnp.concatenate(
                pieces, axis=1
            ).astype(BF16)
    q_lane = lax.broadcasted_iota(jnp.int32, (256, 128), 1)
    copies = []
    for part, x_ref in enumerate((own_x, other_x)):
        for step in range(0, TOK, 256):
            rows = slice(part * TOK + step, part * TOK + step + 256)
            out = jnp.dot(x_ref[step : step + 256, :], w_ref[...], preferred_element_type=F32)
            kv_ref[rows, :] = out[:, :INNER].astype(BF16)
            pair = out[:, INNER : INNER + 128]
            q_ref[rows, 0:128] = jnp.where(q_lane < HEAD_DIM, pair, 0.0).astype(BF16)
            q_ref[rows, 128:256] = jnp.where(q_lane < HEAD_DIM, swap_halves(pair), 0.0).astype(BF16)
            q_ref[rows, 256:384] = jnp.concatenate(
                [out[:, INNER + 128 :], jnp.zeros((256, HEAD_DIM), F32)], axis=1
            ).astype(BF16)
        rows = pl.ds(part * TOK, TOK)
        for at, (here, there) in enumerate(((kv_ref, kv_out), (q_ref, q_out))):
            copies.append(
                pltpu.make_async_copy(here.at[rows], there.at[rows], sems.at[part * 2 + at])
            )
            copies[-1].start()
    for view in range(2):
        for head in range(HALF):
            lanes = slice(head * 128, head * 128 + 128)
            offset = offset_ref[base_ref[0] * HALF + head]
            own = chosen_rows(view, offset, base_ref[1], own_ref)
            other = chosen_rows(view, offset, base_ref[2], other_ref) + TOK
            chosen = one_hot(jnp.concatenate([own, other], axis=0), SEG)
            far_kv = jnp.dot(chosen, kv_ref[:, lanes], preferred_element_type=F32).astype(BF16)
            far_q = jnp.dot(chosen, q_ref[:, lanes], preferred_element_type=F32)
            pair = (view * HALF + head) * 4
            for q_part in range(2):
                row = q_part * 16
                folded = (
                    far_q[row : row + 16] + swap_halves(far_q[SPARSE + row : SPARSE + row + 16])
                ).astype(BF16)
                for k_half in range(2):
                    peer = pair + q_part * 2 + k_half
                    send_ref[peer, 0:32, :] = far_kv[k_half * SPARSE : k_half * SPARSE + 32]
                    send_ref[peer, 32:48, :] = folded
    for peer in range(4 * 2 * HALF, POS):
        send_ref[peer] = jnp.zeros((48, 128), BF16)
    for copy in copies:
        copy.wait()


def near_kernel(q_ref, kv_ref, keep_ref, give_ref):
    keys = kv_ref[...]
    lane = lax.broadcasted_iota(jnp.int32, (SEG, 128), 1)
    values = jnp.where(lane < HEAD_DIM, swap_halves(keys.astype(F32)), 1.0).astype(BF16)
    scores = lax.dot_general(
        q_ref[...], keys, (((1,), (1,)), ((), ())), preferred_element_type=F32
    )
    row_max = jnp.max(scores, axis=1, keepdims=True)
    weights = jnp.exp2((scores - row_max) * EXP_SCALE).astype(BF16)
    summed = jnp.dot(weights, values, preferred_element_type=F32)
    out_lane = lax.broadcasted_iota(jnp.int32, summed.shape, 1)
    result = jnp.where(
        out_lane < HEAD_DIM, summed / swap_halves(summed), row_max * SCALE + jnp.log(summed)
    )

    @pl.when(pl.program_id(1) < 2)
    def _():
        keep_ref[...] = result

    @pl.when(pl.program_id(1) >= 2)
    def _():
        give_ref[...] = result


def near_level(queries, key_pairs):
    tile = 256
    half = shape_of(TOK, HALF * 128, dtype=F32)
    return pl.pallas_call(
        near_kernel,
        out_shape=[half, half],
        grid=(HALF, SEG // tile),
        in_specs=[
            pl.BlockSpec((tile, 128), lambda h, i: (i, h)),
            pl.BlockSpec((SEG, 128), lambda h, i: (0, h)),
        ],
        out_specs=[
            pl.BlockSpec((tile, 128), lambda h, i: (jnp.minimum(i, 1), h)),
            pl.BlockSpec((tile, 128), lambda h, i: (jnp.maximum(i - 2, 0), h)),
        ],
        cost_estimate=pl.CostEstimate(
            flops=4 * HALF * SEG * SEG * 128, bytes_accessed=3 << 20, transcendentals=HALF * SEG * SEG
        ),
        compiler_params=pltpu.CompilerParams(vmem_limit_bytes=LIMITS[1]),
        interpret=INTERPRET,
    )(queries, key_pairs)


def far_kernel(core_ref, got_ref, back_ref):
    core = core_ref[0]
    keys = got_ref[:, 0:32, :].reshape(POS * 32, 128)
    wide = got_ref[:, 32:48, :].reshape(POS * 16, 128).astype(F32)
    lane = lax.broadcasted_iota(jnp.int32, (POS * 32, 128), 1)
    values = jnp.where(lane < HEAD_DIM, swap_halves(keys.astype(F32)), 1.0).astype(BF16)
    q_lane = lax.broadcasted_iota(jnp.int32, (POS * 16, 128), 1)
    q_row = lax.broadcasted_iota(jnp.int32, (POS * 16, 128), 0)
    place = jnp.right_shift(q_lane, 4)
    mine = jnp.bitwise_and(q_lane, 15) == jnp.bitwise_and(q_row, 15)
    source = lax.broadcasted_iota(jnp.int32, (POS, POS * 16), 0)
    member = jnp.right_shift(lax.broadcasted_iota(jnp.int32, (POS, POS * 16), 1), 4)
    spread = jnp.where(source == member, 1.0, 0.0).astype(BF16)
    for part in range(2):
        queries = jnp.where(q_lane < HEAD_DIM, wide if part == 0 else swap_halves(wide), 0.0)
        scores = lax.dot_general(
            queries.astype(BF16), keys, (((1,), (1,)), ((), ())), preferred_element_type=F32
        )
        row_max = jnp.max(scores, axis=1, keepdims=True)
        weights = jnp.exp2((scores - row_max) * EXP_SCALE).astype(BF16)
        summed = jnp.dot(weights, values, preferred_element_type=F32)
        swapped = swap_halves(summed)
        out = (summed / swapped).reshape(POS, 16, 128)
        packed = jnp.concatenate([out[:, 0:8, :HEAD_DIM], out[:, 8:16, :HEAD_DIM]], axis=2)
        high, middle, low = parts3(row_max * SCALE + jnp.log(swapped))
        stats = jnp.where(
            place == 0, high, jnp.where(place == 1, middle, jnp.where(place == 2, low, 0.0))
        )
        stats = jnp.where(mine, stats, 0.0).astype(BF16)
        rows = jnp.dot(spread, stats, preferred_element_type=F32)
        rows = jnp.broadcast_to(rows[:, None, :], (POS, 8, 128))
        block = jnp.concatenate([packed, rows], axis=1).astype(BF16)
        back_ref[:, pl.ds(core if part == 0 else 1 - core, 1)] = block[:, None]


def prepare_kernel(
    base_ref, offset_ref, keep_ref, got_ref, own_ref, gain_ref, own_w, other_w,
    dense_ref, rows_ref, spread_ref, order_ref, weight_ref,
):
    core = base_ref[0]
    width = HALF * HEAD_DIM
    hots = [[], []]
    for group, near_ref in enumerate((keep_ref, got_ref)):
        dense_ref[:, group * width : (group + 1) * width] = jnp.concatenate(
            [near_ref[:, head * 128 : head * 128 + HEAD_DIM] for head in range(HALF)], axis=1
        )
        heads = core if group == 0 else 1 - core
        for head in range(HALF):
            pieces = jnp.concatenate(parts3(near_ref[:, head * 128 : head * 128 + 128]), axis=1)
            offset = offset_ref[heads * HALF + head]
            for view in range(2):
                chosen = one_hot(chosen_rows(view, offset, base_ref[1], own_ref), TOK)
                hots[view].append(chosen)
                taken = jnp.dot(chosen, pieces, preferred_element_type=F32)
                at = group * 192 + (view * HALF + head) * SPARSE
                rows_ref[at : at + SPARSE, :] = taken[:, :128] + taken[:, 128:256] + taken[:, 256:]
    for view in range(2):
        spread_ref[view] = jnp.concatenate(hots[view], axis=0).astype(F32).T.astype(BF16)
    gain = gain_ref[...].reshape(1, INNER)
    order_ref[...] = jnp.where(
        core == 0, gain, jnp.concatenate([gain[:, width:], gain[:, :width]], axis=1)
    )
    own_rows = pl.ds(pl.multiple_of(core * width, 64), width)
    other_rows = pl.ds(pl.multiple_of((1 - core) * width, 64), width)
    for part, place in ((own_w, core), (other_w, 1 - core)):
        cols = pl.ds(pl.multiple_of(place * INNER, 128), INNER)
        weight_ref[0:width, cols] = part[own_rows, :]
        weight_ref[width:INNER, cols] = part[other_rows, :]


def output_kernel(
    core_ref, far_ref, dense_ref, rows_ref, spread_ref, gain_ref, weight_ref, plain_ref, flip_ref
):
    core = core_ref[0]
    lane = lax.broadcasted_iota(jnp.int32, (192, 128), 1)
    mine = jnp.bitwise_and(lane, 15) == jnp.bitwise_and(
        lax.broadcasted_iota(jnp.int32, (192, 128), 0), 15
    )
    deltas = []
    for group in range(2):
        outs, logs = [], []
        for k_half in range(2):
            blocks, stats = [], []
            for pair in range(2 * HALF):
                for q_part in range(2):
                    peer = (pair * 4 + q_part * 2 + k_half) * 2
                    block = far_ref[peer + (core if group == 0 else 1 - core)].astype(F32)
                    blocks += [block[0:8, :HEAD_DIM], block[0:8, HEAD_DIM:]]
                    stats += [block[8:16], block[8:16]]
            outs.append(jnp.concatenate(blocks, axis=0))
            found = jnp.where(mine, jnp.concatenate(stats, axis=0), 0.0)
            logs.append(jnp.sum(found, axis=1, keepdims=True))
        top = jnp.maximum(logs[0], logs[1])
        weight0, weight1 = jnp.exp(logs[0] - top), jnp.exp(logs[1] - top)
        joint = weight0 + weight1
        far = (weight0 * outs[0] + weight1 * outs[1]) / joint
        near = rows_ref[group * 192 : group * 192 + 192, :]
        gap = near[:, HEAD_DIM : HEAD_DIM + 1] - (top + jnp.log(joint))
        deltas.append((far - near[:, :HEAD_DIM]) / (1.0 + jnp.exp(gap)))
    row = jnp.right_shift(lax.broadcasted_iota(jnp.int32, (192, INNER), 0), 5)
    col = jnp.right_shift(lax.broadcasted_iota(jnp.int32, (192, INNER), 1), 6)
    for view, out_ref in enumerate((plain_ref, flip_ref)):
        delta = jnp.concatenate([d[view * 96 : view * 96 + 96] for d in deltas], axis=0)
        blocks = jnp.where(row == col, jnp.concatenate([delta] * HEADS, axis=1), 0.0).astype(BF16)
        for at in range(0, TOK, 256):
            attended = dense_ref[at : at + 256, :] + jnp.dot(
                spread_ref[view, at : at + 256, :], blocks, preferred_element_type=F32
            )
            average = jnp.mean(attended, axis=-1, keepdims=True)
            centred = attended - average
            variance = jnp.mean(centred * centred, axis=-1, keepdims=True)
            mixed = (centred * lax.rsqrt(variance + eps_norm) * gain_ref[...]).astype(BF16)
            out_ref[at : at + 256, :] = jnp.dot(
                mixed, weight_ref[...], preferred_element_type=F32
            ).astype(BF16)


def core_swap(block):
    return lax.ppermute(block, "core", [(0, 1), (1, 0)])


def layer(
    tile_features, flip_perm, head_offsets, input_gain, projection, output_gain, output_weight
):
    core = lax.axis_index("core").astype(jnp.int32)
    pos = lax.axis_index("pos").astype(jnp.int32)
    rank = pos * 2 + core
    core_id = core[None]
    base = jnp.stack([core, rank * TOK, (rank ^ 1) * TOK, lax.axis_index("yh").astype(jnp.int32)])

    packed = gather_weights(core_id, projection, output_weight)
    own_x = call(norm_kernel, shape_of(TOK, D), [VMEM, VMEM], moved=2 << 20)(
        tile_features[0], input_gain
    )
    other_x = core_swap(own_x)
    last = 2 * POS - 1
    ctx = ("pos", "core")
    own_perm = lax.ppermute(flip_perm, ctx, [(last - r, r) for r in range(2 * POS)])
    other_perm = lax.ppermute(flip_perm, ctx, [(last - (r ^ 1), r) for r in range(2 * POS)])

    key_pairs, queries, send, own_w = call(
        project_kernel,
        [
            shape_of(SEG, INNER),
            shape_of(SEG, INNER),
            shape_of(POS, 48, 128),
            shape_of(INNER, INNER),
        ],
        [SMEM, SMEM, VMEM, VMEM, VMEM, VMEM, VMEM],
        [
            pltpu.VMEM((D, INNER + 192), BF16),
            pltpu.VMEM((SEG, INNER), BF16),
            pltpu.VMEM((SEG, INNER), BF16),
            pltpu.SemaphoreType.DMA((4,)),
        ],
        outs=[HBM, HBM, VMEM, VMEM],
        flops=2 * SEG * D * 576,
        moved=4 << 20,
        limit=LIMITS[0],
    )(base, head_offsets, own_x, other_x, packed, own_perm, other_perm)

    got = lax.all_to_all(send, "pos", 0, 0, tiled=True)
    keep, give = near_level(queries, key_pairs)
    near_got = core_swap(give)
    back = call(
        far_kernel, shape_of(POS, 2, 16, 128), [SMEM, VMEM], flops=4 * SEG * SEG * 128, moved=1 << 20,
        limit=LIMITS[2],
    )(core_id, got)
    far = lax.all_to_all(back.reshape(2 * POS, 16, 128), ctx, 0, 0, tiled=True)

    other_w = core_swap(own_w)
    prepared = call(
        prepare_kernel,
        [
            shape_of(TOK, INNER, dtype=F32),
            shape_of(INNER, 128, dtype=F32),
            shape_of(2, TOK, 192),
            shape_of(1, INNER, dtype=F32),
            shape_of(INNER, D),
        ],
        [SMEM, SMEM, VMEM, VMEM, VMEM, VMEM, VMEM, VMEM],
        flops=1 << 28,
        moved=4 << 20,
        limit=LIMITS[3],
    )(base, head_offsets, keep, near_got, own_perm, output_gain, own_w, other_w)

    plain_view, flipped_view = call(
        output_kernel,
        [shape_of(TOK, D), shape_of(TOK, D)],
        [SMEM, VMEM, VMEM, VMEM, VMEM, VMEM, VMEM],
        flops=4 * SEG * INNER * D,
        moved=4 << 20,
        limit=LIMITS[4],
    )(core_id, far, *prepared)
    return (plain_view[None], flipped_view[None])


def solution(mesh):
    fine = Mesh(mesh.devices.reshape(DP_X, DP_Y, POS, 2), ("x", "yh", "pos", "core"))
    dp, ctx = ("x", "yh"), ("pos", "core")
    placed = (P(dp, ctx, None), P(dp, ctx), P(), P(), P(dp, None), P(), P(dp, None))
    return jax.shard_map(
        layer,
        mesh=fine,
        in_specs=placed,
        out_specs=(P(dp, ctx, None), P(dp, ctx, None)),
        check_vma=False,
    )
```

time: 121 us -> 109 us (0.901)
  the two profiles are of different devices: /device:TPU:1 before, /device:TPU:59 now
where the time goes in v2:
time: 109 us; the launch traced here: 108 us
  starting transfers between devices  50.7 us (47%)
  Pallas kernels  27.5 us (25%)
  waiting for transfers between devices  21.5 us (20%)
  local copies, waits for them, and re-layouts  6.42 us (6%)
    ppermute x1, starting transfers between devices, layer(): lax.ppermute(flip_perm, ctx, [(last - (r ^ 1), r) for r in range(2 * POS)])  13 us
    pallas_call x1, Pallas kernels, near_level(): pl.pallas_call(near_kernel, out_shape=[half, half], grid=(HALF, SEG // ti...  11.8 us
    all_to_all x1, starting transfers between devices, layer(): far = lax.all_to_all(back.reshape(2 * POS, 16, 128), ctx, 0, 0, tiled=True)  10.4 us
    ppermute x1, waiting for transfers between devices, gather_weights(): other = lax.ppermute(packed, 'yh', [(0, 1), (1, 0)])  9.31 us
    ppermute x3, starting transfers between devices, core_swap(): return lax.ppermute(block, 'core', [(0, 1), (1, 0)])  8.97 us
    all_to_all x1, starting transfers between devices, layer(): got = lax.all_to_all(send, 'pos', 0, 0, tiled=True)  7.44 us
    unnamed x38, local copies, waits for them, and re-layouts  6.42 us
    ppermute x1, waiting for transfers between devices, layer(): lax.ppermute(flip_perm, ctx, [(last - r, r) for r in range(2 * POS)])  6.21 us
  transfers between devices with their start and end apart: 9, of which 4 were waited for; matrix products, arithmetic and copies ran while one was open for 1% of the time, Pallas kernels for 16%

profile of v2, /device:TPU:59, one launch (start us, length us, event | category | flops | bytes accessed | tf_op | source)
XLA Modules:
  0.0 107.8 jit_solution(10756750927635281113)
XLA Ops:
  0.6 0.0 copy-start.4
  0.6 0.9 copy-done.4
  1.6 0.9 copy-done.5
  2.5 0.1 shard_map.87.own_ref
  2.6 4.4 %collective-permute-start.1 = (bf16[192,384]{1,0:T(8,128)(2,1)S(1)}, bf16[192,384]{1,0:T(8,128)(2,1)S(1)}, u32[]{:S(2)}, u32[]{:S(2)}) collective-permute-start(bf16[192,384]{1,0:T(8,128)(2,1)S(1)} %shard_map.87.own_ref), channel_id=1, source_target_pairs={{0,64},{64,0},{1,65},{65,1},{2,66},{66,2},{3,67},{67,3},{4,68},{68... | collective-permute-start | bytes 442376 | tf_op jit(solution)/shard_map/ppermute | solution.py:96
  7.0 9.3 %collective-permute-done.1.other_ref = bf16[192,384]{1,0:T(8,128)(2,1)S(1)} collective-permute-done((bf16[192,384]{1,0:T(8,128)(2,1)S(1)}, bf16[192,384]{1,0:T(8,128)(2,1)S(1)}, u32[]{:S(2)}, u32[]{:S(2)}) %collective-permute-start.1) | collective-permute-done | bytes 147488 | tf_op jit(solution)/shard_map/ppermute | solution.py:96
  16.3 1.1 %shard_map.88 = bf16[4,2,192,384]{3,2,1,0:T(8,128)(2,1)} custom-call(bf16[192,384]{1,0:T(8,128)(2,1)S(1)} %shard_map.87.own_ref, bf16[192,384]{1,0:T(8,128)(2,1)S(1)} %collective-permute-done.1.other_ref), custom_call_target="tpu_custom_call" | custom-call | tf_op jit(solution)/shard_map/pallas_call | solution.py:97
  17.5 4.6 %all-to-all-start = ((bf16[4,2,192,384]{3,2,1,0:T(8,128)(2,1)}), bf16[4,2,192,384]{3,2,1,0:T(8,128)(2,1)}, u32[]{:S(2)}, u32[]{:S(2)}) async-start(bf16[4,2,192,384]{3,2,1,0:T(8,128)(2,1)} %shard_map.88), calls=%async_computation | async-start | bytes 2359296 | tf_op jit(solution)/shard_map/all_to_all | solution.py:98
  22.1 0.0 copy-done
  22.1 0.0 copy-done.6
  22.1 0.5 shard_map.86.own_x
  22.6 0.0 copy-start.1
  22.6 3.8 %collective-permute-start = (bf16[512,768]{1,0:T(8,128)(2,1)S(1)}, bf16[512,768]{1,0:T(8,128)(2,1)S(1)}, u32[]{:S(2)}, u32[]{:S(2)}) collective-permute-start(bf16[512,768]{1,0:T(8,128)(2,1)S(1)} %shard_map.86.own_x), channel_id=1, source_target_pairs={{0,1},{1,0},{2,3},{3,2},{4,5},{5,4},{6,7},{7,6},{8,9},{9,8},{10,11... | collective-permute-start | bytes 2359304 | tf_op jit(solution)/shard_map/ppermute | solution.py:357
  26.4 0.0 copy-done.17
  26.4 13.0 %collective-permute-start.3 = (s32[1,512]{1,0:T(1,128)S(1)}, s32[1,512]{1,0:T(1,128)S(1)}, u32[]{:S(2)}, u32[]{:S(2)}) collective-permute-start(s32[1,512]{1,0:T(1,128)S(1)} %copy-done.17), channel_id=1, source_target_pairs={{62,0},{63,1},{60,2},{61,3},{58,4},{59,5},{56,6},{57,7},{54,8},{55... | collective-permute-start | bytes 6152 | tf_op jit(solution)/shard_map/ppermute | solution.py:377
  39.4 1.9 %collective-permute-start.2 = (s32[1,512]{1,0:T(1,128)S(1)}, s32[1,512]{1,0:T(1,128)S(1)}, u32[]{:S(2)}, u32[]{:S(2)}) collective-permute-start(s32[1,512]{1,0:T(1,128)S(1)} %copy-done.17), channel_id=1, source_target_pairs={{63,0},{62,1},{61,2},{60,3},{59,4},{58,5},{57,6},{56,7},{55,8},{54... | collective-permute-start | bytes 6152 | tf_op jit(solution)/shard_map/ppermute | solution.py:376
  41.3 0.7 pad_add_fusion.base_ref
  41.9 0.0 collective-permute-done.3.other_ref
  42.0 6.2 %collective-permute-done.2.own_ref = s32[1,512]{1,0:T(1,128)S(1)} collective-permute-done((s32[1,512]{1,0:T(1,128)S(1)}, s32[1,512]{1,0:T(1,128)S(1)}, u32[]{:S(2)}, u32[]{:S(2)}) %collective-permute-start.2) | collective-permute-done | bytes 2080 | tf_op jit(solution)/shard_map/ppermute | solution.py:376
  48.2 0.0 collective-permute-done.other_x
  48.2 0.0 all-to-all-done
  48.2 0.0 copy-done.1
  48.2 0.0 copy-done.18
  48.2 0.6 copy-done.8
  48.8 0.3 copy-done.16
  49.1 5.1 %shard_map.89 = (bf16[1024,384]{1,0:T(8,128)(2,1)}, bf16[1024,384]{1,0:T(8,128)(2,1)}, bf16[32,48,128]{2,1,0:T(8,128)(2,1)}, bf16[384,384]{1,0:T(8,128)(2,1)}) custom-call(s32[4]{0:T(128)} %pad_add_fusion.base_ref, s32[6]{0:T(128)} %offset_ref.3, bf16[512,768]{1,0:T(8,128)(2,1)} %copy-done.1, bf16[512,768]{1,0:T(8,128)(2,1)} %copy-done.16, ...), custom_call_target="tpu_custom_call" | custom-call | flops 905969664 | bytes 4194304 | tf_op jit(solution)/shard_map/pallas_call | solution.py:379
  54.1 7.4 %all-to-all-start.1 = ((bf16[32,48,128]{2,1,0:T(8,128)(2,1)}), bf16[32,48,128]{2,1,0:T(8,128)(2,1)S(1)}, u32[]{:S(2)}, u32[]{:S(2)}) async-start(bf16[32,48,128]{2,1,0:T(8,128)(2,1)} %get-tuple-element.15), calls=%async_computation.1 | async-start | bytes 786432 | tf_op jit(solution)/shard_map/all_to_all | solution.py:400
  61.6 11.8 %shard_map.91 = (f32[512,384]{1,0:T(8,128)}, f32[512,384]{1,0:T(8,128)}) custom-call(bf16[1024,384]{1,0:T(8,128)(2,1)} %get-tuple-element.16.q_ref, bf16[1024,384]{1,0:T(8,128)(2,1)} %get-tuple-element.17.kv_ref), custom_call_target="tpu_custom_call" | custom-call | flops 1610612736 | bytes 3145728 | tf_op jit(solution)/shard_map/pallas_call | solution.py:219
  73.4 0.0 copy-start.9
  73.4 0.0 copy-start.10
  73.4 0.0 copy-start.11
  73.4 2.9 %collective-permute-start.4 = (f32[512,384]{1,0:T(8,128)}, f32[512,384]{1,0:T(8,128)S(1)}, u32[]{:S(2)}, u32[]{:S(2)}) collective-permute-start(f32[512,384]{1,0:T(8,128)} %get-tuple-element.19), channel_id=1, source_target_pairs={{0,1},{1,0},{2,3},{3,2},{4,5},{5,4},{6,7},{7,6},{8,9},{9,8},{10,11... | collective-permute-start | bytes 2359304 | tf_op jit(solution)/shard_map/ppermute | solution.py:357
  76.3 0.0 all-to-all-done.1.got_ref
  76.3 3.7 %shard_map.90 = bf16[32,2,16,128]{3,2,1,0:T(8,128)(2,1)} custom-call(s32[1]{0:T(128)} %bitcast.core_ref, bf16[32,48,128]{2,1,0:T(8,128)(2,1)S(1)} %all-to-all-done.1.got_ref), custom_call_target="tpu_custom_call" | custom-call | flops 536870912 | bytes 1048576 | tf_op jit(solution)/shard_map/pallas_call | solution.py:403
  80.0 10.4 %all-to-all-start.2 = ((bf16[64,16,128]{2,1,0:T(8,128)(2,1)}), bf16[64,16,128]{2,1,0:T(8,128)(2,1)S(1)}, u32[]{:S(2)}, u32[]{:S(2)}) async-start(bf16[64,16,128]{2,1,0:T(8,128)(2,1)} %bitcast.6), calls=%async_computation.2 | async-start | bytes 524288 | tf_op jit(solution)/shard_map/all_to_all | solution.py:407
  90.4 0.0 copy-done.3
  90.4 2.3 %collective-permute-start.5 = (bf16[384,384]{1,0:T(8,128)(2,1)S(1)}, bf16[384,384]{1,0:T(8,128)(2,1)S(1)}, u32[]{:S(2)}, u32[]{:S(2)}) collective-permute-start(bf16[384,384]{1,0:T(8,128)(2,1)S(1)} %copy-done.3), channel_id=1, source_target_pairs={{0,1},{1,0},{2,3},{3,2},{4,5},{5,4},{6,7},{7,6},{8,9},{9,8},{10,11... | collective-permute-start | bytes 884744 | tf_op jit(solution)/shard_map/ppermute | solution.py:357
  92.7 1.2 %collective-permute-done.5.other_w = bf16[384,384]{1,0:T(8,128)(2,1)S(1)} collective-permute-done((bf16[384,384]{1,0:T(8,128)(2,1)S(1)}, bf16[384,384]{1,0:T(8,128)(2,1)S(1)}, u32[]{:S(2)}, u32[]{:S(2)}) %collective-permute-start.5) | collective-permute-done | bytes 294944 | tf_op jit(solution)/shard_map/ppermute | solution.py:357
  93.9 0.0 collective-permute-done.4.got_ref
  93.9 0.0 copy-done.2
  94.0 1.5 %shard_map.92 = (f32[512,384]{1,0:T(8,128)S(1)}, f32[384,128]{1,0:T(8,128)S(1)}, bf16[2,512,192]{2,1,0:T(8,128)(2,1)S(1)}, f32[1,384]{1,0:T(1,128)S(1)}, bf16[384,768]{1,0:T(8,128)(2,1)S(1)}) custom-call(s32[4]{0:T(128)S(1)} %copy-done.10, s32[6]{0:T(128)S(1)} %copy-done.11, f32[512,384]{1,0:T(8,128)S(1)} %copy-done.2, ...), custom_call_target="tpu_custom_call" | custom-call | flops 268435456 | bytes 4194304 | tf_op jit(solution)/shard_map/pallas_call | solution.py:410
  95.5 0.0 copy-start.12
  95.5 0.8 copy-done.12
  96.3 0.8 copy-done.14
  97.1 4.8 %all-to-all-done.2.far_ref = bf16[64,16,128]{2,1,0:T(8,128)(2,1)S(1)} async-done(((bf16[64,16,128]{2,1,0:T(8,128)(2,1)}), bf16[64,16,128]{2,1,0:T(8,128)(2,1)S(1)}, u32[]{:S(2)}, u32[]{:S(2)}) %all-to-all-start.2) | async-done | bytes 262176 | tf_op jit(solution)/shard_map/all_to_all | solution.py:407
  101.9 1.1 copy-done.13
  103.0 1.0 copy-done.15
  104.0 3.8 %shard_map.93 = (bf16[512,768]{1,0:T(8,128)(2,1)}, bf16[512,768]{1,0:T(8,128)(2,1)}) custom-call(s32[1]{0:T(128)} %bitcast.core_ref, bf16[64,16,128]{2,1,0:T(8,128)(2,1)S(1)} %all-to-all-done.2.far_ref, f32[512,384]{1,0:T(8,128)S(1)} %get-tuple-element.21.dense_ref, f32[384,128]{1,0:T(8,128)S(1)} %get-tuple-element.22.rows_ref, ...), custom_call_target="tpu_custom_call" | custom-call | flops 1207959552 | bytes 4194304 | tf_op jit(solution)/shard_map/pallas_call | solution.py:425
  (17 shorter events, 0.0 us)
Async XLA Ops:
  0.6 0.9 copy-start.4
  1.6 0.9 copy-start.5
  2.6 13.8 %collective-permute-start.1 = (bf16[192,384]{1,0:T(8,128)(2,1)S(1)}, bf16[192,384]{1,0:T(8,128)(2,1)S(1)}, u32[]{:S(2)}, u32[]{:S(2)}) collective-permute-start(bf16[192,384]{1,0:T(8,128)(2,1)S(1)} %shard_map.87.own_ref), channel_id=1, source_target_pairs={{0,64},{64,0},{1,65},{65,1},{2,66},{66,2},{3,67},{67,3},{4,68},{68... | collective-permute-start | bytes 442376 | tf_op jit(solution)/shard_map/ppermute | solution.py:96
  17.5 4.6 %copy-start = (bf16[1,512,768]{2,1,0:T(8,128)(2,1)S(1)}, bf16[1,512,768]{2,1,0:T(8,128)(2,1)}, u32[]{:S(2)}) copy-start(bf16[1,512,768]{2,1,0:T(8,128)(2,1)} %param.7) | copy-start | bytes 2359300
  17.5 4.6 %copy-start.6 = (f32[768]{0:T(1024)S(1)}, f32[768]{0:T(1024)}, u32[]{:S(2)}) copy-start(f32[768]{0:T(1024)} %gain_ref.2) | copy-start | bytes 9220
  17.5 30.7 %all-to-all-start = ((bf16[4,2,192,384]{3,2,1,0:T(8,128)(2,1)}), bf16[4,2,192,384]{3,2,1,0:T(8,128)(2,1)}, u32[]{:S(2)}, u32[]{:S(2)}) async-start(bf16[4,2,192,384]{3,2,1,0:T(8,128)(2,1)} %shard_map.88), calls=%async_computation | async-start | bytes 2359296 | tf_op jit(solution)/shard_map/all_to_all | solution.py:98
  22.1 4.3 %copy-start.17 = (s32[1,512]{1,0:T(1,128)S(1)}, s32[1,512]{1,0:T(1,128)}, u32[]{:S(2)}) copy-start(s32[1,512]{1,0:T(1,128)} %param.8) | copy-start | bytes 6148
  22.6 25.6 %copy-start.1 = (bf16[512,768]{1,0:T(8,128)(2,1)}, bf16[512,768]{1,0:T(8,128)(2,1)S(1)}, u32[]{:S(2)}) copy-start(bf16[512,768]{1,0:T(8,128)(2,1)S(1)} %shard_map.86.own_x) | copy-start | bytes 2359300
  22.6 25.6 %collective-permute-start = (bf16[512,768]{1,0:T(8,128)(2,1)S(1)}, bf16[512,768]{1,0:T(8,128)(2,1)S(1)}, u32[]{:S(2)}, u32[]{:S(2)}) collective-permute-start(bf16[512,768]{1,0:T(8,128)(2,1)S(1)} %shard_map.86.own_x), channel_id=1, source_target_pairs={{0,1},{1,0},{2,3},{3,2},{4,5},{5,4},{6,7},{7,6},{8,9},{9,8},{10,11... | collective-permute-start | bytes 2359304 | tf_op jit(solution)/shard_map/ppermute | solution.py:357
  26.4 15.6 %collective-permute-start.3 = (s32[1,512]{1,0:T(1,128)S(1)}, s32[1,512]{1,0:T(1,128)S(1)}, u32[]{:S(2)}, u32[]{:S(2)}) collective-permute-start(s32[1,512]{1,0:T(1,128)S(1)} %copy-done.17), channel_id=1, source_target_pairs={{62,0},{63,1},{60,2},{61,3},{58,4},{59,5},{56,6},{57,7},{54,8},{55... | collective-permute-start | bytes 6152 | tf_op jit(solution)/shard_map/ppermute | solution.py:377
  39.4 8.8 %collective-permute-start.2 = (s32[1,512]{1,0:T(1,128)S(1)}, s32[1,512]{1,0:T(1,128)S(1)}, u32[]{:S(2)}, u32[]{:S(2)}) collective-permute-start(s32[1,512]{1,0:T(1,128)S(1)} %copy-done.17), channel_id=1, source_target_pairs={{63,0},{62,1},{61,2},{60,3},{59,4},{58,5},{57,6},{56,7},{55,8},{54... | collective-permute-start | bytes 6152 | tf_op jit(solution)/shard_map/ppermute | solution.py:376
  42.0 6.2 %copy-start.18 = (s32[1,512]{1,0:T(1,128)}, s32[1,512]{1,0:T(1,128)S(1)}, u32[]{:S(2)}) copy-start(s32[1,512]{1,0:T(1,128)S(1)} %collective-permute-done.3.other_ref) | copy-start | bytes 6148
  48.2 0.6 copy-start.8
  48.2 0.9 copy-start.16
  54.1 22.2 %all-to-all-start.1 = ((bf16[32,48,128]{2,1,0:T(8,128)(2,1)}), bf16[32,48,128]{2,1,0:T(8,128)(2,1)S(1)}, u32[]{:S(2)}, u32[]{:S(2)}) async-start(bf16[32,48,128]{2,1,0:T(8,128)(2,1)} %get-tuple-element.15), calls=%async_computation.1 | async-start | bytes 786432 | tf_op jit(solution)/shard_map/all_to_all | solution.py:400
  73.3 17.1 %copy-start.3 = (bf16[384,384]{1,0:T(8,128)(2,1)S(1)}, bf16[384,384]{1,0:T(8,128)(2,1)}, u32[]{:S(2)}) copy-start(bf16[384,384]{1,0:T(8,128)(2,1)} %get-tuple-element.20.own_w) | copy-start | bytes 884740
  73.3 20.6 %copy-start.2 = (f32[512,384]{1,0:T(8,128)S(1)}, f32[512,384]{1,0:T(8,128)}, u32[]{:S(2)}) copy-start(f32[512,384]{1,0:T(8,128)} %get-tuple-element.18.keep_ref) | copy-start | bytes 2359300
  73.3 20.6 %copy-start.7 = (f32[384]{0:T(512)S(1)}, f32[384]{0:T(512)}, u32[]{:S(2)}) copy-start(f32[384]{0:T(512)} %gain_ref.3) | copy-start | bytes 4612
  73.4 20.6 %copy-start.9 = (s32[1,512]{1,0:T(1,128)S(1)}, s32[1,512]{1,0:T(1,128)}, u32[]{:S(2)}) copy-start(s32[1,512]{1,0:T(1,128)} %copy-done.8) | copy-start | bytes 6148
  73.4 20.6 %copy-start.10 = (s32[4]{0:T(128)S(1)}, s32[4]{0:T(128)}, u32[]{:S(2)}) copy-start(s32[4]{0:T(128)} %pad_add_fusion.base_ref) | copy-start | bytes 52
  73.4 20.6 %copy-start.11 = (s32[6]{0:T(128)S(1)}, s32[6]{0:T(128)}, u32[]{:S(2)}) copy-start(s32[6]{0:T(128)} %offset_ref.3) | copy-start | bytes 76
  73.4 20.5 %collective-permute-start.4 = (f32[512,384]{1,0:T(8,128)}, f32[512,384]{1,0:T(8,128)S(1)}, u32[]{:S(2)}, u32[]{:S(2)}) collective-permute-start(f32[512,384]{1,0:T(8,128)} %get-tuple-element.19), channel_id=1, source_target_pairs={{0,1},{1,0},{2,3},{3,2},{4,5},{5,4},{6,7},{7,6},{8,9},{9,8},{10,11... | collective-permute-start | bytes 2359304 | tf_op jit(solution)/shard_map/ppermute | solution.py:357
  80.0 21.9 %all-to-all-start.2 = ((bf16[64,16,128]{2,1,0:T(8,128)(2,1)}), bf16[64,16,128]{2,1,0:T(8,128)(2,1)S(1)}, u32[]{:S(2)}, u32[]{:S(2)}) async-start(bf16[64,16,128]{2,1,0:T(8,128)(2,1)} %bitcast.6), calls=%async_computation.2 | async-start | bytes 524288 | tf_op jit(solution)/shard_map/all_to_all | solution.py:407
  90.4 3.5 %collective-permute-start.5 = (bf16[384,384]{1,0:T(8,128)(2,1)S(1)}, bf16[384,384]{1,0:T(8,128)(2,1)S(1)}, u32[]{:S(2)}, u32[]{:S(2)}) collective-permute-start(bf16[384,384]{1,0:T(8,128)(2,1)S(1)} %copy-done.3), channel_id=1, source_target_pairs={{0,1},{1,0},{2,3},{3,2},{4,5},{5,4},{6,7},{7,6},{8,9},{9,8},{10,11... | collective-permute-start | bytes 884744 | tf_op jit(solution)/shard_map/ppermute | solution.py:357
  95.5 0.8 copy-start.12
  96.3 0.8 copy-start.14
  101.9 1.1 copy-start.13
  102.9 1.0 copy-start.15

commit v3 on v2

--- a/solution.py
+++ b/solution.py
@@ -18,6 +18,7 @@
 POS = 32
 DP_X, DP_Y = 4, 2
 INTERPRET = False
+NEAR_TILE = 256
 LIMITS = [60 * 1024 * 1024, 60 * 1024 * 1024, 24 << 20, 24 << 20, 24 << 20]
 
 eps_norm = 1e-05
@@ -80,7 +81,7 @@
 
 
 def pack_weights(core, projection, output_weight):
-    return call(pack_kernel, shape_of(192, INNER), [SMEM, VMEM, VMEM])(
+    return call(pack_kernel, shape_of(192, INNER), [SMEM, VMEM, VMEM], limit=60 * 1024 * 1024)(
         core, projection, output_weight
     )
 
@@ -99,7 +100,7 @@
     return got.reshape(DP_X * DP_Y, 192, INNER)
 
 
-def norm_kernel(x_ref, gain_ref, out_ref):
+def norm_kernel(base_ref, x_ref, gain_ref, perm_ref, out_ref, order_ref):
     gain = gain_ref[...].reshape(1, D)
     for row in range(0, TOK, 128):
         values = x_ref[row : row + 128, :].astype(F32)
@@ -109,15 +110,27 @@
         out_ref[row : row + 128, :] = (
             centred * lax.rsqrt(variance + eps_norm) * gain
         ).astype(BF16)
-
-
-def chosen_rows(view, offset, first, perm_ref):
+    order_ref[...] = (perm_ref[...] - base_ref[1]).astype(F32)
+    local = jnp.broadcast_to(perm_ref[...] - base_ref[1], (16, TOK))
+    row = lax.broadcasted_iota(jnp.int32, (16, TOK), 0)
+    parts = jnp.where(row == 0, jnp.right_shift(local, 4), jnp.bitwise_and(local, 15))
+    out_ref[TOK : TOK + 16, 0:TOK] = parts.astype(F32).astype(BF16)
+    out_ref[TOK : TOK + 16, TOK:] = jnp.zeros((16, D - TOK), BF16)
+
+
+def order_of(x_ref):
+    parts = x_ref[TOK : TOK + 16, 0:TOK].astype(F32)
+    return parts[0:1, :] * 16.0 + parts[1:2, :]
+
+
+def chosen_rows(view, offset, order):
     rows = lax.broadcasted_iota(jnp.int32, (SPARSE, 1), 0) * RATIO + offset
     if view == 0:
         return rows
     lane = lax.broadcasted_iota(jnp.int32, (SPARSE, TOK), 1)
-    tiles = jnp.broadcast_to(perm_ref[...], (SPARSE, TOK))
-    return jnp.sum(jnp.where(lane == rows, tiles, 0), axis=1, keepdims=True) - first
+    tiles = jnp.broadcast_to(order, (SPARSE, TOK))
+    picked = jnp.sum(jnp.where(lane == rows, tiles, 0.0), axis=1, keepdims=True)
+    return picked.astype(jnp.int32)
 
 
 def one_hot(index, width):
@@ -126,7 +139,7 @@
 
 
 def project_kernel(
-    base_ref, offset_ref, own_x, other_x, packed_ref, own_ref, other_ref,
+    base_ref, offset_ref, own_x, other_x, packed_ref,
     kv_out, q_out, send_ref, outw_ref, w_ref, kv_ref, q_ref, sems,
 ):
     flip = base_ref[3]
@@ -164,12 +177,13 @@
                 pltpu.make_async_copy(here.at[rows], there.at[rows], sems.at[part * 2 + at])
             )
             copies[-1].start()
+    own_order, other_order = order_of(own_x), order_of(other_x)
     for view in range(2):
         for head in range(HALF):
             lanes = slice(head * 128, head * 128 + 128)
             offset = offset_ref[base_ref[0] * HALF + head]
-            own = chosen_rows(view, offset, base_ref[1], own_ref)
-            other = chosen_rows(view, offset, base_ref[2], other_ref) + TOK
+            own = chosen_rows(view, offset, own_order)
+            other = chosen_rows(view, offset, other_order) + TOK
             chosen = one_hot(jnp.concatenate([own, other], axis=0), SEG)
             far_kv = jnp.dot(chosen, kv_ref[:, lanes], preferred_element_type=F32).astype(BF16)
             far_q = jnp.dot(chosen, q_ref[:, lanes], preferred_element_type=F32)
@@ -193,41 +207,32 @@
     keys = kv_ref[...]
     lane = lax.broadcasted_iota(jnp.int32, (SEG, 128), 1)
     values = jnp.where(lane < HEAD_DIM, swap_halves(keys.astype(F32)), 1.0).astype(BF16)
-    scores = lax.dot_general(
-        q_ref[...], keys, (((1,), (1,)), ((), ())), preferred_element_type=F32
-    )
-    row_max = jnp.max(scores, axis=1, keepdims=True)
-    weights = jnp.exp2((scores - row_max) * EXP_SCALE).astype(BF16)
-    summed = jnp.dot(weights, values, preferred_element_type=F32)
-    out_lane = lax.broadcasted_iota(jnp.int32, summed.shape, 1)
-    result = jnp.where(
-        out_lane < HEAD_DIM, summed / swap_halves(summed), row_max * SCALE + jnp.log(summed)
-    )
-
-    @pl.when(pl.program_id(1) < 2)
-    def _():
-        keep_ref[...] = result
-
-    @pl.when(pl.program_id(1) >= 2)
-    def _():
-        give_ref[...] = result
+    tile = NEAR_TILE
+    out_lane = lax.broadcasted_iota(jnp.int32, (tile, 128), 1)
+    for at in range(0, SEG, tile):
+        scores = lax.dot_general(
+            q_ref[at : at + tile, :], keys, (((1,), (1,)), ((), ())), preferred_element_type=F32
+        )
+        row_max = jnp.max(scores, axis=1, keepdims=True)
+        weights = jnp.exp2((scores - row_max) * EXP_SCALE).astype(BF16)
+        summed = jnp.dot(weights, values, preferred_element_type=F32)
+        result = jnp.where(
+            out_lane < HEAD_DIM, summed / swap_halves(summed), row_max * SCALE + jnp.log(summed)
+        )
+        out_ref = keep_ref if at < TOK else give_ref
+        out_ref[at % TOK : at % TOK + tile, :] = result
 
 
 def near_level(queries, key_pairs):
-    tile = 256
     half = shape_of(TOK, HALF * 128, dtype=F32)
+    whole = pl.BlockSpec((SEG, 128), lambda h: (0, h))
+    part = pl.BlockSpec((TOK, 128), lambda h: (0, h))
     return pl.pallas_call(
         near_kernel,
         out_shape=[half, half],
-        grid=(HALF, SEG // tile),
-        in_specs=[
-            pl.BlockSpec((tile, 128), lambda h, i: (i, h)),
-            pl.BlockSpec((SEG, 128), lambda h, i: (0, h)),
-        ],
-        out_specs=[
-            pl.BlockSpec((tile, 128), lambda h, i: (jnp.minimum(i, 1), h)),
-            pl.BlockSpec((tile, 128), lambda h, i: (jnp.maximum(i - 2, 0), h)),
-        ],
+        grid=(HALF,),
+        in_specs=[whole, whole],
+        out_specs=[part, part],
         cost_estimate=pl.CostEstimate(
             flops=4 * HALF * SEG * SEG * 128, bytes_accessed=3 << 20, transcendentals=HALF * SEG * SEG
         ),
@@ -272,12 +277,13 @@
 
 
 def prepare_kernel(
-    base_ref, offset_ref, keep_ref, got_ref, own_ref, gain_ref, own_w, other_w,
-    dense_ref, rows_ref, spread_ref, order_ref, weight_ref,
+    base_ref, offset_ref, keep_ref, got_ref, order_ref, gain_ref, own_w, other_w,
+    dense_ref, rows_ref, spread_ref, scale_ref, weight_ref,
 ):
     core = base_ref[0]
     width = HALF * HEAD_DIM
     hots = [[], []]
+    order = order_ref[...]
     for group, near_ref in enumerate((keep_ref, got_ref)):
         dense_ref[:, group * width : (group + 1) * width] = jnp.concatenate(
             [near_ref[:, head * 128 : head * 128 + HEAD_DIM] for head in range(HALF)], axis=1
@@ -287,7 +293,7 @@
             pieces = jnp.concatenate(parts3(near_ref[:, head * 128 : head * 128 + 128]), axis=1)
             offset = offset_ref[heads * HALF + head]
             for view in range(2):
-                chosen = one_hot(chosen_rows(view, offset, base_ref[1], own_ref), TOK)
+                chosen = one_hot(chosen_rows(view, offset, order), TOK)
                 hots[view].append(chosen)
                 taken = jnp.dot(chosen, pieces, preferred_element_type=F32)
                 at = group * 192 + (view * HALF + head) * SPARSE
@@ -295,7 +301,7 @@
     for view in range(2):
         spread_ref[view] = jnp.concatenate(hots[view], axis=0).astype(F32).T.astype(BF16)
     gain = gain_ref[...].reshape(1, INNER)
-    order_ref[...] = jnp.where(
+    scale_ref[...] = jnp.where(
         core == 0, gain, jnp.concatenate([gain[:, width:], gain[:, :width]], axis=1)
     )
     own_rows = pl.ds(pl.multiple_of(core * width, 64), width)
@@ -367,14 +373,16 @@
     base = jnp.stack([core, rank * TOK, (rank ^ 1) * TOK, lax.axis_index("yh").astype(jnp.int32)])
 
     packed = gather_weights(core_id, projection, output_weight)
-    own_x = call(norm_kernel, shape_of(TOK, D), [VMEM, VMEM], moved=2 << 20)(
-        tile_features[0], input_gain
-    )
-    other_x = core_swap(own_x)
     last = 2 * POS - 1
     ctx = ("pos", "core")
     own_perm = lax.ppermute(flip_perm, ctx, [(last - r, r) for r in range(2 * POS)])
-    other_perm = lax.ppermute(flip_perm, ctx, [(last - (r ^ 1), r) for r in range(2 * POS)])
+    own_x, own_order = call(
+        norm_kernel,
+        [shape_of(TOK + 16, D), shape_of(1, TOK, dtype=F32)],
+        [SMEM, VMEM, VMEM, VMEM],
+        moved=2 << 20,
+    )(base, tile_features[0], input_gain, own_perm)
+    other_x = core_swap(own_x)
 
     key_pairs, queries, send, own_w = call(
         project_kernel,
@@ -384,7 +392,7 @@
             shape_of(POS, 48, 128),
             shape_of(INNER, INNER),
         ],
-        [SMEM, SMEM, VMEM, VMEM, VMEM, VMEM, VMEM],
+        [SMEM, SMEM, VMEM, VMEM, VMEM],
         [
             pltpu.VMEM((D, INNER + 192), BF16),
             pltpu.VMEM((SEG, INNER), BF16),
@@ -395,7 +403,7 @@
         flops=2 * SEG * D * 576,
         moved=4 << 20,
         limit=LIMITS[0],
-    )(base, head_offsets, own_x, other_x, packed, own_perm, other_perm)
+    )(base, head_offsets, own_x, other_x, packed)
 
     got = lax.all_to_all(send, "pos", 0, 0, tiled=True)
     keep, give = near_level(queries, key_pairs)
@@ -420,7 +428,7 @@
         flops=1 << 28,
         moved=4 << 20,
         limit=LIMITS[3],
-    )(base, head_offsets, keep, near_got, own_perm, output_gain, own_w, other_w)
+    )(base, head_offsets, keep, near_got, own_order, output_gain, own_w, other_w)
 
     plain_view, flipped_view = call(
         output_kernel,

time: 109 us -> 103 us (0.945)
  the two profiles are of different devices: /device:TPU:59 before, /device:TPU:1 now
where the time goes in v3:
time: 103 us; the launch traced here: 102 us
  starting transfers between devices  50.2 us (49%)
  Pallas kernels  26.2 us (25%)
  waiting for transfers between devices  19.5 us (19%)
  local copies, waits for them, and re-layouts  5.67 us (6%)
    ppermute x1, starting transfers between devices, layer(): lax.ppermute(flip_perm, ctx, [(last - r, r) for r in range(2 * POS)])  11.9 us
    all_to_all x1, waiting for transfers between devices, gather_weights(): got = lax.all_to_all(both, 'x', 0, 0, tiled=True)  11.3 us
    all_to_all x1, starting transfers between devices, layer(): far = lax.all_to_all(back.reshape(2 * POS, 16, 128), ctx, 0, 0, tiled=True)  10.4 us
    ppermute x3, starting transfers between devices, core_swap(): return lax.ppermute(block, 'core', [(0, 1), (1, 0)])  8.54 us
    ppermute x1, starting transfers between devices, gather_weights(): other = lax.ppermute(packed, 'yh', [(0, 1), (1, 0)])  8.26 us
    pallas_call x1, Pallas kernels, near_level(): pl.pallas_call(near_kernel, out_shape=[half, half], grid=(HALF,), in_spec...  8.18 us
    all_to_all x1, starting transfers between devices, layer(): got = lax.all_to_all(send, 'pos', 0, 0, tiled=True)  6.99 us
    unnamed x30, local copies, waits for them, and re-layouts  5.67 us
  transfers between devices with their start and end apart: 8, of which 4 were waited for; matrix products, arithmetic and copies ran while one was open for 0% of the time, Pallas kernels for 15%

profile of v3, /device:TPU:1, one launch (start us, length us, event | category | flops | bytes accessed | tf_op | source)
XLA Modules:
  0.0 102.5 jit_solution(11850037318761751648)
XLA Ops:
  0.6 1.8 %shard_map.87.own_ref = bf16[192,384]{1,0:T(8,128)(2,1)} custom-call(s32[1]{0:T(128)} %bitcast.core_ref, bf16[96,1152]{1,0:T(8,128)(2,1)} %proj_ref.1, bf16[48,768]{1,0:T(8,128)(2,1)} %outw_ref.1), custom_call_target="tpu_custom_call" | custom-call | tf_op jit(solution)/shard_map/pallas_call | solution.py:84
  2.4 8.3 %collective-permute-start.2 = (bf16[192,384]{1,0:T(8,128)(2,1)}, bf16[192,384]{1,0:T(8,128)(2,1)S(1)}, u32[]{:S(2)}, u32[]{:S(2)}) collective-permute-start(bf16[192,384]{1,0:T(8,128)(2,1)} %shard_map.87.own_ref), channel_id=1, source_target_pairs={{0,64},{64,0},{1,65},{65,1},{2,66},{66,2},{3,67},{67,3},{4,68},{68... | collective-permute-start | bytes 442376 | tf_op jit(solution)/shard_map/ppermute | solution.py:97
  10.7 11.9 %collective-permute-start = (s32[1,512]{1,0:T(1,128)}, s32[1,512]{1,0:T(1,128)S(1)}, u32[]{:S(2)}, u32[]{:S(2)}) collective-permute-start(s32[1,512]{1,0:T(1,128)} %param.8), channel_id=1, source_target_pairs={{63,0},{62,1},{61,2},{60,3},{59,4},{58,5},{57,6},{56,7},{55,8},{54... | collective-permute-start | bytes 6152 | tf_op jit(solution)/shard_map/ppermute | solution.py:378
  22.5 0.0 collective-permute-done.2.other_ref
  22.5 0.0 copy-start.2
  22.6 0.9 copy-done.2
  23.5 1.1 %shard_map.88 = bf16[4,2,192,384]{3,2,1,0:T(8,128)(2,1)} custom-call(bf16[192,384]{1,0:T(8,128)(2,1)S(1)} %copy-done.2, bf16[192,384]{1,0:T(8,128)(2,1)S(1)} %collective-permute-done.2.other_ref), custom_call_target="tpu_custom_call" | custom-call | tf_op jit(solution)/shard_map/pallas_call | solution.py:98
  24.6 0.0 copy-start
  24.6 0.0 copy-start.6
  24.6 4.1 %all-to-all-start = ((bf16[4,2,192,384]{3,2,1,0:T(8,128)(2,1)}), bf16[4,2,192,384]{3,2,1,0:T(8,128)(2,1)S(1)}, u32[]{:S(2)}, u32[]{:S(2)}) async-start(bf16[4,2,192,384]{3,2,1,0:T(8,128)(2,1)} %shard_map.88), calls=%async_computation | async-start | bytes 2359296 | tf_op jit(solution)/shard_map/all_to_all | solution.py:99
  28.7 0.1 pad_add_fusion.base_ref
  28.8 0.0 copy-start.4
  28.8 0.0 collective-permute-done.perm_ref
  28.8 0.0 copy-done
  28.8 0.0 copy-done.6
  28.8 1.1 %shard_map.86 = (bf16[528,768]{1,0:T(8,128)(2,1)S(1)}, f32[1,512]{1,0:T(1,128)S(1)}) custom-call(s32[4]{0:T(128)S(1)} %pad_add_fusion.base_ref, bf16[512,768]{1,0:T(8,128)(2,1)S(1)} %bitcast.9, f32[768]{0:T(1024)S(1)} %copy-done.6, s32[1,512]{1,0:T(1,128)S(1)} %collective-permute-done.perm_ref), custom_call_target="tpu_custom_call" | custom-call | bytes 2097152 | tf_op jit(solution)/shard_map/pallas_call | solution.py:379
  29.9 0.0 copy-start.9
  29.9 1.9 %collective-permute-start.1 = (bf16[528,768]{1,0:T(8,128)(2,1)S(1)}, bf16[528,768]{1,0:T(8,128)(2,1)}, u32[]{:S(2)}, u32[]{:S(2)}) collective-permute-start(bf16[528,768]{1,0:T(8,128)(2,1)S(1)} %get-tuple-element.17.own_x), channel_id=1, source_target_pairs={{0,1},{1,0},{2,3},{3,2},{4,5},{5,4},{6,7},{7,6},{8,9},{9,8},{10,11... | collective-permute-start | bytes 2433032 | tf_op jit(solution)/shard_map/ppermute | solution.py:363
  31.8 2.4 %collective-permute-done.1.other_x = bf16[528,768]{1,0:T(8,128)(2,1)} collective-permute-done((bf16[528,768]{1,0:T(8,128)(2,1)S(1)}, bf16[528,768]{1,0:T(8,128)(2,1)}, u32[]{:S(2)}, u32[]{:S(2)}) %collective-permute-start.1) | collective-permute-done | bytes 811040 | tf_op jit(solution)/shard_map/ppermute | solution.py:363
  34.3 11.3 %all-to-all-done = bf16[4,2,192,384]{3,2,1,0:T(8,128)(2,1)S(1)} async-done(((bf16[4,2,192,384]{3,2,1,0:T(8,128)(2,1)}), bf16[4,2,192,384]{3,2,1,0:T(8,128)(2,1)S(1)}, u32[]{:S(2)}, u32[]{:S(2)}) %all-to-all-start) | async-done | bytes 1179680 | tf_op jit(solution)/shard_map/all_to_all | solution.py:99
  45.5 0.0 copy-start.14
  45.5 0.0 copy-done.4
  45.5 0.0 copy-done.9
  45.5 1.0 copy-done.14
  46.5 5.0 %shard_map.89 = (bf16[1024,384]{1,0:T(8,128)(2,1)}, bf16[1024,384]{1,0:T(8,128)(2,1)}, bf16[32,48,128]{2,1,0:T(8,128)(2,1)}, bf16[384,384]{1,0:T(8,128)(2,1)}) custom-call(s32[4]{0:T(128)} %copy-done.4, s32[6]{0:T(128)} %offset_ref.3, bf16[528,768]{1,0:T(8,128)(2,1)} %copy-done.9, bf16[528,768]{1,0:T(8,128)(2,1)} %collective-permute-done.1.other_x, ...), custom_call_target="tpu_custom_call" | custom-call | flops 905969664 | bytes 4194304 | tf_op jit(solution)/shard_map/pallas_call | solution.py:387
  51.6 7.0 %all-to-all-start.1 = ((bf16[32,48,128]{2,1,0:T(8,128)(2,1)}), bf16[32,48,128]{2,1,0:T(8,128)(2,1)S(1)}, u32[]{:S(2)}, u32[]{:S(2)}) async-start(bf16[32,48,128]{2,1,0:T(8,128)(2,1)} %get-tuple-element.18), calls=%async_computation.1 | async-start | bytes 786432 | tf_op jit(solution)/shard_map/all_to_all | solution.py:408
  58.6 8.2 %shard_map.91 = (f32[512,384]{1,0:T(8,128)}, f32[512,384]{1,0:T(8,128)}) custom-call(bf16[1024,384]{1,0:T(8,128)(2,1)} %get-tuple-element.19.q_ref, bf16[1024,384]{1,0:T(8,128)(2,1)} %get-tuple-element.20.kv_ref), custom_call_target="tpu_custom_call" | custom-call | flops 1610612736 | bytes 3145728 | tf_op jit(solution)/shard_map/pallas_call | solution.py:230
  66.8 0.0 copy-start.7
  66.8 0.0 copy-start.8
  66.8 4.1 %collective-permute-start.3 = (f32[512,384]{1,0:T(8,128)}, f32[512,384]{1,0:T(8,128)S(1)}, u32[]{:S(2)}, u32[]{:S(2)}) collective-permute-start(f32[512,384]{1,0:T(8,128)} %get-tuple-element.22), channel_id=1, source_target_pairs={{0,1},{1,0},{2,3},{3,2},{4,5},{5,4},{6,7},{7,6},{8,9},{9,8},{10,11... | collective-permute-start | bytes 2359304 | tf_op jit(solution)/shard_map/ppermute | solution.py:363
  70.9 0.0 all-to-all-done.1.got_ref
  70.9 3.7 %shard_map.90 = bf16[32,2,16,128]{3,2,1,0:T(8,128)(2,1)} custom-call(s32[1]{0:T(128)} %bitcast.core_ref, bf16[32,48,128]{2,1,0:T(8,128)(2,1)S(1)} %all-to-all-done.1.got_ref), custom_call_target="tpu_custom_call" | custom-call | flops 536870912 | bytes 1048576 | tf_op jit(solution)/shard_map/pallas_call | solution.py:411
  74.6 10.4 %all-to-all-start.2 = ((bf16[64,16,128]{2,1,0:T(8,128)(2,1)}), bf16[64,16,128]{2,1,0:T(8,128)(2,1)S(1)}, u32[]{:S(2)}, u32[]{:S(2)}) async-start(bf16[64,16,128]{2,1,0:T(8,128)(2,1)} %bitcast.6), calls=%async_computation.2 | async-start | bytes 524288 | tf_op jit(solution)/shard_map/all_to_all | solution.py:415
  85.0 0.0 copy-done.3
  85.1 2.5 %collective-permute-start.4 = (bf16[384,384]{1,0:T(8,128)(2,1)S(1)}, bf16[384,384]{1,0:T(8,128)(2,1)S(1)}, u32[]{:S(2)}, u32[]{:S(2)}) collective-permute-start(bf16[384,384]{1,0:T(8,128)(2,1)S(1)} %copy-done.3), channel_id=1, source_target_pairs={{0,1},{1,0},{2,3},{3,2},{4,5},{5,4},{6,7},{7,6},{8,9},{9,8},{10,11... | collective-permute-start | bytes 884744 | tf_op jit(solution)/shard_map/ppermute | solution.py:363
  87.6 1.0 collective-permute-done.4.other_w
  88.6 0.0 collective-permute-done.3.got_ref
  88.6 0.0 copy-done.1
  88.6 0.0 copy-done.5
  88.6 0.0 copy-done.7
  88.6 0.0 copy-done.8
  88.6 1.5 %shard_map.92 = (f32[512,384]{1,0:T(8,128)S(1)}, f32[384,128]{1,0:T(8,128)S(1)}, bf16[2,512,192]{2,1,0:T(8,128)(2,1)S(1)}, f32[1,384]{1,0:T(1,128)S(1)}, bf16[384,768]{1,0:T(8,128)(2,1)S(1)}) custom-call(s32[4]{0:T(128)S(1)} %copy-done.5, s32[6]{0:T(128)S(1)} %copy-done.8, f32[512,384]{1,0:T(8,128)S(1)} %copy-done.1, ...), custom_call_target="tpu_custom_call" | custom-call | flops 268435456 | bytes 4194304 | tf_op jit(solution)/shard_map/pallas_call | solution.py:418
  90.2 0.8 copy-done.10
  91.0 0.8 copy-done.12
  91.8 4.8 %all-to-all-done.2.far_ref = bf16[64,16,128]{2,1,0:T(8,128)(2,1)S(1)} async-done(((bf16[64,16,128]{2,1,0:T(8,128)(2,1)}), bf16[64,16,128]{2,1,0:T(8,128)(2,1)S(1)}, u32[]{:S(2)}, u32[]{:S(2)}) %all-to-all-start.2) | async-done | bytes 262176 | tf_op jit(solution)/shard_map/all_to_all | solution.py:415
  96.6 1.1 %copy-done.11 = bf16[384,768]{1,0:T(8,128)(2,1)S(1)} copy-done((bf16[384,768]{1,0:T(8,128)(2,1)S(1)}, bf16[384,768]{1,0:T(8,128)(2,1)}, u32[]{:S(2)}) %copy-start.11) | copy-done | bytes 589848
  97.6 1.0 %copy-done.13 = bf16[2,512,192]{2,1,0:T(8,128)(2,1)S(1)} copy-done((bf16[2,512,192]{2,1,0:T(8,128)(2,1)S(1)}, bf16[2,512,192]{2,1,0:T(8,128)(2,1)}, u32[]{:S(2)}) %copy-start.13) | copy-done | bytes 393240
  98.7 3.8 %shard_map.93 = (bf16[512,768]{1,0:T(8,128)(2,1)}, bf16[512,768]{1,0:T(8,128)(2,1)}) custom-call(s32[1]{0:T(128)} %bitcast.core_ref, bf16[64,16,128]{2,1,0:T(8,128)(2,1)S(1)} %all-to-all-done.2.far_ref, f32[512,384]{1,0:T(8,128)S(1)} %get-tuple-element.25.dense_ref, f32[384,128]{1,0:T(8,128)S(1)} %get-tuple-element.26.rows_ref, ...), custom_call_target="tpu_custom_call" | custom-call | flops 1207959552 | bytes 4194304 | tf_op jit(solution)/shard_map/pallas_call | solution.py:433
  (7 shorter events, 0.0 us)
Async XLA Ops:
  2.4 20.1 %collective-permute-start.2 = (bf16[192,384]{1,0:T(8,128)(2,1)}, bf16[192,384]{1,0:T(8,128)(2,1)S(1)}, u32[]{:S(2)}, u32[]{:S(2)}) collective-permute-start(bf16[192,384]{1,0:T(8,128)(2,1)} %shard_map.87.own_ref), channel_id=1, source_target_pairs={{0,64},{64,0},{1,65},{65,1},{2,66},{66,2},{3,67},{67,3},{4,68},{68... | collective-permute-start | bytes 442376 | tf_op jit(solution)/shard_map/ppermute | solution.py:97
  10.7 18.2 %collective-permute-start = (s32[1,512]{1,0:T(1,128)}, s32[1,512]{1,0:T(1,128)S(1)}, u32[]{:S(2)}, u32[]{:S(2)}) collective-permute-start(s32[1,512]{1,0:T(1,128)} %param.8), channel_id=1, source_target_pairs={{63,0},{62,1},{61,2},{60,3},{59,4},{58,5},{57,6},{56,7},{55,8},{54... | collective-permute-start | bytes 6152 | tf_op jit(solution)/shard_map/ppermute | solution.py:378
  22.5 0.9 copy-start.2
  24.6 4.2 %copy-start = (bf16[1,512,768]{2,1,0:T(8,128)(2,1)S(1)}, bf16[1,512,768]{2,1,0:T(8,128)(2,1)}, u32[]{:S(2)}) copy-start(bf16[1,512,768]{2,1,0:T(8,128)(2,1)} %param.7) | copy-start | bytes 2359300
  24.6 4.2 %copy-start.6 = (f32[768]{0:T(1024)S(1)}, f32[768]{0:T(1024)}, u32[]{:S(2)}) copy-start(f32[768]{0:T(1024)} %gain_ref.2) | copy-start | bytes 9220
  24.6 20.9 %all-to-all-start = ((bf16[4,2,192,384]{3,2,1,0:T(8,128)(2,1)}), bf16[4,2,192,384]{3,2,1,0:T(8,128)(2,1)S(1)}, u32[]{:S(2)}, u32[]{:S(2)}) async-start(bf16[4,2,192,384]{3,2,1,0:T(8,128)(2,1)} %shard_map.88), calls=%async_computation | async-start | bytes 2359296 | tf_op jit(solution)/shard_map/all_to_all | solution.py:99
  28.8 16.7 %copy-start.4 = (s32[4]{0:T(128)}, s32[4]{0:T(128)S(1)}, u32[]{:S(2)}) copy-start(s32[4]{0:T(128)S(1)} %pad_add_fusion.base_ref) | copy-start | bytes 52
  29.9 15.6 %copy-start.9 = (bf16[528,768]{1,0:T(8,128)(2,1)}, bf16[528,768]{1,0:T(8,128)(2,1)S(1)}, u32[]{:S(2)}) copy-start(bf16[528,768]{1,0:T(8,128)(2,1)S(1)} %get-tuple-element.17.own_x) | copy-start | bytes 2433028
  29.9 4.3 %collective-permute-start.1 = (bf16[528,768]{1,0:T(8,128)(2,1)S(1)}, bf16[528,768]{1,0:T(8,128)(2,1)}, u32[]{:S(2)}, u32[]{:S(2)}) collective-permute-start(bf16[528,768]{1,0:T(8,128)(2,1)S(1)} %get-tuple-element.17.own_x), channel_id=1, source_target_pairs={{0,1},{1,0},{2,3},{3,2},{4,5},{5,4},{6,7},{7,6},{8,9},{9,8},{10,11... | collective-permute-start | bytes 2433032 | tf_op jit(solution)/shard_map/ppermute | solution.py:363
  45.5 1.0 copy-start.14
  51.6 19.3 %all-to-all-start.1 = ((bf16[32,48,128]{2,1,0:T(8,128)(2,1)}), bf16[32,48,128]{2,1,0:T(8,128)(2,1)S(1)}, u32[]{:S(2)}, u32[]{:S(2)}) async-start(bf16[32,48,128]{2,1,0:T(8,128)(2,1)} %get-tuple-element.18), calls=%async_computation.1 | async-start | bytes 786432 | tf_op jit(solution)/shard_map/all_to_all | solution.py:408
  66.8 18.3 %copy-start.3 = (bf16[384,384]{1,0:T(8,128)(2,1)S(1)}, bf16[384,384]{1,0:T(8,128)(2,1)}, u32[]{:S(2)}) copy-start(bf16[384,384]{1,0:T(8,128)(2,1)} %get-tuple-element.24.own_w) | copy-start | bytes 884740
  66.8 21.9 %copy-start.1 = (f32[512,384]{1,0:T(8,128)S(1)}, f32[512,384]{1,0:T(8,128)}, u32[]{:S(2)}) copy-start(f32[512,384]{1,0:T(8,128)} %get-tuple-element.21.keep_ref) | copy-start | bytes 2359300
  66.8 21.9 %copy-start.5 = (s32[4]{0:T(128)S(1)}, s32[4]{0:T(128)}, u32[]{:S(2)}) copy-start(s32[4]{0:T(128)} %copy-done.4) | copy-start | bytes 52
  66.8 21.8 %copy-start.7 = (f32[384]{0:T(512)S(1)}, f32[384]{0:T(512)}, u32[]{:S(2)}) copy-start(f32[384]{0:T(512)} %gain_ref.3) | copy-start | bytes 4612
  66.8 21.8 %copy-start.8 = (s32[6]{0:T(128)S(1)}, s32[6]{0:T(128)}, u32[]{:S(2)}) copy-start(s32[6]{0:T(128)} %offset_ref.3) | copy-start | bytes 76
  66.8 21.8 %collective-permute-start.3 = (f32[512,384]{1,0:T(8,128)}, f32[512,384]{1,0:T(8,128)S(1)}, u32[]{:S(2)}, u32[]{:S(2)}) collective-permute-start(f32[512,384]{1,0:T(8,128)} %get-tuple-element.22), channel_id=1, source_target_pairs={{0,1},{1,0},{2,3},{3,2},{4,5},{5,4},{6,7},{7,6},{8,9},{9,8},{10,11... | collective-permute-start | bytes 2359304 | tf_op jit(solution)/shard_map/ppermute | solution.py:363
  74.6 21.9 %all-to-all-start.2 = ((bf16[64,16,128]{2,1,0:T(8,128)(2,1)}), bf16[64,16,128]{2,1,0:T(8,128)(2,1)S(1)}, u32[]{:S(2)}, u32[]{:S(2)}) async-start(bf16[64,16,128]{2,1,0:T(8,128)(2,1)} %bitcast.6), calls=%async_computation.2 | async-start | bytes 524288 | tf_op jit(solution)/shard_map/all_to_all | solution.py:415
  85.1 3.6 %collective-permute-start.4 = (bf16[384,384]{1,0:T(8,128)(2,1)S(1)}, bf16[384,384]{1,0:T(8,128)(2,1)S(1)}, u32[]{:S(2)}, u32[]{:S(2)}) collective-permute-start(bf16[384,384]{1,0:T(8,128)(2,1)S(1)} %copy-done.3), channel_id=1, source_target_pairs={{0,1},{1,0},{2,3},{3,2},{4,5},{5,4},{6,7},{7,6},{8,9},{9,8},{10,11... | collective-permute-start | bytes 884744 | tf_op jit(solution)/shard_map/ppermute | solution.py:363
  90.1 0.8 copy-start.10
  91.0 0.8 copy-start.12
  96.6 1.1 %copy-start.11 = (bf16[384,768]{1,0:T(8,128)(2,1)S(1)}, bf16[384,768]{1,0:T(8,128)(2,1)}, u32[]{:S(2)}) copy-start(bf16[384,768]{1,0:T(8,128)(2,1)} %copy-done.10) | copy-start | bytes 1769476
  97.6 1.0 %copy-start.13 = (bf16[2,512,192]{2,1,0:T(8,128)(2,1)S(1)}, bf16[2,512,192]{2,1,0:T(8,128)(2,1)}, u32[]{:S(2)}) copy-start(bf16[2,512,192]{2,1,0:T(8,128)(2,1)} %copy-done.12) | copy-start | bytes 1179652

commit v4 on v3

--- a/solution.py
+++ b/solution.py
@@ -140,62 +140,57 @@
 
 def project_kernel(
     base_ref, offset_ref, own_x, other_x, packed_ref,
-    kv_out, q_out, send_ref, outw_ref, w_ref, kv_ref, q_ref, sems,
+    all_out, send_ref, outw_ref, w_ref, all_ref, sems,
 ):
     flip = base_ref[3]
     lane = lax.broadcasted_iota(jnp.int32, (48, 128), 1)
     for entry in range(8):
         shard = (entry - entry % 2) + (entry % 2 ^ flip)
         row = pl.multiple_of(shard * 96, 16)
-        w_ref[pl.ds(row, 96), 0:INNER] = packed_ref[entry, 0:96, :]
+        for head in range(HALF):
+            at = head * 256
+            w_ref[pl.ds(row, 96), at : at + 128] = packed_ref[
+                entry, 0:96, head * 128 : head * 128 + 128
+            ]
+            folded = packed_ref[entry, 96:144, head * 128 : head * 128 + 128].astype(F32)
+            for first, part in ((0, folded), (48, swap_halves(folded))):
+                w_ref[pl.ds(pl.multiple_of(row + first, 16), 48), at + 128 : at + 256] = jnp.where(
+                    lane < HEAD_DIM, part, 0.0
+                ).astype(BF16)
         outw_ref[pl.ds(pl.multiple_of(shard * 48, 16), 48), :] = packed_ref[entry, 144:192, :]
-        first, second = [], []
-        for head in range(HALF):
-            folded = packed_ref[entry, 96:144, head * 128 : head * 128 + 128].astype(F32)
-            first.append(folded[:, :HEAD_DIM])
-            second.append(folded[:, HEAD_DIM:])
-        for at, pieces in ((0, first), (48, second)):
-            w_ref[pl.ds(pl.multiple_of(row + at, 16), 48), INNER : INNER + 192] = jnp.concatenate(
-                pieces, axis=1
-            ).astype(BF16)
-    q_lane = lax.broadcasted_iota(jnp.int32, (256, 128), 1)
     copies = []
     for part, x_ref in enumerate((own_x, other_x)):
         for step in range(0, TOK, 256):
-            rows = slice(part * TOK + step, part * TOK + step + 256)
-            out = jnp.dot(x_ref[step : step + 256, :], w_ref[...], preferred_element_type=F32)
-            kv_ref[rows, :] = out[:, :INNER].astype(BF16)
-            pair = out[:, INNER : INNER + 128]
-            q_ref[rows, 0:128] = jnp.where(q_lane < HEAD_DIM, pair, 0.0).astype(BF16)
-            q_ref[rows, 128:256] = jnp.where(q_lane < HEAD_DIM, swap_halves(pair), 0.0).astype(BF16)
-            q_ref[rows, 256:384] = jnp.concatenate(
-                [out[:, INNER + 128 :], jnp.zeros((256, HEAD_DIM), F32)], axis=1
+            at = part * TOK + step
+            all_ref[at : at + 256, :] = jnp.dot(
+                x_ref[step : step + 256, :], w_ref[...], preferred_element_type=F32
             ).astype(BF16)
         rows = pl.ds(part * TOK, TOK)
-        for at, (here, there) in enumerate(((kv_ref, kv_out), (q_ref, q_out))):
-            copies.append(
-                pltpu.make_async_copy(here.at[rows], there.at[rows], sems.at[part * 2 + at])
-            )
-            copies[-1].start()
+        copies.append(pltpu.make_async_copy(all_ref.at[rows], all_out.at[rows], sems.at[part]))
+        copies[-1].start()
     own_order, other_order = order_of(own_x), order_of(other_x)
-    for view in range(2):
-        for head in range(HALF):
-            lanes = slice(head * 128, head * 128 + 128)
-            offset = offset_ref[base_ref[0] * HALF + head]
-            own = chosen_rows(view, offset, own_order)
-            other = chosen_rows(view, offset, other_order) + TOK
-            chosen = one_hot(jnp.concatenate([own, other], axis=0), SEG)
-            far_kv = jnp.dot(chosen, kv_ref[:, lanes], preferred_element_type=F32).astype(BF16)
-            far_q = jnp.dot(chosen, q_ref[:, lanes], preferred_element_type=F32)
+    for head in range(HALF):
+        offset = offset_ref[base_ref[0] * HALF + head]
+        index = []
+        for view in range(2):
+            index.append(chosen_rows(view, offset, own_order))
+            index.append(chosen_rows(view, offset, other_order) + TOK)
+        chosen = one_hot(jnp.concatenate(index, axis=0), SEG)
+        far_rows = jnp.dot(
+            chosen, all_ref[:, head * 256 : head * 256 + 256], preferred_element_type=F32
+        )
+        far_kv, far_q = far_rows[:, 0:128].astype(BF16), far_rows[:, 128:256]
+        for view in range(2):
             pair = (view * HALF + head) * 4
             for q_part in range(2):
-                row = q_part * 16
+                row = view * 2 * SPARSE + q_part * 16
                 folded = (
                     far_q[row : row + 16] + swap_halves(far_q[SPARSE + row : SPARSE + row + 16])
                 ).astype(BF16)
                 for k_half in range(2):
                     peer = pair + q_part * 2 + k_half
-                    send_ref[peer, 0:32, :] = far_kv[k_half * SPARSE : k_half * SPARSE + 32]
+                    at = view * 2 * SPARSE + k_half * SPARSE
+                    send_ref[peer, 0:32, :] = far_kv[at : at + SPARSE]
                     send_ref[peer, 32:48, :] = folded
     for peer in range(4 * 2 * HALF, POS):
         send_ref[peer] = jnp.zeros((48, 128), BF16)
@@ -223,22 +218,23 @@
         out_ref[at % TOK : at % TOK + tile, :] = result
 
 
-def near_level(queries, key_pairs):
+def near_level(both):
     half = shape_of(TOK, HALF * 128, dtype=F32)
-    whole = pl.BlockSpec((SEG, 128), lambda h: (0, h))
+    keys = pl.BlockSpec((SEG, 128), lambda h: (0, 2 * h))
+    queries = pl.BlockSpec((SEG, 128), lambda h: (0, 2 * h + 1))
     part = pl.BlockSpec((TOK, 128), lambda h: (0, h))
     return pl.pallas_call(
         near_kernel,
         out_shape=[half, half],
         grid=(HALF,),
-        in_specs=[whole, whole],
+        in_specs=[queries, keys],
         out_specs=[part, part],
         cost_estimate=pl.CostEstimate(
             flops=4 * HALF * SEG * SEG * 128, bytes_accessed=3 << 20, transcendentals=HALF * SEG * SEG
         ),
         compiler_params=pltpu.CompilerParams(vmem_limit_bytes=LIMITS[1]),
         interpret=INTERPRET,
-    )(queries, key_pairs)
+    )(both, both)
 
 
 def far_kernel(core_ref, got_ref, back_ref):
@@ -277,8 +273,8 @@
 
 
 def prepare_kernel(
-    base_ref, offset_ref, keep_ref, got_ref, order_ref, gain_ref, own_w, other_w,
-    dense_ref, rows_ref, spread_ref, scale_ref, weight_ref,
+    base_ref, offset_ref, keep_ref, got_ref, order_ref, gain_ref,
+    dense_ref, rows_ref, spread_ref, scale_ref,
 ):
     core = base_ref[0]
     width = HALF * HEAD_DIM
@@ -298,22 +294,19 @@
                 taken = jnp.dot(chosen, pieces, preferred_element_type=F32)
                 at = group * 192 + (view * HALF + head) * SPARSE
                 rows_ref[at : at + SPARSE, :] = taken[:, :128] + taken[:, 128:256] + taken[:, 256:]
-    for view in range(2):
-        spread_ref[view] = jnp.concatenate(hots[view], axis=0).astype(F32).T.astype(BF16)
+    hots = [jnp.concatenate(part, axis=0) for part in hots]
+    for at, part in enumerate(
+        (hots[0][:128], jnp.concatenate([hots[0][128:], hots[1][128:]], axis=0), hots[1][:128])
+    ):
+        spread_ref[:, at * 128 : at * 128 + 128] = part.astype(F32).T.astype(BF16)
     gain = gain_ref[...].reshape(1, INNER)
     scale_ref[...] = jnp.where(
         core == 0, gain, jnp.concatenate([gain[:, width:], gain[:, :width]], axis=1)
     )
-    own_rows = pl.ds(pl.multiple_of(core * width, 64), width)
-    other_rows = pl.ds(pl.multiple_of((1 - core) * width, 64), width)
-    for part, place in ((own_w, core), (other_w, 1 - core)):
-        cols = pl.ds(pl.multiple_of(place * INNER, 128), INNER)
-        weight_ref[0:width, cols] = part[own_rows, :]
-        weight_ref[width:INNER, cols] = part[other_rows, :]
 
 
 def output_kernel(
-    core_ref, far_ref, dense_ref, rows_ref, spread_ref, gain_ref, weight_ref, plain_ref, flip_ref
+    core_ref, far_ref, dense_ref, rows_ref, spread_ref, gain_ref, own_w, other_w, plain_ref, flip_ref
 ):
     core = core_ref[0]
     lane = lax.broadcasted_iota(jnp.int32, (192, 128), 1)
@@ -341,22 +334,36 @@
         near = rows_ref[group * 192 : group * 192 + 192, :]
         gap = near[:, HEAD_DIM : HEAD_DIM + 1] - (top + jnp.log(joint))
         deltas.append((far - near[:, :HEAD_DIM]) / (1.0 + jnp.exp(gap)))
+    width = HALF * HEAD_DIM
     row = jnp.right_shift(lax.broadcasted_iota(jnp.int32, (192, INNER), 0), 5)
     col = jnp.right_shift(lax.broadcasted_iota(jnp.int32, (192, INNER), 1), 6)
+    none = jnp.zeros((HEAD_DIM, INNER), BF16)
+    own_rows = pl.ds(pl.multiple_of(core * width, 64), width)
+    other_rows = pl.ds(pl.multiple_of((1 - core) * width, 64), width)
+    weights = [
+        jnp.concatenate([part[own_rows, :], part[other_rows, :]], axis=0) for part in (own_w, other_w)
+    ]
     for view, out_ref in enumerate((plain_ref, flip_ref)):
         delta = jnp.concatenate([d[view * 96 : view * 96 + 96] for d in deltas], axis=0)
         blocks = jnp.where(row == col, jnp.concatenate([delta] * HEADS, axis=1), 0.0).astype(BF16)
+        if view == 0:
+            blocks = jnp.concatenate([blocks, none], axis=0)
+        else:
+            blocks = jnp.concatenate([none, blocks[128:], blocks[:128]], axis=0)
         for at in range(0, TOK, 256):
             attended = dense_ref[at : at + 256, :] + jnp.dot(
-                spread_ref[view, at : at + 256, :], blocks, preferred_element_type=F32
+                spread_ref[at : at + 256, view * 128 : view * 128 + 256],
+                blocks,
+                preferred_element_type=F32,
             )
             average = jnp.mean(attended, axis=-1, keepdims=True)
             centred = attended - average
             variance = jnp.mean(centred * centred, axis=-1, keepdims=True)
             mixed = (centred * lax.rsqrt(variance + eps_norm) * gain_ref[...]).astype(BF16)
-            out_ref[at : at + 256, :] = jnp.dot(
-                mixed, weight_ref[...], preferred_element_type=F32
-            ).astype(BF16)
+            for part, place in zip(weights, (core, 1 - core)):
+                out_ref[at : at + 256, pl.ds(pl.multiple_of(place * INNER, 128), INNER)] = jnp.dot(
+                    mixed, part, preferred_element_type=F32
+                ).astype(BF16)
 
 
 def core_swap(block):
@@ -372,10 +379,10 @@
     core_id = core[None]
     base = jnp.stack([core, rank * TOK, (rank ^ 1) * TOK, lax.axis_index("yh").astype(jnp.int32)])
 
-    packed = gather_weights(core_id, projection, output_weight)
     last = 2 * POS - 1
     ctx = ("pos", "core")
     own_perm = lax.ppermute(flip_perm, ctx, [(last - r, r) for r in range(2 * POS)])
+    packed = gather_weights(core_id, projection, output_weight)
     own_x, own_order = call(
         norm_kernel,
         [shape_of(TOK + 16, D), shape_of(1, TOK, dtype=F32)],
@@ -384,29 +391,27 @@
     )(base, tile_features[0], input_gain, own_perm)
     other_x = core_swap(own_x)
 
-    key_pairs, queries, send, own_w = call(
+    both, send, own_w = call(
         project_kernel,
         [
-            shape_of(SEG, INNER),
-            shape_of(SEG, INNER),
+            shape_of(SEG, D),
             shape_of(POS, 48, 128),
             shape_of(INNER, INNER),
         ],
         [SMEM, SMEM, VMEM, VMEM, VMEM],
         [
-            pltpu.VMEM((D, INNER + 192), BF16),
-            pltpu.VMEM((SEG, INNER), BF16),
-            pltpu.VMEM((SEG, INNER), BF16),
-            pltpu.SemaphoreType.DMA((4,)),
+            pltpu.VMEM((D, D), BF16),
+            pltpu.VMEM((SEG, D), BF16),
+            pltpu.SemaphoreType.DMA((2,)),
         ],
-        outs=[HBM, HBM, VMEM, VMEM],
-        flops=2 * SEG * D * 576,
+        outs=[HBM, VMEM, VMEM],
+        flops=2 * SEG * D * D,
         moved=4 << 20,
         limit=LIMITS[0],
     )(base, head_offsets, own_x, other_x, packed)
 
     got = lax.all_to_all(send, "pos", 0, 0, tiled=True)
-    keep, give = near_level(queries, key_pairs)
+    keep, give = near_level(both)
     near_got = core_swap(give)
     back = call(
         far_kernel, shape_of(POS, 2, 16, 128), [SMEM, VMEM], flops=4 * SEG * SEG * 128, moved=1 << 20,
@@ -420,24 +425,23 @@
         [
             shape_of(TOK, INNER, dtype=F32),
             shape_of(INNER, 128, dtype=F32),
-            shape_of(2, TOK, 192),
+            shape_of(TOK, INNER),
             shape_of(1, INNER, dtype=F32),
-            shape_of(INNER, D),
         ],
-        [SMEM, SMEM, VMEM, VMEM, VMEM, VMEM, VMEM, VMEM],
+        [SMEM, SMEM, VMEM, VMEM, VMEM, VMEM],
         flops=1 << 28,
         moved=4 << 20,
         limit=LIMITS[3],
-    )(base, head_offsets, keep, near_got, own_order, output_gain, own_w, other_w)
+    )(base, head_offsets, keep, near_got, own_order, output_gain)
 
     plain_view, flipped_view = call(
         output_kernel,
         [shape_of(TOK, D), shape_of(TOK, D)],
-        [SMEM, VMEM, VMEM, VMEM, VMEM, VMEM, VMEM],
+        [SMEM] + [VMEM] * 7,
         flops=4 * SEG * INNER * D,
         moved=4 << 20,
         limit=LIMITS[4],
-    )(core_id, far, *prepared)
+    )(core_id, far, *prepared, own_w, other_w)
     return (plain_view[None], flipped_view[None])
 
 

time: 103 us -> 103 us (level)
    all_to_all x1, waiting for transfers between devices: 4.8 us -> 6.04 us  [layer(): far = lax.all_to_all(back.reshape(2 * POS, 16, 128), ctx, 0, 0, tiled=True)]
  transfers between devices with their start and end apart: 8 -> 8, of which waited for: 4 -> 3; matrix products, arithmetic and copies ran while one was open for 0% -> 0% of each run, Pallas kernels for 15% -> 15%
where the time goes in v4:
time: 103 us
  starting transfers between devices  50.2 us (49%)
  Pallas kernels  26.6 us (26%)
  waiting for transfers between devices  19.7 us (19%)
  local copies, waits for them, and re-layouts  5.26 us (5%)
    ppermute x1, starting transfers between devices, layer(): lax.ppermute(flip_perm, ctx, [(last - r, r) for r in range(2 * POS)])  11.9 us
    all_to_all x1, waiting for transfers between devices, gather_weights(): got = lax.all_to_all(both, 'x', 0, 0, tiled=True)  11.3 us
    all_to_all x1, starting transfers between devices, layer(): far = lax.all_to_all(back.reshape(2 * POS, 16, 128), ctx, 0, 0, tiled=True)  10.4 us
    ppermute x3, starting transfers between devices, core_swap(): return lax.ppermute(block, 'core', [(0, 1), (1, 0)])  8.53 us
    ppermute x1, starting transfers between devices, gather_weights(): other = lax.ppermute(packed, 'yh', [(0, 1), (1, 0)])  8.26 us
    pallas_call x1, Pallas kernels, near_level(): pl.pallas_call(near_kernel, out_shape=[half, half], grid=(HALF,), in_spec...  8.18 us
    all_to_all x1, starting transfers between devices, layer(): got = lax.all_to_all(send, 'pos', 0, 0, tiled=True)  6.98 us
    all_to_all x1, waiting for transfers between devices, layer(): far = lax.all_to_all(back.reshape(2 * POS, 16, 128), ctx, 0, 0, tiled=True)  6.04 us
  transfers between devices with their start and end apart: 8, of which 3 were waited for; matrix products, arithmetic and copies ran while one was open for 0% of the time, Pallas kernels for 15%

profile of v4, /device:TPU:1, one launch (start us, length us, event | category | flops | bytes accessed | tf_op | source)
XLA Modules:
  0.0 102.8 jit_solution(2345001060651904383)
XLA Ops:
  0.6 1.8 %shard_map.87.own_ref = bf16[192,384]{1,0:T(8,128)(2,1)} custom-call(s32[1]{0:T(128)} %bitcast.core_ref, bf16[96,1152]{1,0:T(8,128)(2,1)} %proj_ref.1, bf16[48,768]{1,0:T(8,128)(2,1)} %outw_ref.1), custom_call_target="tpu_custom_call" | custom-call | tf_op jit(solution)/shard_map/pallas_call | solution.py:84
  2.4 8.3 %collective-permute-start.2 = (bf16[192,384]{1,0:T(8,128)(2,1)}, bf16[192,384]{1,0:T(8,128)(2,1)S(1)}, u32[]{:S(2)}, u32[]{:S(2)}) collective-permute-start(bf16[192,384]{1,0:T(8,128)(2,1)} %shard_map.87.own_ref), channel_id=1, source_target_pairs={{0,64},{64,0},{1,65},{65,1},{2,66},{66,2},{3,67},{67,3},{4,68},{68... | collective-permute-start | bytes 442376 | tf_op jit(solution)/shard_map/ppermute | solution.py:97
  10.7 11.9 %collective-permute-start = (s32[1,512]{1,0:T(1,128)}, s32[1,512]{1,0:T(1,128)S(1)}, u32[]{:S(2)}, u32[]{:S(2)}) collective-permute-start(s32[1,512]{1,0:T(1,128)} %param.8), channel_id=1, source_target_pairs={{63,0},{62,1},{61,2},{60,3},{59,4},{58,5},{57,6},{56,7},{55,8},{54... | collective-permute-start | bytes 6152 | tf_op jit(solution)/shard_map/ppermute | solution.py:384
  22.5 0.0 collective-permute-done.2.other_ref
  22.5 0.0 copy-start.2
  22.6 0.9 copy-done.2
  23.5 1.1 %shard_map.88 = bf16[4,2,192,384]{3,2,1,0:T(8,128)(2,1)} custom-call(bf16[192,384]{1,0:T(8,128)(2,1)S(1)} %copy-done.2, bf16[192,384]{1,0:T(8,128)(2,1)S(1)} %collective-permute-done.2.other_ref), custom_call_target="tpu_custom_call" | custom-call | tf_op jit(solution)/shard_map/pallas_call | solution.py:98
  24.6 0.0 copy-start
  24.6 0.0 copy-start.5
  24.6 4.1 %all-to-all-start = ((bf16[4,2,192,384]{3,2,1,0:T(8,128)(2,1)}), bf16[4,2,192,384]{3,2,1,0:T(8,128)(2,1)S(1)}, u32[]{:S(2)}, u32[]{:S(2)}) async-start(bf16[4,2,192,384]{3,2,1,0:T(8,128)(2,1)} %shard_map.88), calls=%async_computation | async-start | bytes 2359296 | tf_op jit(solution)/shard_map/all_to_all | solution.py:99
  28.7 0.1 pad_add_fusion.base_ref
  28.8 0.0 copy-start.3
  28.8 0.0 collective-permute-done.perm_ref
  28.8 0.0 copy-done
  28.8 0.0 copy-done.5
  28.8 1.1 %shard_map.86 = (bf16[528,768]{1,0:T(8,128)(2,1)S(1)}, f32[1,512]{1,0:T(1,128)S(1)}) custom-call(s32[4]{0:T(128)S(1)} %pad_add_fusion.base_ref, bf16[512,768]{1,0:T(8,128)(2,1)S(1)} %bitcast.9, f32[768]{0:T(1024)S(1)} %copy-done.5, s32[1,512]{1,0:T(1,128)S(1)} %collective-permute-done.perm_ref), custom_call_target="tpu_custom_call" | custom-call | bytes 2097152 | tf_op jit(solution)/shard_map/pallas_call | solution.py:386
  29.9 0.0 copy-start.8
  29.9 1.9 %collective-permute-start.1 = (bf16[528,768]{1,0:T(8,128)(2,1)S(1)}, bf16[528,768]{1,0:T(8,128)(2,1)}, u32[]{:S(2)}, u32[]{:S(2)}) collective-permute-start(bf16[528,768]{1,0:T(8,128)(2,1)S(1)} %get-tuple-element.15.own_x), channel_id=1, source_target_pairs={{0,1},{1,0},{2,3},{3,2},{4,5},{5,4},{6,7},{7,6},{8,9},{9,8},{10,11... | collective-permute-start | bytes 2433032 | tf_op jit(solution)/shard_map/ppermute | solution.py:370
  31.8 2.4 %collective-permute-done.1.other_x = bf16[528,768]{1,0:T(8,128)(2,1)} collective-permute-done((bf16[528,768]{1,0:T(8,128)(2,1)S(1)}, bf16[528,768]{1,0:T(8,128)(2,1)}, u32[]{:S(2)}, u32[]{:S(2)}) %collective-permute-start.1) | collective-permute-done | bytes 811040 | tf_op jit(solution)/shard_map/ppermute | solution.py:370
  34.3 11.3 %all-to-all-done = bf16[4,2,192,384]{3,2,1,0:T(8,128)(2,1)S(1)} async-done(((bf16[4,2,192,384]{3,2,1,0:T(8,128)(2,1)}), bf16[4,2,192,384]{3,2,1,0:T(8,128)(2,1)S(1)}, u32[]{:S(2)}, u32[]{:S(2)}) %all-to-all-start) | async-done | bytes 1179680 | tf_op jit(solution)/shard_map/all_to_all | solution.py:99
  45.5 0.0 copy-done.3
  45.5 0.0 copy-done.8
  45.5 1.0 %copy-done.14 = bf16[4,2,192,384]{3,2,1,0:T(8,128)(2,1)} copy-done((bf16[4,2,192,384]{3,2,1,0:T(8,128)(2,1)}, bf16[4,2,192,384]{3,2,1,0:T(8,128)(2,1)S(1)}, u32[]{:S(2)}) %copy-start.14) | copy-done | bytes 1179672
  46.6 5.3 %shard_map.89 = (bf16[1024,768]{1,0:T(8,128)(2,1)}, bf16[32,48,128]{2,1,0:T(8,128)(2,1)}, bf16[384,384]{1,0:T(8,128)(2,1)}) custom-call(s32[4]{0:T(128)} %copy-done.3, s32[6]{0:T(128)} %offset_ref.3, bf16[528,768]{1,0:T(8,128)(2,1)} %copy-done.8, bf16[528,768]{1,0:T(8,128)(2,1)} %collective-permute-done.1.other_x, bf16[8,192,384]{2,1,0:T(8,128)(2,1)} %bitcast.10), custom_call_target="tpu_custom_call" | custom-call | flops 1207959552 | bytes 4194304 | tf_op jit(solution)/shard_map/pallas_call | solution.py:394
  51.9 7.0 %all-to-all-start.1 = ((bf16[32,48,128]{2,1,0:T(8,128)(2,1)}), bf16[32,48,128]{2,1,0:T(8,128)(2,1)S(1)}, u32[]{:S(2)}, u32[]{:S(2)}) async-start(bf16[32,48,128]{2,1,0:T(8,128)(2,1)} %get-tuple-element.16), calls=%async_computation.1 | async-start | bytes 786432 | tf_op jit(solution)/shard_map/all_to_all | solution.py:413
  58.9 8.2 %shard_map.91 = (f32[512,384]{1,0:T(8,128)}, f32[512,384]{1,0:T(8,128)}) custom-call(bf16[1024,768]{1,0:T(8,128)(2,1)} %get-tuple-element.17.q_ref.kv_ref, bf16[1024,768]{1,0:T(8,128)(2,1)} %get-tuple-element.17.q_ref.kv_ref), custom_call_target="tpu_custom_call" | custom-call | flops 1610612736 | bytes 3145728 | tf_op jit(solution)/shard_map/pallas_call | solution.py:226
  67.1 0.0 copy-start.6
  67.1 0.0 copy-start.7
  67.1 4.1 %collective-permute-start.3 = (f32[512,384]{1,0:T(8,128)}, f32[512,384]{1,0:T(8,128)S(1)}, u32[]{:S(2)}, u32[]{:S(2)}) collective-permute-start(f32[512,384]{1,0:T(8,128)} %get-tuple-element.19), channel_id=1, source_target_pairs={{0,1},{1,0},{2,3},{3,2},{4,5},{5,4},{6,7},{7,6},{8,9},{9,8},{10,11... | collective-permute-start | bytes 2359304 | tf_op jit(solution)/shard_map/ppermute | solution.py:370
  71.2 0.0 all-to-all-done.1.got_ref
  71.2 3.7 %shard_map.90 = bf16[32,2,16,128]{3,2,1,0:T(8,128)(2,1)} custom-call(s32[1]{0:T(128)} %bitcast.core_ref, bf16[32,48,128]{2,1,0:T(8,128)(2,1)S(1)} %all-to-all-done.1.got_ref), custom_call_target="tpu_custom_call" | custom-call | flops 536870912 | bytes 1048576 | tf_op jit(solution)/shard_map/pallas_call | solution.py:416
  74.9 10.4 %all-to-all-start.2 = ((bf16[64,16,128]{2,1,0:T(8,128)(2,1)}), bf16[64,16,128]{2,1,0:T(8,128)(2,1)S(1)}, u32[]{:S(2)}, u32[]{:S(2)}) async-start(bf16[64,16,128]{2,1,0:T(8,128)(2,1)} %bitcast.6), calls=%async_computation.2 | async-start | bytes 524288 | tf_op jit(solution)/shard_map/all_to_all | solution.py:420
  85.3 0.0 copy-done.9
  85.3 2.5 %collective-permute-start.4 = (bf16[384,384]{1,0:T(8,128)(2,1)S(1)}, bf16[384,384]{1,0:T(8,128)(2,1)S(1)}, u32[]{:S(2)}, u32[]{:S(2)}) collective-permute-start(bf16[384,384]{1,0:T(8,128)(2,1)S(1)} %copy-done.9), channel_id=1, source_target_pairs={{0,1},{1,0},{2,3},{3,2},{4,5},{5,4},{6,7},{7,6},{8,9},{9,8},{10,11... | collective-permute-start | bytes 884744 | tf_op jit(solution)/shard_map/ppermute | solution.py:370
  87.9 0.0 collective-permute-done.3.got_ref
  87.9 0.0 copy-done.1
  87.9 0.0 copy-done.4
  87.9 0.0 copy-done.6
  87.9 0.0 copy-done.7
  87.9 1.5 %shard_map.92 = (f32[512,384]{1,0:T(8,128)S(1)}, f32[384,128]{1,0:T(8,128)S(1)}, bf16[512,384]{1,0:T(8,128)(2,1)S(1)}, f32[1,384]{1,0:T(1,128)S(1)}) custom-call(s32[4]{0:T(128)S(1)} %copy-done.4, s32[6]{0:T(128)S(1)} %copy-done.7, f32[512,384]{1,0:T(8,128)S(1)} %copy-done.1, f32[512,384]{1,0:T(8,128)S(1)} %collective-permute-done.3.got_ref, ...), custom_call_target="tpu_custom_call" | custom-call | flops 268435456 | bytes 4194304 | tf_op jit(solution)/shard_map/pallas_call | solution.py:423
  89.4 0.0 copy-start.12
  89.4 0.7 copy-done.12
  90.1 0.0 collective-permute-done.4.other_w
  90.1 0.7 copy-done.10
  90.8 6.0 %all-to-all-done.2.far_ref = bf16[64,16,128]{2,1,0:T(8,128)(2,1)S(1)} async-done(((bf16[64,16,128]{2,1,0:T(8,128)(2,1)}), bf16[64,16,128]{2,1,0:T(8,128)(2,1)S(1)}, u32[]{:S(2)}, u32[]{:S(2)}) %all-to-all-start.2) | async-done | bytes 262176 | tf_op jit(solution)/shard_map/all_to_all | solution.py:420
  96.8 1.0 copy-done.11
  97.8 0.9 copy-done.13
  98.7 4.0 %shard_map.93 = (bf16[512,768]{1,0:T(8,128)(2,1)}, bf16[512,768]{1,0:T(8,128)(2,1)}) custom-call(s32[1]{0:T(128)} %bitcast.core_ref, bf16[64,16,128]{2,1,0:T(8,128)(2,1)S(1)} %all-to-all-done.2.far_ref, f32[512,384]{1,0:T(8,128)S(1)} %get-tuple-element.21.dense_ref, f32[384,128]{1,0:T(8,128)S(1)} %copy-done.13, ...), custom_call_target="tpu_custom_call" | custom-call | flops 1207959552 | bytes 4194304 | tf_op jit(solution)/shard_map/pallas_call | solution.py:437
  (7 shorter events, 0.0 us)
Async XLA Ops:
  2.4 20.1 %collective-permute-start.2 = (bf16[192,384]{1,0:T(8,128)(2,1)}, bf16[192,384]{1,0:T(8,128)(2,1)S(1)}, u32[]{:S(2)}, u32[]{:S(2)}) collective-permute-start(bf16[192,384]{1,0:T(8,128)(2,1)} %shard_map.87.own_ref), channel_id=1, source_target_pairs={{0,64},{64,0},{1,65},{65,1},{2,66},{66,2},{3,67},{67,3},{4,68},{68... | collective-permute-start | bytes 442376 | tf_op jit(solution)/shard_map/ppermute | solution.py:97
  10.7 18.2 %collective-permute-start = (s32[1,512]{1,0:T(1,128)}, s32[1,512]{1,0:T(1,128)S(1)}, u32[]{:S(2)}, u32[]{:S(2)}) collective-permute-start(s32[1,512]{1,0:T(1,128)} %param.8), channel_id=1, source_target_pairs={{63,0},{62,1},{61,2},{60,3},{59,4},{58,5},{57,6},{56,7},{55,8},{54... | collective-permute-start | bytes 6152 | tf_op jit(solution)/shard_map/ppermute | solution.py:384
  22.5 0.9 copy-start.2
  24.6 4.2 %copy-start = (bf16[1,512,768]{2,1,0:T(8,128)(2,1)S(1)}, bf16[1,512,768]{2,1,0:T(8,128)(2,1)}, u32[]{:S(2)}) copy-start(bf16[1,512,768]{2,1,0:T(8,128)(2,1)} %param.7) | copy-start | bytes 2359300
  24.6 4.2 %copy-start.5 = (f32[768]{0:T(1024)S(1)}, f32[768]{0:T(1024)}, u32[]{:S(2)}) copy-start(f32[768]{0:T(1024)} %gain_ref.2) | copy-start | bytes 9220
  24.6 20.9 %all-to-all-start = ((bf16[4,2,192,384]{3,2,1,0:T(8,128)(2,1)}), bf16[4,2,192,384]{3,2,1,0:T(8,128)(2,1)S(1)}, u32[]{:S(2)}, u32[]{:S(2)}) async-start(bf16[4,2,192,384]{3,2,1,0:T(8,128)(2,1)} %shard_map.88), calls=%async_computation | async-start | bytes 2359296 | tf_op jit(solution)/shard_map/all_to_all | solution.py:99
  28.8 16.7 %copy-start.3 = (s32[4]{0:T(128)}, s32[4]{0:T(128)S(1)}, u32[]{:S(2)}) copy-start(s32[4]{0:T(128)S(1)} %pad_add_fusion.base_ref) | copy-start | bytes 52
  29.9 15.6 %copy-start.8 = (bf16[528,768]{1,0:T(8,128)(2,1)}, bf16[528,768]{1,0:T(8,128)(2,1)S(1)}, u32[]{:S(2)}) copy-start(bf16[528,768]{1,0:T(8,128)(2,1)S(1)} %get-tuple-element.15.own_x) | copy-start | bytes 2433028
  29.9 4.3 %collective-permute-start.1 = (bf16[528,768]{1,0:T(8,128)(2,1)S(1)}, bf16[528,768]{1,0:T(8,128)(2,1)}, u32[]{:S(2)}, u32[]{:S(2)}) collective-permute-start(bf16[528,768]{1,0:T(8,128)(2,1)S(1)} %get-tuple-element.15.own_x), channel_id=1, source_target_pairs={{0,1},{1,0},{2,3},{3,2},{4,5},{5,4},{6,7},{7,6},{8,9},{9,8},{10,11... | collective-permute-start | bytes 2433032 | tf_op jit(solution)/shard_map/ppermute | solution.py:370
  45.5 1.0 %copy-start.14 = (bf16[4,2,192,384]{3,2,1,0:T(8,128)(2,1)}, bf16[4,2,192,384]{3,2,1,0:T(8,128)(2,1)S(1)}, u32[]{:S(2)}) copy-start(bf16[4,2,192,384]{3,2,1,0:T(8,128)(2,1)S(1)} %all-to-all-done) | copy-start | bytes 3538948
  51.9 19.3 %all-to-all-start.1 = ((bf16[32,48,128]{2,1,0:T(8,128)(2,1)}), bf16[32,48,128]{2,1,0:T(8,128)(2,1)S(1)}, u32[]{:S(2)}, u32[]{:S(2)}) async-start(bf16[32,48,128]{2,1,0:T(8,128)(2,1)} %get-tuple-element.16), calls=%async_computation.1 | async-start | bytes 786432 | tf_op jit(solution)/shard_map/all_to_all | solution.py:413
  67.1 18.3 %copy-start.9 = (bf16[384,384]{1,0:T(8,128)(2,1)S(1)}, bf16[384,384]{1,0:T(8,128)(2,1)}, u32[]{:S(2)}) copy-start(bf16[384,384]{1,0:T(8,128)(2,1)} %get-tuple-element.25.own_w) | copy-start | bytes 884740
  67.1 20.8 %copy-start.1 = (f32[512,384]{1,0:T(8,128)S(1)}, f32[512,384]{1,0:T(8,128)}, u32[]{:S(2)}) copy-start(f32[512,384]{1,0:T(8,128)} %get-tuple-element.18.keep_ref) | copy-start | bytes 2359300
  67.1 20.8 %copy-start.4 = (s32[4]{0:T(128)S(1)}, s32[4]{0:T(128)}, u32[]{:S(2)}) copy-start(s32[4]{0:T(128)} %copy-done.3) | copy-start | bytes 52
  67.1 20.8 %copy-start.6 = (f32[384]{0:T(512)S(1)}, f32[384]{0:T(512)}, u32[]{:S(2)}) copy-start(f32[384]{0:T(512)} %gain_ref.3) | copy-start | bytes 4612
  67.1 20.8 %copy-start.7 = (s32[6]{0:T(128)S(1)}, s32[6]{0:T(128)}, u32[]{:S(2)}) copy-start(s32[6]{0:T(128)} %offset_ref.3) | copy-start | bytes 76
  67.1 20.8 %collective-permute-start.3 = (f32[512,384]{1,0:T(8,128)}, f32[512,384]{1,0:T(8,128)S(1)}, u32[]{:S(2)}, u32[]{:S(2)}) collective-permute-start(f32[512,384]{1,0:T(8,128)} %get-tuple-element.19), channel_id=1, source_target_pairs={{0,1},{1,0},{2,3},{3,2},{4,5},{5,4},{6,7},{7,6},{8,9},{9,8},{10,11... | collective-permute-start | bytes 2359304 | tf_op jit(solution)/shard_map/ppermute | solution.py:370
  74.9 21.9 %all-to-all-start.2 = ((bf16[64,16,128]{2,1,0:T(8,128)(2,1)}), bf16[64,16,128]{2,1,0:T(8,128)(2,1)S(1)}, u32[]{:S(2)}, u32[]{:S(2)}) async-start(bf16[64,16,128]{2,1,0:T(8,128)(2,1)} %bitcast.6), calls=%async_computation.2 | async-start | bytes 524288 | tf_op jit(solution)/shard_map/all_to_all | solution.py:420
  85.3 4.7 %collective-permute-start.4 = (bf16[384,384]{1,0:T(8,128)(2,1)S(1)}, bf16[384,384]{1,0:T(8,128)(2,1)S(1)}, u32[]{:S(2)}, u32[]{:S(2)}) collective-permute-start(bf16[384,384]{1,0:T(8,128)(2,1)S(1)} %copy-done.9), channel_id=1, source_target_pairs={{0,1},{1,0},{2,3},{3,2},{4,5},{5,4},{6,7},{7,6},{8,9},{9,8},{10,11... | collective-permute-start | bytes 884744 | tf_op jit(solution)/shard_map/ppermute | solution.py:370
  89.4 0.7 copy-start.12
  90.1 0.7 copy-start.10
  96.8 1.0 copy-start.11
  97.8 0.9 copy-start.13

commit v5 on v4

--- a/solution.py
+++ b/solution.py
@@ -19,7 +19,7 @@
 DP_X, DP_Y = 4, 2
 INTERPRET = False
 NEAR_TILE = 256
-LIMITS = [60 * 1024 * 1024, 60 * 1024 * 1024, 24 << 20, 24 << 20, 24 << 20]
+LIMITS = [24 << 20, 60 * 1024 * 1024, 24 << 20, 24 << 20, 24 << 20]
 
 eps_norm = 1e-05
 EXP_SCALE = HEAD_DIM ** (-0.5) * 1.4426950408889634
@@ -29,7 +29,7 @@
 BF16 = jnp.bfloat16
 VMEM = pl.BlockSpec(memory_space=pltpu.VMEM)
 SMEM = pl.BlockSpec(memory_space=pltpu.SMEM)
-HBM = pl.BlockSpec(memory_space=pltpu.HBM)
+ANY = pl.BlockSpec(memory_space=pl.ANY)
 
 
 def call(kernel, out_shape, specs, scratch=(), flops=0, moved=0, limit=24 << 20, outs=None):
@@ -95,7 +95,9 @@
 def gather_weights(core, projection, output_weight):
     packed = pack_weights(core, projection, output_weight)
     other = lax.ppermute(packed, "yh", [(0, 1), (1, 0)])
-    both = call(fan_kernel, shape_of(DP_X, DP_Y, 192, INNER), [VMEM, VMEM])(packed, other)
+    both = call(fan_kernel, shape_of(DP_X, DP_Y, 192, INNER), [VMEM, VMEM], limit=60 * 1024 * 1024)(
+        packed, other
+    )
     got = lax.all_to_all(both, "x", 0, 0, tiled=True)
     return got.reshape(DP_X * DP_Y, 192, INNER)
 
@@ -138,48 +140,47 @@
     return jnp.where(token == index, 1.0, 0.0).astype(BF16)
 
 
-def project_kernel(
-    base_ref, offset_ref, own_x, other_x, packed_ref,
-    all_out, send_ref, outw_ref, w_ref, all_ref, sems,
-):
-    flip = base_ref[3]
+def pick_kernel(base_ref, offset_ref, own_x, other_x, picked_ref):
+    orders = order_of(own_x), order_of(other_x)
+    hots = [[], []]
+    for head in range(HALF):
+        offset = offset_ref[base_ref[0] * HALF + head]
+        for view in range(2):
+            for part in range(2):
+                chosen = one_hot(chosen_rows(view, offset, orders[part]), TOK)
+                hots[part].append(chosen)
+    for part, x_ref in enumerate((own_x, other_x)):
+        rows = jnp.dot(
+            jnp.concatenate(hots[part], axis=0), x_ref[0:TOK, :], preferred_element_type=F32
+        ).astype(BF16)
+        for block in range(2 * HALF):
+            at = block * 2 * SPARSE + part * SPARSE
+            picked_ref[at : at + SPARSE, :] = rows[block * SPARSE : block * SPARSE + SPARSE]
+
+
+def unpack_head(flip, packed_ref, lanes, w_ref, at):
     lane = lax.broadcasted_iota(jnp.int32, (48, 128), 1)
     for entry in range(8):
         shard = (entry - entry % 2) + (entry % 2 ^ flip)
         row = pl.multiple_of(shard * 96, 16)
-        for head in range(HALF):
-            at = head * 256
-            w_ref[pl.ds(row, 96), at : at + 128] = packed_ref[
-                entry, 0:96, head * 128 : head * 128 + 128
-            ]
-            folded = packed_ref[entry, 96:144, head * 128 : head * 128 + 128].astype(F32)
-            for first, part in ((0, folded), (48, swap_halves(folded))):
-                w_ref[pl.ds(pl.multiple_of(row + first, 16), 48), at + 128 : at + 256] = jnp.where(
-                    lane < HEAD_DIM, part, 0.0
-                ).astype(BF16)
-        outw_ref[pl.ds(pl.multiple_of(shard * 48, 16), 48), :] = packed_ref[entry, 144:192, :]
-    copies = []
-    for part, x_ref in enumerate((own_x, other_x)):
-        for step in range(0, TOK, 256):
-            at = part * TOK + step
-            all_ref[at : at + 256, :] = jnp.dot(
-                x_ref[step : step + 256, :], w_ref[...], preferred_element_type=F32
+        w_ref[pl.ds(row, 96), at : at + 128] = packed_ref[entry, 0:96, lanes]
+        folded = packed_ref[entry, 96:144, lanes].astype(F32)
+        for first, part in ((0, folded), (48, swap_halves(folded))):
+            w_ref[pl.ds(pl.multiple_of(row + first, 16), 48), at + 128 : at + 256] = jnp.where(
+                lane < HEAD_DIM, part, 0.0
             ).astype(BF16)
-        rows = pl.ds(part * TOK, TOK)
-        copies.append(pltpu.make_async_copy(all_ref.at[rows], all_out.at[rows], sems.at[part]))
-        copies[-1].start()
-    own_order, other_order = order_of(own_x), order_of(other_x)
+
+
+def send_kernel(base_ref, picked_ref, packed_ref, send_ref, w_ref):
     for head in range(HALF):
-        offset = offset_ref[base_ref[0] * HALF + head]
-        index = []
-        for view in range(2):
-            index.append(chosen_rows(view, offset, own_order))
-            index.append(chosen_rows(view, offset, other_order) + TOK)
-        chosen = one_hot(jnp.concatenate(index, axis=0), SEG)
+        at = head * 256
+        unpack_head(base_ref[3], packed_ref, slice(head * 128, head * 128 + 128), w_ref, at)
         far_rows = jnp.dot(
-            chosen, all_ref[:, head * 256 : head * 256 + 256], preferred_element_type=F32
-        )
-        far_kv, far_q = far_rows[:, 0:128].astype(BF16), far_rows[:, 128:256]
+            picked_ref[head * 128 : head * 128 + 128, :],
+            w_ref[:, at : at + 256],
+            preferred_element_type=F32,
+        ).astype(BF16)
+        far_kv, far_q = far_rows[:, 0:128], far_rows[:, 128:256].astype(F32)
         for view in range(2):
             pair = (view * HALF + head) * 4
             for q_part in range(2):
@@ -189,24 +190,39 @@
                 ).astype(BF16)
                 for k_half in range(2):
                     peer = pair + q_part * 2 + k_half
-                    at = view * 2 * SPARSE + k_half * SPARSE
-                    send_ref[peer, 0:32, :] = far_kv[at : at + SPARSE]
+                    first = view * 2 * SPARSE + k_half * SPARSE
+                    send_ref[peer, 0:32, :] = far_kv[first : first + SPARSE]
                     send_ref[peer, 32:48, :] = folded
     for peer in range(4 * 2 * HALF, POS):
         send_ref[peer] = jnp.zeros((48, 128), BF16)
-    for copy in copies:
-        copy.wait()
-
-
-def near_kernel(q_ref, kv_ref, keep_ref, give_ref):
-    keys = kv_ref[...]
+
+
+def near_kernel(base_ref, own_x, other_x, packed_ref, keep_ref, give_ref, outw_ref, w_ref, all_ref):
+    flip = base_ref[3]
+
+    @pl.when(pl.program_id(0) == 0)
+    def _():
+        for entry in range(8):
+            shard = (entry - entry % 2) + (entry % 2 ^ flip)
+            outw_ref[pl.ds(pl.multiple_of(shard * 48, 16), 48), :] = packed_ref[entry, 144:192, :]
+
+    lanes = pl.ds(pl.multiple_of(pl.program_id(0) * 128, 128), 128)
+    unpack_head(flip, packed_ref, lanes, w_ref, 0)
+    for part, x_ref in enumerate((own_x, other_x)):
+        all_ref[part * TOK : part * TOK + TOK, :] = jnp.dot(
+            x_ref[0:TOK, :], w_ref[...], preferred_element_type=F32
+        ).astype(BF16)
+    keys = all_ref[:, 0:128]
     lane = lax.broadcasted_iota(jnp.int32, (SEG, 128), 1)
     values = jnp.where(lane < HEAD_DIM, swap_halves(keys.astype(F32)), 1.0).astype(BF16)
     tile = NEAR_TILE
     out_lane = lax.broadcasted_iota(jnp.int32, (tile, 128), 1)
     for at in range(0, SEG, tile):
         scores = lax.dot_general(
-            q_ref[at : at + tile, :], keys, (((1,), (1,)), ((), ())), preferred_element_type=F32
+            all_ref[at : at + tile, 128:256],
+            keys,
+            (((1,), (1,)), ((), ())),
+            preferred_element_type=F32,
         )
         row_max = jnp.max(scores, axis=1, keepdims=True)
         weights = jnp.exp2((scores - row_max) * EXP_SCALE).astype(BF16)
@@ -218,23 +234,23 @@
         out_ref[at % TOK : at % TOK + tile, :] = result
 
 
-def near_level(both):
+def near_level(base, own_x, other_x, packed):
     half = shape_of(TOK, HALF * 128, dtype=F32)
-    keys = pl.BlockSpec((SEG, 128), lambda h: (0, 2 * h))
-    queries = pl.BlockSpec((SEG, 128), lambda h: (0, 2 * h + 1))
+    tiles = pl.BlockSpec((TOK + 16, D), lambda h: (0, 0))
     part = pl.BlockSpec((TOK, 128), lambda h: (0, h))
     return pl.pallas_call(
         near_kernel,
-        out_shape=[half, half],
+        out_shape=[half, half, shape_of(INNER, INNER)],
         grid=(HALF,),
-        in_specs=[queries, keys],
-        out_specs=[part, part],
+        in_specs=[SMEM, tiles, tiles, pl.BlockSpec((8, 192, INNER), lambda h: (0, 0, 0))],
+        out_specs=[part, part, pl.BlockSpec((INNER, INNER), lambda h: (0, 0))],
+        scratch_shapes=[pltpu.VMEM((D, 256), BF16), pltpu.VMEM((SEG, 256), BF16)],
         cost_estimate=pl.CostEstimate(
-            flops=4 * HALF * SEG * SEG * 128, bytes_accessed=3 << 20, transcendentals=HALF * SEG * SEG
+            flops=4 * HALF * SEG * SEG * 128, bytes_accessed=5 << 20, transcendentals=HALF * SEG * SEG
         ),
         compiler_params=pltpu.CompilerParams(vmem_limit_bytes=LIMITS[1]),
         interpret=INTERPRET,
-    )(both, both)
+    )(base, own_x, other_x, packed)
 
 
 def far_kernel(core_ref, got_ref, back_ref):
@@ -306,7 +322,8 @@
 
 
 def output_kernel(
-    core_ref, far_ref, dense_ref, rows_ref, spread_ref, gain_ref, own_w, other_w, plain_ref, flip_ref
+    core_ref, far_ref, dense_ref, rows_ref, spread_ref, gain_ref, own_w, other_w, plain_out, flip_out,
+    plain_ref, flip_ref, sems,
 ):
     core = core_ref[0]
     lane = lax.broadcasted_iota(jnp.int32, (192, 128), 1)
@@ -343,7 +360,8 @@
     weights = [
         jnp.concatenate([part[own_rows, :], part[other_rows, :]], axis=0) for part in (own_w, other_w)
     ]
-    for view, out_ref in enumerate((plain_ref, flip_ref)):
+    copies = []
+    for view, (out_ref, hbm_ref) in enumerate(((plain_ref, plain_out), (flip_ref, flip_out))):
         delta = jnp.concatenate([d[view * 96 : view * 96 + 96] for d in deltas], axis=0)
         blocks = jnp.where(row == col, jnp.concatenate([delta] * HEADS, axis=1), 0.0).astype(BF16)
         if view == 0:
@@ -364,6 +382,15 @@
                 out_ref[at : at + 256, pl.ds(pl.multiple_of(place * INNER, 128), INNER)] = jnp.dot(
                     mixed, part, preferred_element_type=F32
                 ).astype(BF16)
+            rows = pl.ds(at, 256)
+            copies.append(
+                pltpu.make_async_copy(
+                    out_ref.at[rows], hbm_ref.at[rows], sems.at[view * 2 + at // 256]
+                )
+            )
+            copies[-1].start()
+    for copy in copies:
+        copy.wait()
 
 
 def core_swap(block):
@@ -391,27 +418,25 @@
     )(base, tile_features[0], input_gain, own_perm)
     other_x = core_swap(own_x)
 
-    both, send, own_w = call(
-        project_kernel,
-        [
-            shape_of(SEG, D),
-            shape_of(POS, 48, 128),
-            shape_of(INNER, INNER),
-        ],
-        [SMEM, SMEM, VMEM, VMEM, VMEM],
-        [
-            pltpu.VMEM((D, D), BF16),
-            pltpu.VMEM((SEG, D), BF16),
-            pltpu.SemaphoreType.DMA((2,)),
-        ],
-        outs=[HBM, VMEM, VMEM],
-        flops=2 * SEG * D * D,
-        moved=4 << 20,
+    picked = call(
+        pick_kernel,
+        shape_of(HALF * 128, D),
+        [SMEM, SMEM, VMEM, VMEM],
+        flops=2 * HALF * 128 * SEG * D,
+        moved=3 << 20,
+    )(base, head_offsets, own_x, other_x)
+    send = call(
+        send_kernel,
+        shape_of(POS, 48, 128),
+        [SMEM, VMEM, VMEM],
+        [pltpu.VMEM((D, D), BF16)],
+        flops=2 * HALF * 128 * D * 256,
+        moved=2 << 20,
         limit=LIMITS[0],
-    )(base, head_offsets, own_x, other_x, packed)
+    )(base, picked, packed)
 
     got = lax.all_to_all(send, "pos", 0, 0, tiled=True)
-    keep, give = near_level(both)
+    keep, give, own_w = near_level(base, own_x, other_x, packed)
     near_got = core_swap(give)
     back = call(
         far_kernel, shape_of(POS, 2, 16, 128), [SMEM, VMEM], flops=4 * SEG * SEG * 128, moved=1 << 20,
@@ -438,6 +463,8 @@
         output_kernel,
         [shape_of(TOK, D), shape_of(TOK, D)],
         [SMEM] + [VMEM] * 7,
+        [pltpu.VMEM((TOK, D), BF16), pltpu.VMEM((TOK, D), BF16), pltpu.SemaphoreType.DMA((4,))],
+        outs=[ANY, ANY],
         flops=4 * SEG * INNER * D,
         moved=4 << 20,
         limit=LIMITS[4],

time: 103 us -> 103 us (level)
  waiting for transfers between devices: 19.7 us -> 17.7 us
  Pallas kernels: 26.6 us -> 28.1 us
    all_to_all x1, waiting for transfers between devices: 11.3 us -> 9.39 us  [gather_weights(): got = lax.all_to_all(both, 'x', 0, 0, tiled=True)]
    pallas_call x3 -> x4, Pallas kernels: 14.7 us -> 16.4 us  [the longest x1 11.2 us: near_level(): pl.pallas_call(near_kernel, out_shape=[half, half, shape_of(INNER, INNER)...]
    unnamed x30 -> x32, local copies, waits for them, and re-layouts: 5.26 us -> 4.87 us
  transfers between devices with their start and end apart: 8 -> 8, of which waited for: 3 -> 3; matrix products, arithmetic and copies ran while one was open for 0% -> 0% of each run, Pallas kernels for 15% -> 20%
where the time goes in v5:
time: 103 us; the launch traced here: 102 us
  starting transfers between devices  50.2 us (49%)
  Pallas kernels  28.1 us (27%)
  waiting for transfers between devices  17.7 us (17%)
  local copies, waits for them, and re-layouts  4.87 us (5%)
    ppermute x1, starting transfers between devices, layer(): lax.ppermute(flip_perm, ctx, [(last - r, r) for r in range(2 * POS)])  11.9 us
    pallas_call x1, Pallas kernels, near_level(): pl.pallas_call(near_kernel, out_shape=[half, half, shape_of(INNER, INNER)...  11.2 us
    all_to_all x1, starting transfers between devices, layer(): far = lax.all_to_all(back.reshape(2 * POS, 16, 128), ctx, 0, 0, tiled=True)  10.4 us
    all_to_all x1, waiting for transfers between devices, gather_weights(): got = lax.all_to_all(both, 'x', 0, 0, tiled=True)  9.39 us
    ppermute x3, starting transfers between devices, core_swap(): return lax.ppermute(block, 'core', [(0, 1), (1, 0)])  8.53 us
    ppermute x1, starting transfers between devices, gather_weights(): other = lax.ppermute(packed, 'yh', [(0, 1), (1, 0)])  8.26 us
    all_to_all x1, starting transfers between devices, layer(): got = lax.all_to_all(send, 'pos', 0, 0, tiled=True)  6.97 us
    all_to_all x1, waiting for transfers between devices, layer(): far = lax.all_to_all(back.reshape(2 * POS, 16, 128), ctx, 0, 0, tiled=True)  6.04 us
  transfers between devices with their start and end apart: 8, of which 3 were waited for; matrix products, arithmetic and copies ran while one was open for 0% of the time, Pallas kernels for 20%

profile of v5, /device:TPU:1, one launch (start us, length us, event | category | flops | bytes accessed | tf_op | source)
XLA Modules:
  0.0 102.0 jit_solution(3710679599842406169)
XLA Ops:
  0.6 1.8 %shard_map.88.own_ref = bf16[192,384]{1,0:T(8,128)(2,1)} custom-call(s32[1]{0:T(128)} %bitcast.core_ref, bf16[96,1152]{1,0:T(8,128)(2,1)} %proj_ref.1, bf16[48,768]{1,0:T(8,128)(2,1)} %outw_ref.1), custom_call_target="tpu_custom_call" | custom-call | tf_op jit(solution)/shard_map/pallas_call | solution.py:84
  2.4 8.3 %collective-permute-start.2 = (bf16[192,384]{1,0:T(8,128)(2,1)}, bf16[192,384]{1,0:T(8,128)(2,1)S(1)}, u32[]{:S(2)}, u32[]{:S(2)}) collective-permute-start(bf16[192,384]{1,0:T(8,128)(2,1)} %shard_map.88.own_ref), channel_id=1, source_target_pairs={{0,64},{64,0},{1,65},{65,1},{2,66},{66,2},{3,67},{67,3},{4,68},{68... | collective-permute-start | bytes 442376 | tf_op jit(solution)/shard_map/ppermute | solution.py:97
  10.7 11.9 %collective-permute-start = (s32[1,512]{1,0:T(1,128)}, s32[1,512]{1,0:T(1,128)S(1)}, u32[]{:S(2)}, u32[]{:S(2)}) collective-permute-start(s32[1,512]{1,0:T(1,128)} %param.8), channel_id=1, source_target_pairs={{63,0},{62,1},{61,2},{60,3},{59,4},{58,5},{57,6},{56,7},{55,8},{54... | collective-permute-start | bytes 6152 | tf_op jit(solution)/shard_map/ppermute | solution.py:411
  22.5 0.0 collective-permute-done.2.other_ref
  22.5 0.0 copy-start.15
  22.6 0.7 copy-done.15
  23.2 2.1 %shard_map.89 = bf16[4,2,192,384]{3,2,1,0:T(8,128)(2,1)} custom-call(bf16[192,384]{1,0:T(8,128)(2,1)} %shard_map.88.own_ref, bf16[192,384]{1,0:T(8,128)(2,1)} %copy-done.15), custom_call_target="tpu_custom_call" | custom-call | tf_op jit(solution)/shard_map/pallas_call | solution.py:98
  25.3 0.0 copy-start.1
  25.3 4.1 %all-to-all-start = ((bf16[4,2,192,384]{3,2,1,0:T(8,128)(2,1)}), bf16[4,2,192,384]{3,2,1,0:T(8,128)(2,1)S(1)}, u32[]{:S(2)}, u32[]{:S(2)}) async-start(bf16[4,2,192,384]{3,2,1,0:T(8,128)(2,1)} %shard_map.89), calls=%async_computation | async-start | bytes 2359296 | tf_op jit(solution)/shard_map/all_to_all | solution.py:101
  29.5 0.1 pad_add_fusion.base_ref
  29.5 0.0 collective-permute-done.perm_ref
  29.6 0.0 copy-done.1
  29.6 0.0 copy-done.5
  29.6 1.1 %shard_map.86 = (bf16[528,768]{1,0:T(8,128)(2,1)S(1)}, f32[1,512]{1,0:T(1,128)S(1)}) custom-call(s32[4]{0:T(128)S(1)} %pad_add_fusion.base_ref, bf16[512,768]{1,0:T(8,128)(2,1)S(1)} %bitcast.11, f32[768]{0:T(1024)S(1)} %copy-done.5, s32[1,512]{1,0:T(1,128)S(1)} %collective-permute-done.perm_ref), custom_call_target="tpu_custom_call" | custom-call | bytes 2097152 | tf_op jit(solution)/shard_map/pallas_call | solution.py:413
  30.6 0.0 copy-start.8
  30.6 1.9 %collective-permute-start.1 = (bf16[528,768]{1,0:T(8,128)(2,1)S(1)}, bf16[528,768]{1,0:T(8,128)(2,1)S(1)}, u32[]{:S(2)}, u32[]{:S(2)}) collective-permute-start(bf16[528,768]{1,0:T(8,128)(2,1)S(1)} %get-tuple-element.13.own_x), channel_id=1, source_target_pairs={{0,1},{1,0},{2,3},{3,2},{4,5},{5,4},{6,7},{7,6},{8,9},{9,8},{10,11... | collective-permute-start | bytes 2433032 | tf_op jit(solution)/shard_map/ppermute | solution.py:397
  32.6 2.3 %collective-permute-done.1.other_x = bf16[528,768]{1,0:T(8,128)(2,1)S(1)} collective-permute-done((bf16[528,768]{1,0:T(8,128)(2,1)S(1)}, bf16[528,768]{1,0:T(8,128)(2,1)S(1)}, u32[]{:S(2)}, u32[]{:S(2)}) %collective-permute-start.1) | collective-permute-done | bytes 811040 | tf_op jit(solution)/shard_map/ppermute | solution.py:397
  34.9 0.0 copy-done.7
  34.9 1.1 %shard_map.87.picked_ref = bf16[384,768]{1,0:T(8,128)(2,1)S(1)} custom-call(s32[4]{0:T(128)S(1)} %pad_add_fusion.base_ref, s32[6]{0:T(128)S(1)} %copy-done.7, bf16[528,768]{1,0:T(8,128)(2,1)S(1)} %get-tuple-element.13.own_x, bf16[528,768]{1,0:T(8,128)(2,1)S(1)} %collective-permute-done.1.other_x), custom_call_target="tpu_custom_call" | custom-call | flops 603979776 | bytes 3145728 | tf_op jit(solution)/shard_map/pallas_call | solution.py:421
  35.9 0.0 copy-start.9
  36.0 0.9 copy-done.9
  36.9 9.4 %all-to-all-done = bf16[4,2,192,384]{3,2,1,0:T(8,128)(2,1)S(1)} async-done(((bf16[4,2,192,384]{3,2,1,0:T(8,128)(2,1)}), bf16[4,2,192,384]{3,2,1,0:T(8,128)(2,1)S(1)}, u32[]{:S(2)}, u32[]{:S(2)}) %all-to-all-start) | async-done | bytes 1179680 | tf_op jit(solution)/shard_map/all_to_all | solution.py:101
  46.2 0.0 copy-done.3
  46.2 2.0 %shard_map.90 = bf16[32,48,128]{2,1,0:T(8,128)(2,1)} custom-call(s32[4]{0:T(128)S(1)} %pad_add_fusion.base_ref, bf16[384,768]{1,0:T(8,128)(2,1)S(1)} %shard_map.87.picked_ref, bf16[8,192,384]{2,1,0:T(8,128)(2,1)S(1)} %bitcast.9), custom_call_target="tpu_custom_call" | custom-call | flops 150994944 | bytes 2097152 | tf_op jit(solution)/shard_map/pallas_call | solution.py:428
  48.2 0.0 copy-done.8
  48.2 0.0 copy-done
  48.2 7.0 %all-to-all-start.1 = ((bf16[32,48,128]{2,1,0:T(8,128)(2,1)}), bf16[32,48,128]{2,1,0:T(8,128)(2,1)S(1)}, u32[]{:S(2)}, u32[]{:S(2)}) async-start(bf16[32,48,128]{2,1,0:T(8,128)(2,1)} %shard_map.90), calls=%async_computation.1 | async-start | bytes 786432 | tf_op jit(solution)/shard_map/all_to_all | solution.py:438
  55.2 11.2 %shard_map.92 = (f32[512,384]{1,0:T(8,128)}, f32[512,384]{1,0:T(8,128)}, bf16[384,384]{1,0:T(8,128)(2,1)}) custom-call(s32[4]{0:T(128)} %copy-done.3, bf16[528,768]{1,0:T(8,128)(2,1)} %copy-done.8, bf16[528,768]{1,0:T(8,128)(2,1)} %copy-done.9, bf16[8,192,384]{2,1,0:T(8,128)(2,1)} %bitcast.10), custom_call_target="tpu_custom_call" | custom-call | flops 1610612736 | bytes 5242880 | tf_op jit(solution)/shard_map/pallas_call | solution.py:241
  66.4 0.0 copy-start.6
  66.5 4.1 %collective-permute-start.3 = (f32[512,384]{1,0:T(8,128)}, f32[512,384]{1,0:T(8,128)S(1)}, u32[]{:S(2)}, u32[]{:S(2)}) collective-permute-start(f32[512,384]{1,0:T(8,128)} %get-tuple-element.15), channel_id=1, source_target_pairs={{0,1},{1,0},{2,3},{3,2},{4,5},{5,4},{6,7},{7,6},{8,9},{9,8},{10,11... | collective-permute-start | bytes 2359304 | tf_op jit(solution)/shard_map/ppermute | solution.py:397
  70.5 0.0 all-to-all-done.1.got_ref
  70.5 3.7 %shard_map.91 = bf16[32,2,16,128]{3,2,1,0:T(8,128)(2,1)} custom-call(s32[1]{0:T(128)} %bitcast.core_ref, bf16[32,48,128]{2,1,0:T(8,128)(2,1)S(1)} %all-to-all-done.1.got_ref), custom_call_target="tpu_custom_call" | custom-call | flops 536870912 | bytes 1048576 | tf_op jit(solution)/shard_map/pallas_call | solution.py:441
  74.3 10.4 %all-to-all-start.2 = ((bf16[64,16,128]{2,1,0:T(8,128)(2,1)}), bf16[64,16,128]{2,1,0:T(8,128)(2,1)S(1)}, u32[]{:S(2)}, u32[]{:S(2)}) async-start(bf16[64,16,128]{2,1,0:T(8,128)(2,1)} %bitcast.6), calls=%async_computation.2 | async-start | bytes 524288 | tf_op jit(solution)/shard_map/all_to_all | solution.py:445
  84.7 0.0 copy-done.10
  84.7 2.5 %collective-permute-start.4 = (bf16[384,384]{1,0:T(8,128)(2,1)S(1)}, bf16[384,384]{1,0:T(8,128)(2,1)S(1)}, u32[]{:S(2)}, u32[]{:S(2)}) collective-permute-start(bf16[384,384]{1,0:T(8,128)(2,1)S(1)} %copy-done.10), channel_id=1, source_target_pairs={{0,1},{1,0},{2,3},{3,2},{4,5},{5,4},{6,7},{7,6},{8,9},{9,8},{10,11... | collective-permute-start | bytes 884744 | tf_op jit(solution)/shard_map/ppermute | solution.py:397
  87.2 0.0 collective-permute-done.3.got_ref
  87.2 0.0 copy-done.2
  87.3 0.0 copy-done.4
  87.3 0.0 copy-done.6
  87.3 1.5 %shard_map.93 = (f32[512,384]{1,0:T(8,128)S(1)}, f32[384,128]{1,0:T(8,128)S(1)}, bf16[512,384]{1,0:T(8,128)(2,1)S(1)}, f32[1,384]{1,0:T(1,128)S(1)}) custom-call(s32[4]{0:T(128)S(1)} %copy-done.4, s32[6]{0:T(128)S(1)} %copy-done.7, f32[512,384]{1,0:T(8,128)S(1)} %copy-done.2, f32[512,384]{1,0:T(8,128)S(1)} %collective-permute-done.3.got_ref, ...), custom_call_target="tpu_custom_call" | custom-call | flops 268435456 | bytes 4194304 | tf_op jit(solution)/shard_map/pallas_call | solution.py:448
  88.7 0.0 copy-start.13
  88.8 0.7 copy-done.13
  89.4 0.0 collective-permute-done.4.other_w
  89.4 0.7 copy-done.11
  90.1 6.0 %all-to-all-done.2.far_ref = bf16[64,16,128]{2,1,0:T(8,128)(2,1)S(1)} async-done(((bf16[64,16,128]{2,1,0:T(8,128)(2,1)}), bf16[64,16,128]{2,1,0:T(8,128)(2,1)S(1)}, u32[]{:S(2)}, u32[]{:S(2)}) %all-to-all-start.2) | async-done | bytes 262176 | tf_op jit(solution)/shard_map/all_to_all | solution.py:445
  96.2 1.0 copy-done.12
  97.2 0.9 copy-done.14
  98.1 3.8 %shard_map.94 = (bf16[512,768]{1,0:T(8,128)(2,1)}, bf16[512,768]{1,0:T(8,128)(2,1)}) custom-call(s32[1]{0:T(128)} %bitcast.core_ref, bf16[64,16,128]{2,1,0:T(8,128)(2,1)S(1)} %all-to-all-done.2.far_ref, f32[512,384]{1,0:T(8,128)S(1)} %get-tuple-element.17.dense_ref, f32[384,128]{1,0:T(8,128)S(1)} %copy-done.14, ...), custom_call_target="tpu_custom_call" | custom-call | flops 1207959552 | bytes 4194304 | tf_op jit(solution)/shard_map/pallas_call | solution.py:462
  (10 shorter events, 0.0 us)
Async XLA Ops:
  2.4 20.1 %collective-permute-start.2 = (bf16[192,384]{1,0:T(8,128)(2,1)}, bf16[192,384]{1,0:T(8,128)(2,1)S(1)}, u32[]{:S(2)}, u32[]{:S(2)}) collective-permute-start(bf16[192,384]{1,0:T(8,128)(2,1)} %shard_map.88.own_ref), channel_id=1, source_target_pairs={{0,64},{64,0},{1,65},{65,1},{2,66},{66,2},{3,67},{67,3},{4,68},{68... | collective-permute-start | bytes 442376 | tf_op jit(solution)/shard_map/ppermute | solution.py:97
  10.7 18.9 %collective-permute-start = (s32[1,512]{1,0:T(1,128)}, s32[1,512]{1,0:T(1,128)S(1)}, u32[]{:S(2)}, u32[]{:S(2)}) collective-permute-start(s32[1,512]{1,0:T(1,128)} %param.8), channel_id=1, source_target_pairs={{63,0},{62,1},{61,2},{60,3},{59,4},{58,5},{57,6},{56,7},{55,8},{54... | collective-permute-start | bytes 6152 | tf_op jit(solution)/shard_map/ppermute | solution.py:411
  22.5 0.7 copy-start.15
  25.3 4.2 %copy-start.1 = (bf16[1,512,768]{2,1,0:T(8,128)(2,1)S(1)}, bf16[1,512,768]{2,1,0:T(8,128)(2,1)}, u32[]{:S(2)}) copy-start(bf16[1,512,768]{2,1,0:T(8,128)(2,1)} %param.7) | copy-start | bytes 2359300
  25.3 4.2 %copy-start.5 = (f32[768]{0:T(1024)S(1)}, f32[768]{0:T(1024)}, u32[]{:S(2)}) copy-start(f32[768]{0:T(1024)} %gain_ref.2) | copy-start | bytes 9220
  25.3 9.5 %copy-start.7 = (s32[6]{0:T(128)S(1)}, s32[6]{0:T(128)}, u32[]{:S(2)}) copy-start(s32[6]{0:T(128)} %offset_ref.3) | copy-start | bytes 76
  25.3 20.9 %all-to-all-start = ((bf16[4,2,192,384]{3,2,1,0:T(8,128)(2,1)}), bf16[4,2,192,384]{3,2,1,0:T(8,128)(2,1)S(1)}, u32[]{:S(2)}, u32[]{:S(2)}) async-start(bf16[4,2,192,384]{3,2,1,0:T(8,128)(2,1)} %shard_map.89), calls=%async_computation | async-start | bytes 2359296 | tf_op jit(solution)/shard_map/all_to_all | solution.py:101
  29.5 16.7 %copy-start.3 = (s32[4]{0:T(128)}, s32[4]{0:T(128)S(1)}, u32[]{:S(2)}) copy-start(s32[4]{0:T(128)S(1)} %pad_add_fusion.base_ref) | copy-start | bytes 52
  30.6 17.6 %copy-start.8 = (bf16[528,768]{1,0:T(8,128)(2,1)}, bf16[528,768]{1,0:T(8,128)(2,1)S(1)}, u32[]{:S(2)}) copy-start(bf16[528,768]{1,0:T(8,128)(2,1)S(1)} %get-tuple-element.13.own_x) | copy-start | bytes 2433028
  30.6 4.2 %collective-permute-start.1 = (bf16[528,768]{1,0:T(8,128)(2,1)S(1)}, bf16[528,768]{1,0:T(8,128)(2,1)S(1)}, u32[]{:S(2)}, u32[]{:S(2)}) collective-permute-start(bf16[528,768]{1,0:T(8,128)(2,1)S(1)} %get-tuple-element.13.own_x), channel_id=1, source_target_pairs={{0,1},{1,0},{2,3},{3,2},{4,5},{5,4},{6,7},{7,6},{8,9},{9,8},{10,11... | collective-permute-start | bytes 2433032 | tf_op jit(solution)/shard_map/ppermute | solution.py:397
  35.9 0.9 copy-start.9
  46.2 2.0 %copy-start = (bf16[4,2,192,384]{3,2,1,0:T(8,128)(2,1)}, bf16[4,2,192,384]{3,2,1,0:T(8,128)(2,1)S(1)}, u32[]{:S(2)}) copy-start(bf16[4,2,192,384]{3,2,1,0:T(8,128)(2,1)S(1)} %all-to-all-done) | copy-start | bytes 3538948
  48.2 22.3 %all-to-all-start.1 = ((bf16[32,48,128]{2,1,0:T(8,128)(2,1)}), bf16[32,48,128]{2,1,0:T(8,128)(2,1)S(1)}, u32[]{:S(2)}, u32[]{:S(2)}) async-start(bf16[32,48,128]{2,1,0:T(8,128)(2,1)} %shard_map.90), calls=%async_computation.1 | async-start | bytes 786432 | tf_op jit(solution)/shard_map/all_to_all | solution.py:438
  66.4 18.2 %copy-start.10 = (bf16[384,384]{1,0:T(8,128)(2,1)S(1)}, bf16[384,384]{1,0:T(8,128)(2,1)}, u32[]{:S(2)}) copy-start(bf16[384,384]{1,0:T(8,128)(2,1)} %get-tuple-element.21.own_w) | copy-start | bytes 884740
  66.4 20.8 %copy-start.2 = (f32[512,384]{1,0:T(8,128)S(1)}, f32[512,384]{1,0:T(8,128)}, u32[]{:S(2)}) copy-start(f32[512,384]{1,0:T(8,128)} %get-tuple-element.14.keep_ref) | copy-start | bytes 2359300
  66.4 20.8 %copy-start.4 = (s32[4]{0:T(128)S(1)}, s32[4]{0:T(128)}, u32[]{:S(2)}) copy-start(s32[4]{0:T(128)} %copy-done.3) | copy-start | bytes 52
  66.4 20.8 %copy-start.6 = (f32[384]{0:T(512)S(1)}, f32[384]{0:T(512)}, u32[]{:S(2)}) copy-start(f32[384]{0:T(512)} %gain_ref.3) | copy-start | bytes 4612
  66.5 20.8 %collective-permute-start.3 = (f32[512,384]{1,0:T(8,128)}, f32[512,384]{1,0:T(8,128)S(1)}, u32[]{:S(2)}, u32[]{:S(2)}) collective-permute-start(f32[512,384]{1,0:T(8,128)} %get-tuple-element.15), channel_id=1, source_target_pairs={{0,1},{1,0},{2,3},{3,2},{4,5},{5,4},{6,7},{7,6},{8,9},{9,8},{10,11... | collective-permute-start | bytes 2359304 | tf_op jit(solution)/shard_map/ppermute | solution.py:397
  74.3 21.9 %all-to-all-start.2 = ((bf16[64,16,128]{2,1,0:T(8,128)(2,1)}), bf16[64,16,128]{2,1,0:T(8,128)(2,1)S(1)}, u32[]{:S(2)}, u32[]{:S(2)}) async-start(bf16[64,16,128]{2,1,0:T(8,128)(2,1)} %bitcast.6), calls=%async_computation.2 | async-start | bytes 524288 | tf_op jit(solution)/shard_map/all_to_all | solution.py:445
  84.7 4.7 %collective-permute-start.4 = (bf16[384,384]{1,0:T(8,128)(2,1)S(1)}, bf16[384,384]{1,0:T(8,128)(2,1)S(1)}, u32[]{:S(2)}, u32[]{:S(2)}) collective-permute-start(bf16[384,384]{1,0:T(8,128)(2,1)S(1)} %copy-done.10), channel_id=1, source_target_pairs={{0,1},{1,0},{2,3},{3,2},{4,5},{5,4},{6,7},{7,6},{8,9},{9,8},{10,11... | collective-permute-start | bytes 884744 | tf_op jit(solution)/shard_map/ppermute | solution.py:397
  88.7 0.7 copy-start.13
  89.4 0.7 copy-start.11
  96.2 1.0 copy-start.12
  97.2 0.9 copy-start.14

commit v6 on v5

--- a/solution.py
+++ b/solution.py
@@ -18,7 +18,7 @@
 POS = 32
 DP_X, DP_Y = 4, 2
 INTERPRET = False
-NEAR_TILE = 256
+NEAR_TILE = 512
 LIMITS = [24 << 20, 60 * 1024 * 1024, 24 << 20, 24 << 20, 24 << 20]
 
 eps_norm = 1e-05
@@ -230,8 +230,12 @@
         result = jnp.where(
             out_lane < HEAD_DIM, summed / swap_halves(summed), row_max * SCALE + jnp.log(summed)
         )
-        out_ref = keep_ref if at < TOK else give_ref
-        out_ref[at % TOK : at % TOK + tile, :] = result
+        if tile == SEG:
+            keep_ref[...] = result[:TOK]
+            give_ref[...] = result[TOK:]
+        else:
+            out_ref = keep_ref if at < TOK else give_ref
+            out_ref[at % TOK : at % TOK + tile, :] = result
 
 
 def near_level(base, own_x, other_x, packed):
@@ -266,25 +270,28 @@
     source = lax.broadcasted_iota(jnp.int32, (POS, POS * 16), 0)
     member = jnp.right_shift(lax.broadcasted_iota(jnp.int32, (POS, POS * 16), 1), 4)
     spread = jnp.where(source == member, 1.0, 0.0).astype(BF16)
+    queries = jnp.concatenate(
+        [jnp.where(q_lane < HEAD_DIM, part, 0.0) for part in (wide, swap_halves(wide))], axis=0
+    ).astype(BF16)
+    scores = lax.dot_general(queries, keys, (((1,), (1,)), ((), ())), preferred_element_type=F32)
+    row_max = jnp.max(scores, axis=1, keepdims=True)
+    weights = jnp.exp2((scores - row_max) * EXP_SCALE).astype(BF16)
+    summed = jnp.dot(weights, values, preferred_element_type=F32)
+    swapped = swap_halves(summed)
+    outs = summed / swapped
+    logs = row_max * SCALE + jnp.log(swapped)
     for part in range(2):
-        queries = jnp.where(q_lane < HEAD_DIM, wide if part == 0 else swap_halves(wide), 0.0)
-        scores = lax.dot_general(
-            queries.astype(BF16), keys, (((1,), (1,)), ((), ())), preferred_element_type=F32
-        )
-        row_max = jnp.max(scores, axis=1, keepdims=True)
-        weights = jnp.exp2((scores - row_max) * EXP_SCALE).astype(BF16)
-        summed = jnp.dot(weights, values, preferred_element_type=F32)
-        swapped = swap_halves(summed)
-        out = (summed / swapped).reshape(POS, 16, 128)
+        rows = slice(part * POS * 16, (part + 1) * POS * 16)
+        out = outs[rows].reshape(POS, 16, 128)
         packed = jnp.concatenate([out[:, 0:8, :HEAD_DIM], out[:, 8:16, :HEAD_DIM]], axis=2)
-        high, middle, low = parts3(row_max * SCALE + jnp.log(swapped))
+        high, middle, low = parts3(logs[rows])
         stats = jnp.where(
             place == 0, high, jnp.where(place == 1, middle, jnp.where(place == 2, low, 0.0))
         )
         stats = jnp.where(mine, stats, 0.0).astype(BF16)
-        rows = jnp.dot(spread, stats, preferred_element_type=F32)
-        rows = jnp.broadcast_to(rows[:, None, :], (POS, 8, 128))
-        block = jnp.concatenate([packed, rows], axis=1).astype(BF16)
+        means = jnp.dot(spread, stats, preferred_element_type=F32)
+        means = jnp.broadcast_to(means[:, None, :], (POS, 8, 128))
+        block = jnp.concatenate([packed, means], axis=1).astype(BF16)
         back_ref[:, pl.ds(core if part == 0 else 1 - core, 1)] = block[:, None]
 
 

time: 103 us -> 101 us (0.981)
  Pallas kernels: 28.1 us -> 26.9 us
  transfers between devices with their start and end apart: 8 -> 8, of which waited for: 3 -> 3; matrix products, arithmetic and copies ran while one was open for 0% -> 0% of each run, Pallas kernels for 20% -> 19%
where the time goes in v6:
time: 101 us
  starting transfers between devices  50 us (50%)
  Pallas kernels  26.9 us (27%)
  waiting for transfers between devices  17.9 us (18%)
  local copies, waits for them, and re-layouts  4.87 us (5%)
    ppermute x1, starting transfers between devices, layer(): lax.ppermute(flip_perm, ctx, [(last - r, r) for r in range(2 * POS)])  11.9 us
    pallas_call x1, Pallas kernels, near_level(): pl.pallas_call(near_kernel, out_shape=[half, half, shape_of(INNER, INNER)...  10.7 us
    all_to_all x1, starting transfers between devices, layer(): far = lax.all_to_all(back.reshape(2 * POS, 16, 128), ctx, 0, 0, tiled=True)  10.4 us
    all_to_all x1, waiting for transfers between devices, gather_weights(): got = lax.all_to_all(both, 'x', 0, 0, tiled=True)  9.39 us
    ppermute x3, starting transfers between devices, core_swap(): return lax.ppermute(block, 'core', [(0, 1), (1, 0)])  8.35 us
    ppermute x1, starting transfers between devices, gather_weights(): other = lax.ppermute(packed, 'yh', [(0, 1), (1, 0)])  8.26 us
    all_to_all x1, starting transfers between devices, layer(): got = lax.all_to_all(send, 'pos', 0, 0, tiled=True)  6.97 us
    all_to_all x1, waiting for transfers between devices, layer(): far = lax.all_to_all(back.reshape(2 * POS, 16, 128), ctx, 0, 0, tiled=True)  6.22 us
  transfers between devices with their start and end apart: 8, of which 3 were waited for; matrix products, arithmetic and copies ran while one was open for 0% of the time, Pallas kernels for 19%

profile of v6, /device:TPU:1, one launch (start us, length us, event | category | flops | bytes accessed | tf_op | source)
XLA Modules:
  0.0 100.6 jit_solution(4920935821379940419)
XLA Ops:
  0.6 1.8 %shard_map.88.own_ref = bf16[192,384]{1,0:T(8,128)(2,1)} custom-call(s32[1]{0:T(128)} %bitcast.core_ref, bf16[96,1152]{1,0:T(8,128)(2,1)} %proj_ref.1, bf16[48,768]{1,0:T(8,128)(2,1)} %outw_ref.1), custom_call_target="tpu_custom_call" | custom-call | tf_op jit(solution)/shard_map/pallas_call | solution.py:84
  2.4 8.3 %collective-permute-start.2 = (bf16[192,384]{1,0:T(8,128)(2,1)}, bf16[192,384]{1,0:T(8,128)(2,1)S(1)}, u32[]{:S(2)}, u32[]{:S(2)}) collective-permute-start(bf16[192,384]{1,0:T(8,128)(2,1)} %shard_map.88.own_ref), channel_id=1, source_target_pairs={{0,64},{64,0},{1,65},{65,1},{2,66},{66,2},{3,67},{67,3},{4,68},{68... | collective-permute-start | bytes 442376 | tf_op jit(solution)/shard_map/ppermute | solution.py:97
  10.7 11.9 %collective-permute-start = (s32[1,512]{1,0:T(1,128)}, s32[1,512]{1,0:T(1,128)S(1)}, u32[]{:S(2)}, u32[]{:S(2)}) collective-permute-start(s32[1,512]{1,0:T(1,128)} %param.8), channel_id=1, source_target_pairs={{63,0},{62,1},{61,2},{60,3},{59,4},{58,5},{57,6},{56,7},{55,8},{54... | collective-permute-start | bytes 6152 | tf_op jit(solution)/shard_map/ppermute | solution.py:418
  22.5 0.0 collective-permute-done.2.other_ref
  22.5 0.0 copy-start.15
  22.6 0.7 copy-done.15
  23.2 2.1 %shard_map.89 = bf16[4,2,192,384]{3,2,1,0:T(8,128)(2,1)} custom-call(bf16[192,384]{1,0:T(8,128)(2,1)} %shard_map.88.own_ref, bf16[192,384]{1,0:T(8,128)(2,1)} %copy-done.15), custom_call_target="tpu_custom_call" | custom-call | tf_op jit(solution)/shard_map/pallas_call | solution.py:98
  25.3 0.0 copy-start.1
  25.3 4.1 %all-to-all-start = ((bf16[4,2,192,384]{3,2,1,0:T(8,128)(2,1)}), bf16[4,2,192,384]{3,2,1,0:T(8,128)(2,1)S(1)}, u32[]{:S(2)}, u32[]{:S(2)}) async-start(bf16[4,2,192,384]{3,2,1,0:T(8,128)(2,1)} %shard_map.89), calls=%async_computation | async-start | bytes 2359296 | tf_op jit(solution)/shard_map/all_to_all | solution.py:101
  29.5 0.1 pad_add_fusion.base_ref
  29.5 0.0 collective-permute-done.perm_ref
  29.6 0.0 copy-done.1
  29.6 0.0 copy-done.5
  29.6 1.1 %shard_map.86 = (bf16[528,768]{1,0:T(8,128)(2,1)S(1)}, f32[1,512]{1,0:T(1,128)S(1)}) custom-call(s32[4]{0:T(128)S(1)} %pad_add_fusion.base_ref, bf16[512,768]{1,0:T(8,128)(2,1)S(1)} %bitcast.11, f32[768]{0:T(1024)S(1)} %copy-done.5, s32[1,512]{1,0:T(1,128)S(1)} %collective-permute-done.perm_ref), custom_call_target="tpu_custom_call" | custom-call | bytes 2097152 | tf_op jit(solution)/shard_map/pallas_call | solution.py:420
  30.6 0.0 copy-start.8
  30.6 1.9 %collective-permute-start.1 = (bf16[528,768]{1,0:T(8,128)(2,1)S(1)}, bf16[528,768]{1,0:T(8,128)(2,1)S(1)}, u32[]{:S(2)}, u32[]{:S(2)}) collective-permute-start(bf16[528,768]{1,0:T(8,128)(2,1)S(1)} %get-tuple-element.13.own_x), channel_id=1, source_target_pairs={{0,1},{1,0},{2,3},{3,2},{4,5},{5,4},{6,7},{7,6},{8,9},{9,8},{10,11... | collective-permute-start | bytes 2433032 | tf_op jit(solution)/shard_map/ppermute | solution.py:404
  32.6 2.3 %collective-permute-done.1.other_x = bf16[528,768]{1,0:T(8,128)(2,1)S(1)} collective-permute-done((bf16[528,768]{1,0:T(8,128)(2,1)S(1)}, bf16[528,768]{1,0:T(8,128)(2,1)S(1)}, u32[]{:S(2)}, u32[]{:S(2)}) %collective-permute-start.1) | collective-permute-done | bytes 811040 | tf_op jit(solution)/shard_map/ppermute | solution.py:404
  34.9 0.0 copy-done.7
  34.9 1.1 %shard_map.87.picked_ref = bf16[384,768]{1,0:T(8,128)(2,1)S(1)} custom-call(s32[4]{0:T(128)S(1)} %pad_add_fusion.base_ref, s32[6]{0:T(128)S(1)} %copy-done.7, bf16[528,768]{1,0:T(8,128)(2,1)S(1)} %get-tuple-element.13.own_x, bf16[528,768]{1,0:T(8,128)(2,1)S(1)} %collective-permute-done.1.other_x), custom_call_target="tpu_custom_call" | custom-call | flops 603979776 | bytes 3145728 | tf_op jit(solution)/shard_map/pallas_call | solution.py:428
  35.9 0.0 copy-start.9
  36.0 0.9 copy-done.9
  36.8 9.4 %all-to-all-done = bf16[4,2,192,384]{3,2,1,0:T(8,128)(2,1)S(1)} async-done(((bf16[4,2,192,384]{3,2,1,0:T(8,128)(2,1)}), bf16[4,2,192,384]{3,2,1,0:T(8,128)(2,1)S(1)}, u32[]{:S(2)}, u32[]{:S(2)}) %all-to-all-start) | async-done | bytes 1179680 | tf_op jit(solution)/shard_map/all_to_all | solution.py:101
  46.2 0.0 copy-done.3
  46.2 2.0 %shard_map.90 = bf16[32,48,128]{2,1,0:T(8,128)(2,1)} custom-call(s32[4]{0:T(128)S(1)} %pad_add_fusion.base_ref, bf16[384,768]{1,0:T(8,128)(2,1)S(1)} %shard_map.87.picked_ref, bf16[8,192,384]{2,1,0:T(8,128)(2,1)S(1)} %bitcast.9), custom_call_target="tpu_custom_call" | custom-call | flops 150994944 | bytes 2097152 | tf_op jit(solution)/shard_map/pallas_call | solution.py:435
  48.2 0.0 copy-done.8
  48.2 0.0 copy-done
  48.2 7.0 %all-to-all-start.1 = ((bf16[32,48,128]{2,1,0:T(8,128)(2,1)}), bf16[32,48,128]{2,1,0:T(8,128)(2,1)S(1)}, u32[]{:S(2)}, u32[]{:S(2)}) async-start(bf16[32,48,128]{2,1,0:T(8,128)(2,1)} %shard_map.90), calls=%async_computation.1 | async-start | bytes 786432 | tf_op jit(solution)/shard_map/all_to_all | solution.py:445
  55.2 10.7 %shard_map.92 = (f32[512,384]{1,0:T(8,128)}, f32[512,384]{1,0:T(8,128)}, bf16[384,384]{1,0:T(8,128)(2,1)}) custom-call(s32[4]{0:T(128)} %copy-done.3, bf16[528,768]{1,0:T(8,128)(2,1)} %copy-done.8, bf16[528,768]{1,0:T(8,128)(2,1)} %copy-done.9, bf16[8,192,384]{2,1,0:T(8,128)(2,1)} %bitcast.10), custom_call_target="tpu_custom_call" | custom-call | flops 1610612736 | bytes 5242880 | tf_op jit(solution)/shard_map/pallas_call | solution.py:245
  65.9 0.0 copy-start.6
  65.9 4.1 %collective-permute-start.3 = (f32[512,384]{1,0:T(8,128)}, f32[512,384]{1,0:T(8,128)S(1)}, u32[]{:S(2)}, u32[]{:S(2)}) collective-permute-start(f32[512,384]{1,0:T(8,128)} %get-tuple-element.15), channel_id=1, source_target_pairs={{0,1},{1,0},{2,3},{3,2},{4,5},{5,4},{6,7},{7,6},{8,9},{9,8},{10,11... | collective-permute-start | bytes 2359304 | tf_op jit(solution)/shard_map/ppermute | solution.py:404
  70.0 0.0 all-to-all-done.1.got_ref
  70.0 3.0 %shard_map.91 = bf16[32,2,16,128]{3,2,1,0:T(8,128)(2,1)} custom-call(s32[1]{0:T(128)} %bitcast.core_ref, bf16[32,48,128]{2,1,0:T(8,128)(2,1)S(1)} %all-to-all-done.1.got_ref), custom_call_target="tpu_custom_call" | custom-call | flops 536870912 | bytes 1048576 | tf_op jit(solution)/shard_map/pallas_call | solution.py:448
  73.0 10.4 %all-to-all-start.2 = ((bf16[64,16,128]{2,1,0:T(8,128)(2,1)}), bf16[64,16,128]{2,1,0:T(8,128)(2,1)S(1)}, u32[]{:S(2)}, u32[]{:S(2)}) async-start(bf16[64,16,128]{2,1,0:T(8,128)(2,1)} %bitcast.6), calls=%async_computation.2 | async-start | bytes 524288 | tf_op jit(solution)/shard_map/all_to_all | solution.py:452
  83.4 0.0 copy-done.10
  83.5 2.4 %collective-permute-start.4 = (bf16[384,384]{1,0:T(8,128)(2,1)S(1)}, bf16[384,384]{1,0:T(8,128)(2,1)S(1)}, u32[]{:S(2)}, u32[]{:S(2)}) collective-permute-start(bf16[384,384]{1,0:T(8,128)(2,1)S(1)} %copy-done.10), channel_id=1, source_target_pairs={{0,1},{1,0},{2,3},{3,2},{4,5},{5,4},{6,7},{7,6},{8,9},{9,8},{10,11... | collective-permute-start | bytes 884744 | tf_op jit(solution)/shard_map/ppermute | solution.py:404
  85.8 0.0 collective-permute-done.3.got_ref
  85.8 0.0 copy-done.2
  85.8 0.0 copy-done.4
  85.9 0.0 copy-done.6
  85.9 1.5 %shard_map.93 = (f32[512,384]{1,0:T(8,128)S(1)}, f32[384,128]{1,0:T(8,128)S(1)}, bf16[512,384]{1,0:T(8,128)(2,1)S(1)}, f32[1,384]{1,0:T(1,128)S(1)}) custom-call(s32[4]{0:T(128)S(1)} %copy-done.4, s32[6]{0:T(128)S(1)} %copy-done.7, f32[512,384]{1,0:T(8,128)S(1)} %copy-done.2, f32[512,384]{1,0:T(8,128)S(1)} %collective-permute-done.3.got_ref, ...), custom_call_target="tpu_custom_call" | custom-call | flops 268435456 | bytes 4194304 | tf_op jit(solution)/shard_map/pallas_call | solution.py:455
  87.3 0.0 copy-start.13
  87.3 0.7 copy-done.13
  88.0 0.0 collective-permute-done.4.other_w
  88.0 0.7 copy-done.11
  88.7 6.2 %all-to-all-done.2.far_ref = bf16[64,16,128]{2,1,0:T(8,128)(2,1)S(1)} async-done(((bf16[64,16,128]{2,1,0:T(8,128)(2,1)}), bf16[64,16,128]{2,1,0:T(8,128)(2,1)S(1)}, u32[]{:S(2)}, u32[]{:S(2)}) %all-to-all-start.2) | async-done | bytes 262176 | tf_op jit(solution)/shard_map/all_to_all | solution.py:452
  95.0 1.0 copy-done.12
  95.9 0.9 copy-done.14
  96.8 3.7 %shard_map.94 = (bf16[512,768]{1,0:T(8,128)(2,1)}, bf16[512,768]{1,0:T(8,128)(2,1)}) custom-call(s32[1]{0:T(128)} %bitcast.core_ref, bf16[64,16,128]{2,1,0:T(8,128)(2,1)S(1)} %all-to-all-done.2.far_ref, f32[512,384]{1,0:T(8,128)S(1)} %get-tuple-element.17.dense_ref, f32[384,128]{1,0:T(8,128)S(1)} %copy-done.14, ...), custom_call_target="tpu_custom_call" | custom-call | flops 1207959552 | bytes 4194304 | tf_op jit(solution)/shard_map/pallas_call | solution.py:469
  (10 shorter events, 0.0 us)
Async XLA Ops:
  2.4 20.1 %collective-permute-start.2 = (bf16[192,384]{1,0:T(8,128)(2,1)}, bf16[192,384]{1,0:T(8,128)(2,1)S(1)}, u32[]{:S(2)}, u32[]{:S(2)}) collective-permute-start(bf16[192,384]{1,0:T(8,128)(2,1)} %shard_map.88.own_ref), channel_id=1, source_target_pairs={{0,64},{64,0},{1,65},{65,1},{2,66},{66,2},{3,67},{67,3},{4,68},{68... | collective-permute-start | bytes 442376 | tf_op jit(solution)/shard_map/ppermute | solution.py:97
  10.7 18.9 %collective-permute-start = (s32[1,512]{1,0:T(1,128)}, s32[1,512]{1,0:T(1,128)S(1)}, u32[]{:S(2)}, u32[]{:S(2)}) collective-permute-start(s32[1,512]{1,0:T(1,128)} %param.8), channel_id=1, source_target_pairs={{63,0},{62,1},{61,2},{60,3},{59,4},{58,5},{57,6},{56,7},{55,8},{54... | collective-permute-start | bytes 6152 | tf_op jit(solution)/shard_map/ppermute | solution.py:418
  22.5 0.7 copy-start.15
  25.3 4.2 %copy-start.1 = (bf16[1,512,768]{2,1,0:T(8,128)(2,1)S(1)}, bf16[1,512,768]{2,1,0:T(8,128)(2,1)}, u32[]{:S(2)}) copy-start(bf16[1,512,768]{2,1,0:T(8,128)(2,1)} %param.7) | copy-start | bytes 2359300
  25.3 4.2 %copy-start.5 = (f32[768]{0:T(1024)S(1)}, f32[768]{0:T(1024)}, u32[]{:S(2)}) copy-start(f32[768]{0:T(1024)} %gain_ref.2) | copy-start | bytes 9220
  25.3 9.5 %copy-start.7 = (s32[6]{0:T(128)S(1)}, s32[6]{0:T(128)}, u32[]{:S(2)}) copy-start(s32[6]{0:T(128)} %offset_ref.3) | copy-start | bytes 76
  25.3 20.9 %all-to-all-start = ((bf16[4,2,192,384]{3,2,1,0:T(8,128)(2,1)}), bf16[4,2,192,384]{3,2,1,0:T(8,128)(2,1)S(1)}, u32[]{:S(2)}, u32[]{:S(2)}) async-start(bf16[4,2,192,384]{3,2,1,0:T(8,128)(2,1)} %shard_map.89), calls=%async_computation | async-start | bytes 2359296 | tf_op jit(solution)/shard_map/all_to_all | solution.py:101
  29.5 16.7 %copy-start.3 = (s32[4]{0:T(128)}, s32[4]{0:T(128)S(1)}, u32[]{:S(2)}) copy-start(s32[4]{0:T(128)S(1)} %pad_add_fusion.base_ref) | copy-start | bytes 52
  30.6 17.6 %copy-start.8 = (bf16[528,768]{1,0:T(8,128)(2,1)}, bf16[528,768]{1,0:T(8,128)(2,1)S(1)}, u32[]{:S(2)}) copy-start(bf16[528,768]{1,0:T(8,128)(2,1)S(1)} %get-tuple-element.13.own_x) | copy-start | bytes 2433028
  30.6 4.2 %collective-permute-start.1 = (bf16[528,768]{1,0:T(8,128)(2,1)S(1)}, bf16[528,768]{1,0:T(8,128)(2,1)S(1)}, u32[]{:S(2)}, u32[]{:S(2)}) collective-permute-start(bf16[528,768]{1,0:T(8,128)(2,1)S(1)} %get-tuple-element.13.own_x), channel_id=1, source_target_pairs={{0,1},{1,0},{2,3},{3,2},{4,5},{5,4},{6,7},{7,6},{8,9},{9,8},{10,11... | collective-permute-start | bytes 2433032 | tf_op jit(solution)/shard_map/ppermute | solution.py:404
  35.9 0.9 copy-start.9
  46.2 2.0 %copy-start = (bf16[4,2,192,384]{3,2,1,0:T(8,128)(2,1)}, bf16[4,2,192,384]{3,2,1,0:T(8,128)(2,1)S(1)}, u32[]{:S(2)}) copy-start(bf16[4,2,192,384]{3,2,1,0:T(8,128)(2,1)S(1)} %all-to-all-done) | copy-start | bytes 3538948
  48.2 21.8 %all-to-all-start.1 = ((bf16[32,48,128]{2,1,0:T(8,128)(2,1)}), bf16[32,48,128]{2,1,0:T(8,128)(2,1)S(1)}, u32[]{:S(2)}, u32[]{:S(2)}) async-start(bf16[32,48,128]{2,1,0:T(8,128)(2,1)} %shard_map.90), calls=%async_computation.1 | async-start | bytes 786432 | tf_op jit(solution)/shard_map/all_to_all | solution.py:445
  65.9 17.5 %copy-start.10 = (bf16[384,384]{1,0:T(8,128)(2,1)S(1)}, bf16[384,384]{1,0:T(8,128)(2,1)}, u32[]{:S(2)}) copy-start(bf16[384,384]{1,0:T(8,128)(2,1)} %get-tuple-element.21.own_w) | copy-start | bytes 884740
  65.9 19.9 %copy-start.2 = (f32[512,384]{1,0:T(8,128)S(1)}, f32[512,384]{1,0:T(8,128)}, u32[]{:S(2)}) copy-start(f32[512,384]{1,0:T(8,128)} %get-tuple-element.14.keep_ref) | copy-start | bytes 2359300
  65.9 19.9 %copy-start.4 = (s32[4]{0:T(128)S(1)}, s32[4]{0:T(128)}, u32[]{:S(2)}) copy-start(s32[4]{0:T(128)} %copy-done.3) | copy-start | bytes 52
  65.9 19.9 %copy-start.6 = (f32[384]{0:T(512)S(1)}, f32[384]{0:T(512)}, u32[]{:S(2)}) copy-start(f32[384]{0:T(512)} %gain_ref.3) | copy-start | bytes 4612
  65.9 19.9 %collective-permute-start.3 = (f32[512,384]{1,0:T(8,128)}, f32[512,384]{1,0:T(8,128)S(1)}, u32[]{:S(2)}, u32[]{:S(2)}) collective-permute-start(f32[512,384]{1,0:T(8,128)} %get-tuple-element.15), channel_id=1, source_target_pairs={{0,1},{1,0},{2,3},{3,2},{4,5},{5,4},{6,7},{7,6},{8,9},{9,8},{10,11... | collective-permute-start | bytes 2359304 | tf_op jit(solution)/shard_map/ppermute | solution.py:404
  73.0 21.9 %all-to-all-start.2 = ((bf16[64,16,128]{2,1,0:T(8,128)(2,1)}), bf16[64,16,128]{2,1,0:T(8,128)(2,1)S(1)}, u32[]{:S(2)}, u32[]{:S(2)}) async-start(bf16[64,16,128]{2,1,0:T(8,128)(2,1)} %bitcast.6), calls=%async_computation.2 | async-start | bytes 524288 | tf_op jit(solution)/shard_map/all_to_all | solution.py:452
  83.5 4.6 %collective-permute-start.4 = (bf16[384,384]{1,0:T(8,128)(2,1)S(1)}, bf16[384,384]{1,0:T(8,128)(2,1)S(1)}, u32[]{:S(2)}, u32[]{:S(2)}) collective-permute-start(bf16[384,384]{1,0:T(8,128)(2,1)S(1)} %copy-done.10), channel_id=1, source_target_pairs={{0,1},{1,0},{2,3},{3,2},{4,5},{5,4},{6,7},{7,6},{8,9},{9,8},{10,11... | collective-permute-start | bytes 884744 | tf_op jit(solution)/shard_map/ppermute | solution.py:404
  87.3 0.7 copy-start.13
  88.0 0.7 copy-start.11
  95.0 1.0 copy-start.12
  95.9 0.9 copy-start.14

commit v7 on v6

--- a/solution.py
+++ b/solution.py
@@ -81,23 +81,33 @@
 
 
 def pack_weights(core, projection, output_weight):
-    return call(pack_kernel, shape_of(192, INNER), [SMEM, VMEM, VMEM], limit=60 * 1024 * 1024)(
+    return call(pack_kernel, shape_of(192, INNER), [SMEM, VMEM, VMEM])(
         core, projection, output_weight
     )
 
 
-def fan_kernel(own_ref, other_ref, both_ref):
+def fan_kernel(own_ref, other_ref, both_ref, sems):
+    copies = []
     for peer in range(DP_X):
-        both_ref[peer, 0] = own_ref[...]
-        both_ref[peer, 1] = other_ref[...]
+        for at, part in enumerate((own_ref, other_ref)):
+            copies.append(
+                pltpu.make_async_copy(part, both_ref.at[peer, at], sems.at[peer * 2 + at])
+            )
+            copies[-1].start()
+    for copy in copies:
+        copy.wait()
 
 
 def gather_weights(core, projection, output_weight):
     packed = pack_weights(core, projection, output_weight)
     other = lax.ppermute(packed, "yh", [(0, 1), (1, 0)])
-    both = call(fan_kernel, shape_of(DP_X, DP_Y, 192, INNER), [VMEM, VMEM], limit=60 * 1024 * 1024)(
-        packed, other
-    )
+    both = call(
+        fan_kernel,
+        shape_of(DP_X, DP_Y, 192, INNER),
+        [VMEM, VMEM],
+        [pltpu.SemaphoreType.DMA((2 * DP_X,))],
+        outs=ANY,
+    )(packed, other)
     got = lax.all_to_all(both, "x", 0, 0, tiled=True)
     return got.reshape(DP_X * DP_Y, 192, INNER)
 

time: 101 us -> 99.6 us (0.986)
  Pallas kernels: 26.9 us -> 24.1 us
  local copies, waits for them, and re-layouts: 4.87 us -> 6.03 us
    pallas_call x2, Pallas kernels: 3.87 us -> 1.19 us  [the longest x1 1.09 us: gather_weights(): call(fan_kernel, shape_of(DP_X, DP_Y, 192, INNER), [VMEM, VMEM], [pltpu.S...]
    unnamed x32 -> x34, local copies, waits for them, and re-layouts: 4.87 us -> 6.03 us
where the time goes in v7:
time: 99.6 us; the launch traced here: 98.9 us
  starting transfers between devices  49.8 us (50%)
  Pallas kernels  24.1 us (24%)
  waiting for transfers between devices  18 us (18%)
  local copies, waits for them, and re-layouts  6.03 us (6%)
    ppermute x1, starting transfers between devices, layer(): lax.ppermute(flip_perm, ctx, [(last - r, r) for r in range(2 * POS)])  11.9 us
    pallas_call x1, Pallas kernels, near_level(): pl.pallas_call(near_kernel, out_shape=[half, half, shape_of(INNER, INNER)...  10.7 us
    all_to_all x1, starting transfers between devices, layer(): far = lax.all_to_all(back.reshape(2 * POS, 16, 128), ctx, 0, 0, tiled=True)  10.4 us
    all_to_all x1, waiting for transfers between devices, gather_weights(): got = lax.all_to_all(both, 'x', 0, 0, tiled=True)  9.39 us
    ppermute x3, starting transfers between devices, core_swap(): return lax.ppermute(block, 'core', [(0, 1), (1, 0)])  8.37 us
    ppermute x1, starting transfers between devices, gather_weights(): other = lax.ppermute(packed, 'yh', [(0, 1), (1, 0)])  8.27 us
    all_to_all x1, starting transfers between devices, layer(): got = lax.all_to_all(send, 'pos', 0, 0, tiled=True)  6.76 us
    all_to_all x1, waiting for transfers between devices, layer(): far = lax.all_to_all(back.reshape(2 * POS, 16, 128), ctx, 0, 0, tiled=True)  6.29 us
  transfers between devices with their start and end apart: 8, of which 3 were waited for; matrix products, arithmetic and copies ran while one was open for 0% of the time, Pallas kernels for 19%

profile of v7, /device:TPU:1, one launch (start us, length us, event | category | flops | bytes accessed | tf_op | source)
XLA Modules:
  0.0 98.9 jit_solution(16224562311773827449)
XLA Ops:
  0.6 0.0 copy-start.3
  0.6 0.9 copy-done.3
  1.6 0.9 copy-done.4
  2.5 0.1 shard_map.88.own_ref
  2.6 8.3 %collective-permute-start.2 = (bf16[192,384]{1,0:T(8,128)(2,1)S(1)}, bf16[192,384]{1,0:T(8,128)(2,1)S(1)}, u32[]{:S(2)}, u32[]{:S(2)}) collective-permute-start(bf16[192,384]{1,0:T(8,128)(2,1)S(1)} %shard_map.88.own_ref), channel_id=1, source_target_pairs={{0,64},{64,0},{1,65},{65,1},{2,66},{66,2},{3,67},{67,3},{4,68},{68... | collective-permute-start | bytes 442376 | tf_op jit(solution)/shard_map/ppermute | solution.py:103
  10.8 11.9 %collective-permute-start = (s32[1,512]{1,0:T(1,128)}, s32[1,512]{1,0:T(1,128)S(1)}, u32[]{:S(2)}, u32[]{:S(2)}) collective-permute-start(s32[1,512]{1,0:T(1,128)} %param.8), channel_id=1, source_target_pairs={{63,0},{62,1},{61,2},{60,3},{59,4},{58,5},{57,6},{56,7},{55,8},{54... | collective-permute-start | bytes 6152 | tf_op jit(solution)/shard_map/ppermute | solution.py:428
  22.7 0.0 collective-permute-done.2.other_ref
  22.7 1.1 %shard_map.89 = bf16[4,2,192,384]{3,2,1,0:T(8,128)(2,1)} custom-call(bf16[192,384]{1,0:T(8,128)(2,1)S(1)} %shard_map.88.own_ref, bf16[192,384]{1,0:T(8,128)(2,1)S(1)} %collective-permute-done.2.other_ref), custom_call_target="tpu_custom_call" | custom-call | tf_op jit(solution)/shard_map/pallas_call | solution.py:104
  23.8 0.0 copy-start.1
  23.8 0.0 copy-start.7
  23.9 0.0 copy-start.9
  23.9 4.2 %all-to-all-start = ((bf16[4,2,192,384]{3,2,1,0:T(8,128)(2,1)}), bf16[4,2,192,384]{3,2,1,0:T(8,128)(2,1)S(1)}, u32[]{:S(2)}, u32[]{:S(2)}) async-start(bf16[4,2,192,384]{3,2,1,0:T(8,128)(2,1)} %shard_map.89), calls=%async_computation | async-start | bytes 2359296 | tf_op jit(solution)/shard_map/all_to_all | solution.py:111
  28.0 0.1 pad_add_fusion.base_ref
  28.1 0.0 collective-permute-done.perm_ref
  28.1 0.0 copy-done.1
  28.1 0.0 copy-done.7
  28.1 1.1 %shard_map.86 = (bf16[528,768]{1,0:T(8,128)(2,1)S(1)}, f32[1,512]{1,0:T(1,128)S(1)}) custom-call(s32[4]{0:T(128)S(1)} %pad_add_fusion.base_ref, bf16[512,768]{1,0:T(8,128)(2,1)S(1)} %bitcast.11, f32[768]{0:T(1024)S(1)} %copy-done.7, s32[1,512]{1,0:T(1,128)S(1)} %collective-permute-done.perm_ref), custom_call_target="tpu_custom_call" | custom-call | bytes 2097152 | tf_op jit(solution)/shard_map/pallas_call | solution.py:430
  29.2 0.0 copy-start.10
  29.2 1.9 %collective-permute-start.1 = (bf16[528,768]{1,0:T(8,128)(2,1)S(1)}, bf16[528,768]{1,0:T(8,128)(2,1)S(1)}, u32[]{:S(2)}, u32[]{:S(2)}) collective-permute-start(bf16[528,768]{1,0:T(8,128)(2,1)S(1)} %get-tuple-element.13.own_x), channel_id=1, source_target_pairs={{0,1},{1,0},{2,3},{3,2},{4,5},{5,4},{6,7},{7,6},{8,9},{9,8},{10,11... | collective-permute-start | bytes 2433032 | tf_op jit(solution)/shard_map/ppermute | solution.py:414
  31.1 2.3 %collective-permute-done.1.other_x = bf16[528,768]{1,0:T(8,128)(2,1)S(1)} collective-permute-done((bf16[528,768]{1,0:T(8,128)(2,1)S(1)}, bf16[528,768]{1,0:T(8,128)(2,1)S(1)}, u32[]{:S(2)}, u32[]{:S(2)}) %collective-permute-start.1) | collective-permute-done | bytes 811040 | tf_op jit(solution)/shard_map/ppermute | solution.py:414
  33.4 0.0 copy-done.9
  33.4 1.1 %shard_map.87.picked_ref = bf16[384,768]{1,0:T(8,128)(2,1)S(1)} custom-call(s32[4]{0:T(128)S(1)} %pad_add_fusion.base_ref, s32[6]{0:T(128)S(1)} %copy-done.9, bf16[528,768]{1,0:T(8,128)(2,1)S(1)} %get-tuple-element.13.own_x, bf16[528,768]{1,0:T(8,128)(2,1)S(1)} %collective-permute-done.1.other_x), custom_call_target="tpu_custom_call" | custom-call | flops 603979776 | bytes 3145728 | tf_op jit(solution)/shard_map/pallas_call | solution.py:438
  34.5 0.0 copy-start.11
  34.5 0.9 copy-done.11
  35.4 9.4 %all-to-all-done = bf16[4,2,192,384]{3,2,1,0:T(8,128)(2,1)S(1)} async-done(((bf16[4,2,192,384]{3,2,1,0:T(8,128)(2,1)}), bf16[4,2,192,384]{3,2,1,0:T(8,128)(2,1)S(1)}, u32[]{:S(2)}, u32[]{:S(2)}) %all-to-all-start) | async-done | bytes 1179680 | tf_op jit(solution)/shard_map/all_to_all | solution.py:111
  44.8 0.0 copy-done.5
  44.8 2.0 %shard_map.90 = bf16[32,48,128]{2,1,0:T(8,128)(2,1)} custom-call(s32[4]{0:T(128)S(1)} %pad_add_fusion.base_ref, bf16[384,768]{1,0:T(8,128)(2,1)S(1)} %shard_map.87.picked_ref, bf16[8,192,384]{2,1,0:T(8,128)(2,1)S(1)} %bitcast.9), custom_call_target="tpu_custom_call" | custom-call | flops 150994944 | bytes 2097152 | tf_op jit(solution)/shard_map/pallas_call | solution.py:445
  46.8 0.0 copy-done.10
  46.8 0.0 copy-done
  46.8 6.8 %all-to-all-start.1 = ((bf16[32,48,128]{2,1,0:T(8,128)(2,1)}), bf16[32,48,128]{2,1,0:T(8,128)(2,1)S(1)}, u32[]{:S(2)}, u32[]{:S(2)}) async-start(bf16[32,48,128]{2,1,0:T(8,128)(2,1)} %shard_map.90), calls=%async_computation.1 | async-start | bytes 786432 | tf_op jit(solution)/shard_map/all_to_all | solution.py:455
  53.5 10.7 %shard_map.92 = (f32[512,384]{1,0:T(8,128)}, f32[512,384]{1,0:T(8,128)}, bf16[384,384]{1,0:T(8,128)(2,1)}) custom-call(s32[4]{0:T(128)} %copy-done.5, bf16[528,768]{1,0:T(8,128)(2,1)} %copy-done.10, bf16[528,768]{1,0:T(8,128)(2,1)} %copy-done.11, bf16[8,192,384]{2,1,0:T(8,128)(2,1)} %bitcast.10), custom_call_target="tpu_custom_call" | custom-call | flops 1610612736 | bytes 5242880 | tf_op jit(solution)/shard_map/pallas_call | solution.py:255
  64.3 0.0 copy-start.8
  64.3 4.1 %collective-permute-start.3 = (f32[512,384]{1,0:T(8,128)}, f32[512,384]{1,0:T(8,128)S(1)}, u32[]{:S(2)}, u32[]{:S(2)}) collective-permute-start(f32[512,384]{1,0:T(8,128)} %get-tuple-element.15), channel_id=1, source_target_pairs={{0,1},{1,0},{2,3},{3,2},{4,5},{5,4},{6,7},{7,6},{8,9},{9,8},{10,11... | collective-permute-start | bytes 2359304 | tf_op jit(solution)/shard_map/ppermute | solution.py:414
  68.4 0.0 all-to-all-done.1.got_ref
  68.4 3.0 %shard_map.91 = bf16[32,2,16,128]{3,2,1,0:T(8,128)(2,1)} custom-call(s32[1]{0:T(128)} %bitcast.core_ref, bf16[32,48,128]{2,1,0:T(8,128)(2,1)S(1)} %all-to-all-done.1.got_ref), custom_call_target="tpu_custom_call" | custom-call | flops 536870912 | bytes 1048576 | tf_op jit(solution)/shard_map/pallas_call | solution.py:458
  71.4 10.4 %all-to-all-start.2 = ((bf16[64,16,128]{2,1,0:T(8,128)(2,1)}), bf16[64,16,128]{2,1,0:T(8,128)(2,1)S(1)}, u32[]{:S(2)}, u32[]{:S(2)}) async-start(bf16[64,16,128]{2,1,0:T(8,128)(2,1)} %bitcast.6), calls=%async_computation.2 | async-start | bytes 524288 | tf_op jit(solution)/shard_map/all_to_all | solution.py:462
  81.8 0.0 copy-done.12
  81.8 2.4 %collective-permute-start.4 = (bf16[384,384]{1,0:T(8,128)(2,1)S(1)}, bf16[384,384]{1,0:T(8,128)(2,1)S(1)}, u32[]{:S(2)}, u32[]{:S(2)}) collective-permute-start(bf16[384,384]{1,0:T(8,128)(2,1)S(1)} %copy-done.12), channel_id=1, source_target_pairs={{0,1},{1,0},{2,3},{3,2},{4,5},{5,4},{6,7},{7,6},{8,9},{9,8},{10,11... | collective-permute-start | bytes 884744 | tf_op jit(solution)/shard_map/ppermute | solution.py:414
  84.2 0.0 collective-permute-done.3.got_ref
  84.2 0.0 copy-done.2
  84.2 1.4 %shard_map.93 = (f32[512,384]{1,0:T(8,128)S(1)}, f32[384,128]{1,0:T(8,128)S(1)}, bf16[512,384]{1,0:T(8,128)(2,1)S(1)}, f32[1,384]{1,0:T(1,128)S(1)}) custom-call(s32[4]{0:T(128)S(1)} %copy-done.6, s32[6]{0:T(128)S(1)} %copy-done.9, f32[512,384]{1,0:T(8,128)S(1)} %copy-done.2, f32[512,384]{1,0:T(8,128)S(1)} %collective-permute-done.3.got_ref, ...), custom_call_target="tpu_custom_call" | custom-call | flops 268435456 | bytes 4194304 | tf_op jit(solution)/shard_map/pallas_call | solution.py:465
  85.6 0.7 copy-done.15
  86.3 0.0 collective-permute-done.4.other_w
  86.3 0.7 copy-done.13
  87.0 6.3 %all-to-all-done.2.far_ref = bf16[64,16,128]{2,1,0:T(8,128)(2,1)S(1)} async-done(((bf16[64,16,128]{2,1,0:T(8,128)(2,1)}), bf16[64,16,128]{2,1,0:T(8,128)(2,1)S(1)}, u32[]{:S(2)}, u32[]{:S(2)}) %all-to-all-start.2) | async-done | bytes 262176 | tf_op jit(solution)/shard_map/all_to_all | solution.py:462
  93.3 1.0 copy-done.14
  94.3 0.9 copy-done.16
  95.2 3.7 %shard_map.94 = (bf16[512,768]{1,0:T(8,128)(2,1)}, bf16[512,768]{1,0:T(8,128)(2,1)}) custom-call(s32[1]{0:T(128)} %bitcast.core_ref, bf16[64,16,128]{2,1,0:T(8,128)(2,1)S(1)} %all-to-all-done.2.far_ref, f32[512,384]{1,0:T(8,128)S(1)} %get-tuple-element.17.dense_ref, f32[384,128]{1,0:T(8,128)S(1)} %copy-done.16, ...), custom_call_target="tpu_custom_call" | custom-call | flops 1207959552 | bytes 4194304 | tf_op jit(solution)/shard_map/pallas_call | solution.py:479
  (12 shorter events, 0.0 us)
Async XLA Ops:
  0.6 0.9 copy-start.3
  1.6 0.9 copy-start.4
  2.6 20.2 %collective-permute-start.2 = (bf16[192,384]{1,0:T(8,128)(2,1)S(1)}, bf16[192,384]{1,0:T(8,128)(2,1)S(1)}, u32[]{:S(2)}, u32[]{:S(2)}) collective-permute-start(bf16[192,384]{1,0:T(8,128)(2,1)S(1)} %shard_map.88.own_ref), channel_id=1, source_target_pairs={{0,64},{64,0},{1,65},{65,1},{2,66},{66,2},{3,67},{67,3},{4,68},{68... | collective-permute-start | bytes 442376 | tf_op jit(solution)/shard_map/ppermute | solution.py:103
  10.8 17.3 %collective-permute-start = (s32[1,512]{1,0:T(1,128)}, s32[1,512]{1,0:T(1,128)S(1)}, u32[]{:S(2)}, u32[]{:S(2)}) collective-permute-start(s32[1,512]{1,0:T(1,128)} %param.8), channel_id=1, source_target_pairs={{63,0},{62,1},{61,2},{60,3},{59,4},{58,5},{57,6},{56,7},{55,8},{54... | collective-permute-start | bytes 6152 | tf_op jit(solution)/shard_map/ppermute | solution.py:428
  23.8 4.3 %copy-start.1 = (bf16[1,512,768]{2,1,0:T(8,128)(2,1)S(1)}, bf16[1,512,768]{2,1,0:T(8,128)(2,1)}, u32[]{:S(2)}) copy-start(bf16[1,512,768]{2,1,0:T(8,128)(2,1)} %param.7) | copy-start | bytes 2359300
  23.8 4.3 %copy-start.7 = (f32[768]{0:T(1024)S(1)}, f32[768]{0:T(1024)}, u32[]{:S(2)}) copy-start(f32[768]{0:T(1024)} %gain_ref.2) | copy-start | bytes 9220
  23.9 9.6 %copy-start.9 = (s32[6]{0:T(128)S(1)}, s32[6]{0:T(128)}, u32[]{:S(2)}) copy-start(s32[6]{0:T(128)} %offset_ref.3) | copy-start | bytes 76
  23.9 20.9 %all-to-all-start = ((bf16[4,2,192,384]{3,2,1,0:T(8,128)(2,1)}), bf16[4,2,192,384]{3,2,1,0:T(8,128)(2,1)S(1)}, u32[]{:S(2)}, u32[]{:S(2)}) async-start(bf16[4,2,192,384]{3,2,1,0:T(8,128)(2,1)} %shard_map.89), calls=%async_computation | async-start | bytes 2359296 | tf_op jit(solution)/shard_map/all_to_all | solution.py:111
  28.1 16.7 %copy-start.5 = (s32[4]{0:T(128)}, s32[4]{0:T(128)S(1)}, u32[]{:S(2)}) copy-start(s32[4]{0:T(128)S(1)} %pad_add_fusion.base_ref) | copy-start | bytes 52
  29.2 17.6 %copy-start.10 = (bf16[528,768]{1,0:T(8,128)(2,1)}, bf16[528,768]{1,0:T(8,128)(2,1)S(1)}, u32[]{:S(2)}) copy-start(bf16[528,768]{1,0:T(8,128)(2,1)S(1)} %get-tuple-element.13.own_x) | copy-start | bytes 2433028
  29.2 4.2 %collective-permute-start.1 = (bf16[528,768]{1,0:T(8,128)(2,1)S(1)}, bf16[528,768]{1,0:T(8,128)(2,1)S(1)}, u32[]{:S(2)}, u32[]{:S(2)}) collective-permute-start(bf16[528,768]{1,0:T(8,128)(2,1)S(1)} %get-tuple-element.13.own_x), channel_id=1, source_target_pairs={{0,1},{1,0},{2,3},{3,2},{4,5},{5,4},{6,7},{7,6},{8,9},{9,8},{10,11... | collective-permute-start | bytes 2433032 | tf_op jit(solution)/shard_map/ppermute | solution.py:414
  34.5 0.9 copy-start.11
  44.8 2.0 %copy-start = (bf16[4,2,192,384]{3,2,1,0:T(8,128)(2,1)}, bf16[4,2,192,384]{3,2,1,0:T(8,128)(2,1)S(1)}, u32[]{:S(2)}) copy-start(bf16[4,2,192,384]{3,2,1,0:T(8,128)(2,1)S(1)} %all-to-all-done) | copy-start | bytes 3538948
  46.8 21.6 %all-to-all-start.1 = ((bf16[32,48,128]{2,1,0:T(8,128)(2,1)}), bf16[32,48,128]{2,1,0:T(8,128)(2,1)S(1)}, u32[]{:S(2)}, u32[]{:S(2)}) async-start(bf16[32,48,128]{2,1,0:T(8,128)(2,1)} %shard_map.90), calls=%async_computation.1 | async-start | bytes 786432 | tf_op jit(solution)/shard_map/all_to_all | solution.py:455
  64.3 17.5 %copy-start.12 = (bf16[384,384]{1,0:T(8,128)(2,1)S(1)}, bf16[384,384]{1,0:T(8,128)(2,1)}, u32[]{:S(2)}) copy-start(bf16[384,384]{1,0:T(8,128)(2,1)} %get-tuple-element.21.own_w) | copy-start | bytes 884740
  64.3 19.9 %copy-start.2 = (f32[512,384]{1,0:T(8,128)S(1)}, f32[512,384]{1,0:T(8,128)}, u32[]{:S(2)}) copy-start(f32[512,384]{1,0:T(8,128)} %get-tuple-element.14.keep_ref) | copy-start | bytes 2359300
  64.3 19.9 %copy-start.6 = (s32[4]{0:T(128)S(1)}, s32[4]{0:T(128)}, u32[]{:S(2)}) copy-start(s32[4]{0:T(128)} %copy-done.5) | copy-start | bytes 52
  64.3 19.9 %copy-start.8 = (f32[384]{0:T(512)S(1)}, f32[384]{0:T(512)}, u32[]{:S(2)}) copy-start(f32[384]{0:T(512)} %gain_ref.3) | copy-start | bytes 4612
  64.3 19.9 %collective-permute-start.3 = (f32[512,384]{1,0:T(8,128)}, f32[512,384]{1,0:T(8,128)S(1)}, u32[]{:S(2)}, u32[]{:S(2)}) collective-permute-start(f32[512,384]{1,0:T(8,128)} %get-tuple-element.15), channel_id=1, source_target_pairs={{0,1},{1,0},{2,3},{3,2},{4,5},{5,4},{6,7},{7,6},{8,9},{9,8},{10,11... | collective-permute-start | bytes 2359304 | tf_op jit(solution)/shard_map/ppermute | solution.py:414
  71.4 21.9 %all-to-all-start.2 = ((bf16[64,16,128]{2,1,0:T(8,128)(2,1)}), bf16[64,16,128]{2,1,0:T(8,128)(2,1)S(1)}, u32[]{:S(2)}, u32[]{:S(2)}) async-start(bf16[64,16,128]{2,1,0:T(8,128)(2,1)} %bitcast.6), calls=%async_computation.2 | async-start | bytes 524288 | tf_op jit(solution)/shard_map/all_to_all | solution.py:462
  81.8 4.5 %collective-permute-start.4 = (bf16[384,384]{1,0:T(8,128)(2,1)S(1)}, bf16[384,384]{1,0:T(8,128)(2,1)S(1)}, u32[]{:S(2)}, u32[]{:S(2)}) collective-permute-start(bf16[384,384]{1,0:T(8,128)(2,1)S(1)} %copy-done.12), channel_id=1, source_target_pairs={{0,1},{1,0},{2,3},{3,2},{4,5},{5,4},{6,7},{7,6},{8,9},{9,8},{10,11... | collective-permute-start | bytes 884744 | tf_op jit(solution)/shard_map/ppermute | solution.py:414
  85.6 0.7 copy-start.15
  86.3 0.7 copy-start.13
  93.3 1.0 copy-start.14
  94.3 0.9 copy-start.16

commit v8 on v7

--- a/solution.py
+++ b/solution.py
@@ -112,7 +112,7 @@
     return got.reshape(DP_X * DP_Y, 192, INNER)
 
 
-def norm_kernel(base_ref, x_ref, gain_ref, perm_ref, out_ref, order_ref):
+def norm_kernel(x_ref, gain_ref, out_ref):
     gain = gain_ref[...].reshape(1, D)
     for row in range(0, TOK, 128):
         values = x_ref[row : row + 128, :].astype(F32)
@@ -122,17 +122,6 @@
         out_ref[row : row + 128, :] = (
             centred * lax.rsqrt(variance + eps_norm) * gain
         ).astype(BF16)
-    order_ref[...] = (perm_ref[...] - base_ref[1]).astype(F32)
-    local = jnp.broadcast_to(perm_ref[...] - base_ref[1], (16, TOK))
-    row = lax.broadcasted_iota(jnp.int32, (16, TOK), 0)
-    parts = jnp.where(row == 0, jnp.right_shift(local, 4), jnp.bitwise_and(local, 15))
-    out_ref[TOK : TOK + 16, 0:TOK] = parts.astype(F32).astype(BF16)
-    out_ref[TOK : TOK + 16, TOK:] = jnp.zeros((16, D - TOK), BF16)
-
-
-def order_of(x_ref):
-    parts = x_ref[TOK : TOK + 16, 0:TOK].astype(F32)
-    return parts[0:1, :] * 16.0 + parts[1:2, :]
 
 
 def chosen_rows(view, offset, order):
@@ -150,8 +139,10 @@
     return jnp.where(token == index, 1.0, 0.0).astype(BF16)
 
 
-def pick_kernel(base_ref, offset_ref, own_x, other_x, picked_ref):
-    orders = order_of(own_x), order_of(other_x)
+def pick_kernel(base_ref, offset_ref, own_x, other_x, own_perm, other_perm, picked_ref):
+    orders = [
+        (perm[...] - base_ref[at]).astype(F32) for at, perm in ((1, own_perm), (2, other_perm))
+    ]
     hots = [[], []]
     for head in range(HALF):
         offset = offset_ref[base_ref[0] * HALF + head]
@@ -161,7 +152,7 @@
                 hots[part].append(chosen)
     for part, x_ref in enumerate((own_x, other_x)):
         rows = jnp.dot(
-            jnp.concatenate(hots[part], axis=0), x_ref[0:TOK, :], preferred_element_type=F32
+            jnp.concatenate(hots[part], axis=0), x_ref[...], preferred_element_type=F32
         ).astype(BF16)
         for block in range(2 * HALF):
             at = block * 2 * SPARSE + part * SPARSE
@@ -220,7 +211,7 @@
     unpack_head(flip, packed_ref, lanes, w_ref, 0)
     for part, x_ref in enumerate((own_x, other_x)):
         all_ref[part * TOK : part * TOK + TOK, :] = jnp.dot(
-            x_ref[0:TOK, :], w_ref[...], preferred_element_type=F32
+            x_ref[...], w_ref[...], preferred_element_type=F32
         ).astype(BF16)
     keys = all_ref[:, 0:128]
     lane = lax.broadcasted_iota(jnp.int32, (SEG, 128), 1)
@@ -250,7 +241,7 @@
 
 def near_level(base, own_x, other_x, packed):
     half = shape_of(TOK, HALF * 128, dtype=F32)
-    tiles = pl.BlockSpec((TOK + 16, D), lambda h: (0, 0))
+    tiles = pl.BlockSpec((TOK, D), lambda h: (0, 0))
     part = pl.BlockSpec((TOK, 128), lambda h: (0, h))
     return pl.pallas_call(
         near_kernel,
@@ -312,7 +303,7 @@
     core = base_ref[0]
     width = HALF * HEAD_DIM
     hots = [[], []]
-    order = order_ref[...]
+    order = (order_ref[...] - base_ref[1]).astype(F32)
     for group, near_ref in enumerate((keep_ref, got_ref)):
         dense_ref[:, group * width : (group + 1) * width] = jnp.concatenate(
             [near_ref[:, head * 128 : head * 128 + HEAD_DIM] for head in range(HALF)], axis=1
@@ -427,21 +418,19 @@
     ctx = ("pos", "core")
     own_perm = lax.ppermute(flip_perm, ctx, [(last - r, r) for r in range(2 * POS)])
     packed = gather_weights(core_id, projection, output_weight)
-    own_x, own_order = call(
-        norm_kernel,
-        [shape_of(TOK + 16, D), shape_of(1, TOK, dtype=F32)],
-        [SMEM, VMEM, VMEM, VMEM],
-        moved=2 << 20,
-    )(base, tile_features[0], input_gain, own_perm)
+    other_perm = core_swap(own_perm)
+    own_x = call(norm_kernel, shape_of(TOK, D), [VMEM, VMEM], moved=2 << 20)(
+        tile_features[0], input_gain
+    )
     other_x = core_swap(own_x)
 
     picked = call(
         pick_kernel,
         shape_of(HALF * 128, D),
-        [SMEM, SMEM, VMEM, VMEM],
+        [SMEM, SMEM, VMEM, VMEM, VMEM, VMEM],
         flops=2 * HALF * 128 * SEG * D,
         moved=3 << 20,
-    )(base, head_offsets, own_x, other_x)
+    )(base, head_offsets, own_x, other_x, own_perm, other_perm)
     send = call(
         send_kernel,
         shape_of(POS, 48, 128),
@@ -474,7 +463,7 @@
         flops=1 << 28,
         moved=4 << 20,
         limit=LIMITS[3],
-    )(base, head_offsets, keep, near_got, own_order, output_gain)
+    )(base, head_offsets, keep, near_got, own_perm, output_gain)
 
     plain_view, flipped_view = call(
         output_kernel,

time: 99.6 us -> 101 us (1.014)
  starting transfers between devices: 49.8 us -> 56.2 us
  waiting for transfers between devices: 18 us -> 14.1 us
    all_to_all x1, waiting for transfers between devices: 9.39 us -> 0.01 us  [gather_weights(): got = lax.all_to_all(both, 'x', 0, 0, tiled=True)]
    ppermute x3 -> x4, starting transfers between devices: 8.37 us -> 14.5 us  [core_swap(): return lax.ppermute(block, 'core', [(0, 1), (1, 0)])]
    ppermute x1, waiting for transfers between devices: 0.01 us -> 5.57 us  [gather_weights(): other = lax.ppermute(packed, 'yh', [(0, 1), (1, 0)])]
    all_to_all x1, starting transfers between devices: 6.76 us -> 9.03 us  [layer(): got = lax.all_to_all(send, 'pos', 0, 0, tiled=True)]
    ppermute x3 -> x4, waiting for transfers between devices: 2.29 us -> 0.73 us  [core_swap(): return lax.ppermute(block, 'core', [(0, 1), (1, 0)])]
    ppermute x1, starting transfers between devices: 11.9 us -> 10.4 us  [layer(): lax.ppermute(flip_perm, ctx, [(last - r, r) for r in range(2 * POS)])]
    ppermute x1, waiting for transfers between devices: 0.01 us -> 1.35 us  [layer(): lax.ppermute(flip_perm, ctx, [(last - r, r) for r in range(2 * POS)])]
    unnamed x34 -> x36, local copies, waits for them, and re-layouts: 6.03 us -> 5.15 us
  transfers between devices with their start and end apart: 8 -> 9, of which waited for: 3 -> 5; matrix products, arithmetic and copies ran while one was open for 0% -> 0% of each run, Pallas kernels for 19% -> 17%
where the time goes in v8:
time: 101 us; the launch traced here: 100 us
  starting transfers between devices  56.2 us (56%)
  Pallas kernels  23.6 us (23%)
  waiting for transfers between devices  14.1 us (14%)
  local copies, waits for them, and re-layouts  5.15 us (5%)
    ppermute x4, starting transfers between devices, core_swap(): return lax.ppermute(block, 'core', [(0, 1), (1, 0)])  14.5 us
    pallas_call x1, Pallas kernels, near_level(): pl.pallas_call(near_kernel, out_shape=[half, half, shape_of(INNER, INNER)...  10.7 us
    ppermute x1, starting transfers between devices, layer(): lax.ppermute(flip_perm, ctx, [(last - r, r) for r in range(2 * POS)])  10.4 us
    all_to_all x1, starting transfers between devices, layer(): far = lax.all_to_all(back.reshape(2 * POS, 16, 128), ctx, 0, 0, tiled=True)  10.3 us
    all_to_all x1, starting transfers between devices, layer(): got = lax.all_to_all(send, 'pos', 0, 0, tiled=True)  9.03 us
    ppermute x1, starting transfers between devices, gather_weights(): other = lax.ppermute(packed, 'yh', [(0, 1), (1, 0)])  8.27 us
    all_to_all x1, waiting for transfers between devices, layer(): far = lax.all_to_all(back.reshape(2 * POS, 16, 128), ctx, 0, 0, tiled=True)  6.3 us
    ppermute x1, waiting for transfers between devices, gather_weights(): other = lax.ppermute(packed, 'yh', [(0, 1), (1, 0)])  5.57 us
  transfers between devices with their start and end apart: 9, of which 5 were waited for; matrix products, arithmetic and copies ran while one was open for 0% of the time, Pallas kernels for 17%

profile of v8, /device:TPU:1, one launch (start us, length us, event | category | flops | bytes accessed | tf_op | source)
XLA Modules:
  0.0 100.0 jit_solution(8125629516200953550)
XLA Ops:
  0.6 0.0 copy-start.4
  0.6 0.9 copy-done.4
  1.6 0.9 copy-done.5
  2.5 0.1 shard_map.88.own_ref
  2.6 8.3 %collective-permute-start.3 = (bf16[192,384]{1,0:T(8,128)(2,1)S(1)}, bf16[192,384]{1,0:T(8,128)(2,1)S(1)}, u32[]{:S(2)}, u32[]{:S(2)}) collective-permute-start(bf16[192,384]{1,0:T(8,128)(2,1)S(1)} %shard_map.88.own_ref), channel_id=1, source_target_pairs={{0,64},{64,0},{1,65},{65,1},{2,66},{66,2},{3,67},{67,3},{4,68},{68... | collective-permute-start | bytes 442376 | tf_op jit(solution)/shard_map/ppermute | solution.py:103
  10.8 5.6 %collective-permute-done.3.other_ref = bf16[192,384]{1,0:T(8,128)(2,1)S(1)} collective-permute-done((bf16[192,384]{1,0:T(8,128)(2,1)S(1)}, bf16[192,384]{1,0:T(8,128)(2,1)S(1)}, u32[]{:S(2)}, u32[]{:S(2)}) %collective-permute-start.3) | collective-permute-done | bytes 147488 | tf_op jit(solution)/shard_map/ppermute | solution.py:103
  16.4 1.1 %shard_map.89 = bf16[4,2,192,384]{3,2,1,0:T(8,128)(2,1)} custom-call(bf16[192,384]{1,0:T(8,128)(2,1)S(1)} %shard_map.88.own_ref, bf16[192,384]{1,0:T(8,128)(2,1)S(1)} %collective-permute-done.3.other_ref), custom_call_target="tpu_custom_call" | custom-call | tf_op jit(solution)/shard_map/pallas_call | solution.py:104
  17.5 0.0 copy-start.1
  17.5 0.0 copy-start.8
  17.5 3.7 %all-to-all-start = ((bf16[4,2,192,384]{3,2,1,0:T(8,128)(2,1)}), bf16[4,2,192,384]{3,2,1,0:T(8,128)(2,1)S(1)}, u32[]{:S(2)}, u32[]{:S(2)}) async-start(bf16[4,2,192,384]{3,2,1,0:T(8,128)(2,1)} %shard_map.89), calls=%async_computation | async-start | bytes 2359296 | tf_op jit(solution)/shard_map/all_to_all | solution.py:111
  21.2 0.0 copy-start.17
  21.2 0.0 copy-start.10
  21.2 0.0 copy-done.1
  21.2 0.0 copy-done.8
  21.3 0.5 shard_map.86.own_x
  21.8 0.0 copy-start.2
  21.8 7.3 %collective-permute-start = (bf16[512,768]{1,0:T(8,128)(2,1)S(1)}, bf16[512,768]{1,0:T(8,128)(2,1)S(1)}, u32[]{:S(2)}, u32[]{:S(2)}) collective-permute-start(bf16[512,768]{1,0:T(8,128)(2,1)S(1)} %shard_map.86.own_x), channel_id=1, source_target_pairs={{0,1},{1,0},{2,3},{3,2},{4,5},{5,4},{6,7},{7,6},{8,9},{9,8},{10,11... | collective-permute-start | bytes 2359304 | tf_op jit(solution)/shard_map/ppermute | solution.py:405
  29.1 0.0 copy-done.17
  29.1 10.4 %collective-permute-start.1 = (s32[1,512]{1,0:T(1,128)S(1)}, s32[1,512]{1,0:T(1,128)S(1)}, u32[]{:S(2)}, u32[]{:S(2)}) collective-permute-start(s32[1,512]{1,0:T(1,128)S(1)} %copy-done.17), channel_id=1, source_target_pairs={{63,0},{62,1},{61,2},{60,3},{59,4},{58,5},{57,6},{56,7},{55,8},{54... | collective-permute-start | bytes 6152 | tf_op jit(solution)/shard_map/ppermute | solution.py:419
  39.6 1.3 %collective-permute-done.1.own_perm.order_ref = s32[1,512]{1,0:T(1,128)S(1)} collective-permute-done((s32[1,512]{1,0:T(1,128)S(1)}, s32[1,512]{1,0:T(1,128)S(1)}, u32[]{:S(2)}, u32[]{:S(2)}) %collective-permute-start.1) | collective-permute-done | bytes 2080 | tf_op jit(solution)/shard_map/ppermute | solution.py:419
  40.9 2.3 %collective-permute-start.2 = (s32[1,512]{1,0:T(1,128)S(1)}, s32[1,512]{1,0:T(1,128)S(1)}, u32[]{:S(2)}, u32[]{:S(2)}) collective-permute-start(s32[1,512]{1,0:T(1,128)S(1)} %collective-permute-done.1.own_perm.order_ref), channel_id=1, source_target_pairs={{0,1},{1,0},{2,3},{3,2},{4,5},{5,4},{6,7},{7,6},{8,9},{9,8},{10,11... | collective-permute-start | bytes 6152 | tf_op jit(solution)/shard_map/ppermute | solution.py:405
  43.3 0.1 pad_add_fusion.base_ref
  43.4 0.7 collective-permute-done.2.other_perm
  44.1 0.0 collective-permute-done.other_x
  44.1 0.0 copy-done.10
  44.1 1.1 %shard_map.87.picked_ref = bf16[384,768]{1,0:T(8,128)(2,1)S(1)} custom-call(s32[4]{0:T(128)S(1)} %pad_add_fusion.base_ref, s32[6]{0:T(128)S(1)} %copy-done.10, bf16[512,768]{1,0:T(8,128)(2,1)S(1)} %shard_map.86.own_x, bf16[512,768]{1,0:T(8,128)(2,1)S(1)} %collective-permute-done.other_x, s32[1,512]{1,0:T(1,128)S(1)} %collective-permute-done.1.own_perm.order_ref, ...), custom_call_target="tpu_custom_call" | custom-call | flops 603979776 | bytes 3145728 | tf_op jit(solution)/shard_map/pallas_call | solution.py:427
  45.2 0.0 all-to-all-done
  45.2 0.0 copy-start
  45.2 2.0 %shard_map.90 = bf16[32,48,128]{2,1,0:T(8,128)(2,1)} custom-call(s32[4]{0:T(128)S(1)} %pad_add_fusion.base_ref, bf16[384,768]{1,0:T(8,128)(2,1)S(1)} %shard_map.87.picked_ref, bf16[8,192,384]{2,1,0:T(8,128)(2,1)S(1)} %bitcast.9), custom_call_target="tpu_custom_call" | custom-call | flops 150994944 | bytes 2097152 | tf_op jit(solution)/shard_map/pallas_call | solution.py:434
  47.2 0.0 copy-done.2
  47.2 0.0 copy-done.6
  47.2 9.0 %all-to-all-start.1 = ((bf16[32,48,128]{2,1,0:T(8,128)(2,1)}), bf16[32,48,128]{2,1,0:T(8,128)(2,1)S(1)}, u32[]{:S(2)}, u32[]{:S(2)}) async-start(bf16[32,48,128]{2,1,0:T(8,128)(2,1)} %shard_map.90), calls=%async_computation.1 | async-start | bytes 786432 | tf_op jit(solution)/shard_map/all_to_all | solution.py:444
  56.2 10.7 %shard_map.92 = (f32[512,384]{1,0:T(8,128)}, f32[512,384]{1,0:T(8,128)}, bf16[384,384]{1,0:T(8,128)(2,1)}) custom-call(s32[4]{0:T(128)} %copy-done.6, bf16[512,768]{1,0:T(8,128)(2,1)} %copy-done.2, bf16[512,768]{1,0:T(8,128)(2,1)} %copy-done.11, bf16[8,192,384]{2,1,0:T(8,128)(2,1)} %bitcast.10), custom_call_target="tpu_custom_call" | custom-call | flops 1610612736 | bytes 5242880 | tf_op jit(solution)/shard_map/pallas_call | solution.py:246
  67.0 0.0 copy-start.9
  67.0 2.5 %collective-permute-start.4 = (f32[512,384]{1,0:T(8,128)}, f32[512,384]{1,0:T(8,128)S(1)}, u32[]{:S(2)}, u32[]{:S(2)}) collective-permute-start(f32[512,384]{1,0:T(8,128)} %get-tuple-element.12), channel_id=1, source_target_pairs={{0,1},{1,0},{2,3},{3,2},{4,5},{5,4},{6,7},{7,6},{8,9},{9,8},{10,11... | collective-permute-start | bytes 2359304 | tf_op jit(solution)/shard_map/ppermute | solution.py:405
  69.5 0.2 all-to-all-done.1.got_ref
  69.6 3.0 %shard_map.91 = bf16[32,2,16,128]{3,2,1,0:T(8,128)(2,1)} custom-call(s32[1]{0:T(128)} %bitcast.core_ref, bf16[32,48,128]{2,1,0:T(8,128)(2,1)S(1)} %all-to-all-done.1.got_ref), custom_call_target="tpu_custom_call" | custom-call | flops 536870912 | bytes 1048576 | tf_op jit(solution)/shard_map/pallas_call | solution.py:447
  72.6 10.3 %all-to-all-start.2 = ((bf16[64,16,128]{2,1,0:T(8,128)(2,1)}), bf16[64,16,128]{2,1,0:T(8,128)(2,1)S(1)}, u32[]{:S(2)}, u32[]{:S(2)}) async-start(bf16[64,16,128]{2,1,0:T(8,128)(2,1)} %bitcast.6), calls=%async_computation.2 | async-start | bytes 524288 | tf_op jit(solution)/shard_map/all_to_all | solution.py:451
  82.9 2.4 %collective-permute-start.5 = (bf16[384,384]{1,0:T(8,128)(2,1)S(1)}, bf16[384,384]{1,0:T(8,128)(2,1)S(1)}, u32[]{:S(2)}, u32[]{:S(2)}) collective-permute-start(bf16[384,384]{1,0:T(8,128)(2,1)S(1)} %copy-done.12), channel_id=1, source_target_pairs={{0,1},{1,0},{2,3},{3,2},{4,5},{5,4},{6,7},{7,6},{8,9},{9,8},{10,11... | collective-permute-start | bytes 884744 | tf_op jit(solution)/shard_map/ppermute | solution.py:405
  85.3 0.0 collective-permute-done.4.got_ref
  85.3 1.4 %shard_map.93 = (f32[512,384]{1,0:T(8,128)S(1)}, f32[384,128]{1,0:T(8,128)S(1)}, bf16[512,384]{1,0:T(8,128)(2,1)S(1)}, f32[1,384]{1,0:T(1,128)S(1)}) custom-call(s32[4]{0:T(128)S(1)} %copy-done.7, s32[6]{0:T(128)S(1)} %copy-done.10, f32[512,384]{1,0:T(8,128)S(1)} %copy-done.3, f32[512,384]{1,0:T(8,128)S(1)} %collective-permute-done.4.got_ref, ...), custom_call_target="tpu_custom_call" | custom-call | flops 268435456 | bytes 4194304 | tf_op jit(solution)/shard_map/pallas_call | solution.py:454
  86.7 0.7 copy-done.15
  87.4 0.0 collective-permute-done.5.other_w
  87.4 0.7 copy-done.13
  88.1 6.3 %all-to-all-done.2.far_ref = bf16[64,16,128]{2,1,0:T(8,128)(2,1)S(1)} async-done(((bf16[64,16,128]{2,1,0:T(8,128)(2,1)}), bf16[64,16,128]{2,1,0:T(8,128)(2,1)S(1)}, u32[]{:S(2)}, u32[]{:S(2)}) %all-to-all-start.2) | async-done | bytes 262176 | tf_op jit(solution)/shard_map/all_to_all | solution.py:451
  94.4 1.0 copy-done.14
  95.4 0.9 copy-done.16
  96.3 3.8 %shard_map.94 = (bf16[512,768]{1,0:T(8,128)(2,1)}, bf16[512,768]{1,0:T(8,128)(2,1)}) custom-call(s32[1]{0:T(128)} %bitcast.core_ref, bf16[64,16,128]{2,1,0:T(8,128)(2,1)S(1)} %all-to-all-done.2.far_ref, f32[512,384]{1,0:T(8,128)S(1)} %get-tuple-element.13.dense_ref, f32[384,128]{1,0:T(8,128)S(1)} %copy-done.16, ...), custom_call_target="tpu_custom_call" | custom-call | flops 1207959552 | bytes 4194304 | tf_op jit(solution)/shard_map/pallas_call | solution.py:468
  (16 shorter events, 0.0 us)
Async XLA Ops:
  0.6 0.9 copy-start.4
  1.6 0.9 copy-start.5
  2.6 13.9 %collective-permute-start.3 = (bf16[192,384]{1,0:T(8,128)(2,1)S(1)}, bf16[192,384]{1,0:T(8,128)(2,1)S(1)}, u32[]{:S(2)}, u32[]{:S(2)}) collective-permute-start(bf16[192,384]{1,0:T(8,128)(2,1)S(1)} %shard_map.88.own_ref), channel_id=1, source_target_pairs={{0,64},{64,0},{1,65},{65,1},{2,66},{66,2},{3,67},{67,3},{4,68},{68... | collective-permute-start | bytes 442376 | tf_op jit(solution)/shard_map/ppermute | solution.py:103
  17.5 3.7 %copy-start.1 = (bf16[1,512,768]{2,1,0:T(8,128)(2,1)S(1)}, bf16[1,512,768]{2,1,0:T(8,128)(2,1)}, u32[]{:S(2)}) copy-start(bf16[1,512,768]{2,1,0:T(8,128)(2,1)} %param.7) | copy-start | bytes 2359300
  17.5 3.7 %copy-start.8 = (f32[768]{0:T(1024)S(1)}, f32[768]{0:T(1024)}, u32[]{:S(2)}) copy-start(f32[768]{0:T(1024)} %gain_ref.2) | copy-start | bytes 9220
  17.5 27.7 %all-to-all-start = ((bf16[4,2,192,384]{3,2,1,0:T(8,128)(2,1)}), bf16[4,2,192,384]{3,2,1,0:T(8,128)(2,1)S(1)}, u32[]{:S(2)}, u32[]{:S(2)}) async-start(bf16[4,2,192,384]{3,2,1,0:T(8,128)(2,1)} %shard_map.89), calls=%async_computation | async-start | bytes 2359296 | tf_op jit(solution)/shard_map/all_to_all | solution.py:111
  21.2 7.9 %copy-start.17 = (s32[1,512]{1,0:T(1,128)S(1)}, s32[1,512]{1,0:T(1,128)}, u32[]{:S(2)}) copy-start(s32[1,512]{1,0:T(1,128)} %param.8) | copy-start | bytes 6148
  21.2 22.9 %copy-start.10 = (s32[6]{0:T(128)S(1)}, s32[6]{0:T(128)}, u32[]{:S(2)}) copy-start(s32[6]{0:T(128)} %offset_ref.3) | copy-start | bytes 76
  21.8 25.4 %copy-start.2 = (bf16[512,768]{1,0:T(8,128)(2,1)}, bf16[512,768]{1,0:T(8,128)(2,1)S(1)}, u32[]{:S(2)}) copy-start(bf16[512,768]{1,0:T(8,128)(2,1)S(1)} %shard_map.86.own_x) | copy-start | bytes 2359300
  21.8 22.3 %collective-permute-start = (bf16[512,768]{1,0:T(8,128)(2,1)S(1)}, bf16[512,768]{1,0:T(8,128)(2,1)S(1)}, u32[]{:S(2)}, u32[]{:S(2)}) collective-permute-start(bf16[512,768]{1,0:T(8,128)(2,1)S(1)} %shard_map.86.own_x), channel_id=1, source_target_pairs={{0,1},{1,0},{2,3},{3,2},{4,5},{5,4},{6,7},{7,6},{8,9},{9,8},{10,11... | collective-permute-start | bytes 2359304 | tf_op jit(solution)/shard_map/ppermute | solution.py:405
  29.1 11.8 %collective-permute-start.1 = (s32[1,512]{1,0:T(1,128)S(1)}, s32[1,512]{1,0:T(1,128)S(1)}, u32[]{:S(2)}, u32[]{:S(2)}) collective-permute-start(s32[1,512]{1,0:T(1,128)S(1)} %copy-done.17), channel_id=1, source_target_pairs={{63,0},{62,1},{61,2},{60,3},{59,4},{58,5},{57,6},{56,7},{55,8},{54... | collective-permute-start | bytes 6152 | tf_op jit(solution)/shard_map/ppermute | solution.py:419
  40.9 3.1 %collective-permute-start.2 = (s32[1,512]{1,0:T(1,128)S(1)}, s32[1,512]{1,0:T(1,128)S(1)}, u32[]{:S(2)}, u32[]{:S(2)}) collective-permute-start(s32[1,512]{1,0:T(1,128)S(1)} %collective-permute-done.1.own_perm.order_ref), channel_id=1, source_target_pairs={{0,1},{1,0},{2,3},{3,2},{4,5},{5,4},{6,7},{7,6},{8,9},{9,8},{10,11... | collective-permute-start | bytes 6152 | tf_op jit(solution)/shard_map/ppermute | solution.py:405
  43.4 3.8 %copy-start.6 = (s32[4]{0:T(128)}, s32[4]{0:T(128)S(1)}, u32[]{:S(2)}) copy-start(s32[4]{0:T(128)S(1)} %pad_add_fusion.base_ref) | copy-start | bytes 52
  44.1 3.1 %copy-start.11 = (bf16[512,768]{1,0:T(8,128)(2,1)}, bf16[512,768]{1,0:T(8,128)(2,1)S(1)}, u32[]{:S(2)}) copy-start(bf16[512,768]{1,0:T(8,128)(2,1)S(1)} %collective-permute-done.other_x) | copy-start | bytes 2359300
  45.2 2.0 %copy-start = (bf16[4,2,192,384]{3,2,1,0:T(8,128)(2,1)}, bf16[4,2,192,384]{3,2,1,0:T(8,128)(2,1)S(1)}, u32[]{:S(2)}) copy-start(bf16[4,2,192,384]{3,2,1,0:T(8,128)(2,1)S(1)} %all-to-all-done) | copy-start | bytes 3538948
  47.2 22.4 %all-to-all-start.1 = ((bf16[32,48,128]{2,1,0:T(8,128)(2,1)}), bf16[32,48,128]{2,1,0:T(8,128)(2,1)S(1)}, u32[]{:S(2)}, u32[]{:S(2)}) async-start(bf16[32,48,128]{2,1,0:T(8,128)(2,1)} %shard_map.90), calls=%async_computation.1 | async-start | bytes 786432 | tf_op jit(solution)/shard_map/all_to_all | solution.py:444
  67.0 15.9 %copy-start.12 = (bf16[384,384]{1,0:T(8,128)(2,1)S(1)}, bf16[384,384]{1,0:T(8,128)(2,1)}, u32[]{:S(2)}) copy-start(bf16[384,384]{1,0:T(8,128)(2,1)} %get-tuple-element.17.own_w) | copy-start | bytes 884740
  67.0 18.3 %copy-start.3 = (f32[512,384]{1,0:T(8,128)S(1)}, f32[512,384]{1,0:T(8,128)}, u32[]{:S(2)}) copy-start(f32[512,384]{1,0:T(8,128)} %get-tuple-element.11.keep_ref) | copy-start | bytes 2359300
  67.0 18.3 %copy-start.7 = (s32[4]{0:T(128)S(1)}, s32[4]{0:T(128)}, u32[]{:S(2)}) copy-start(s32[4]{0:T(128)} %copy-done.6) | copy-start | bytes 52
  67.0 18.3 %copy-start.9 = (f32[384]{0:T(512)S(1)}, f32[384]{0:T(512)}, u32[]{:S(2)}) copy-start(f32[384]{0:T(512)} %gain_ref.3) | copy-start | bytes 4612
  67.0 18.3 %collective-permute-start.4 = (f32[512,384]{1,0:T(8,128)}, f32[512,384]{1,0:T(8,128)S(1)}, u32[]{:S(2)}, u32[]{:S(2)}) collective-permute-start(f32[512,384]{1,0:T(8,128)} %get-tuple-element.12), channel_id=1, source_target_pairs={{0,1},{1,0},{2,3},{3,2},{4,5},{5,4},{6,7},{7,6},{8,9},{9,8},{10,11... | collective-permute-start | bytes 2359304 | tf_op jit(solution)/shard_map/ppermute | solution.py:405
  72.6 21.8 %all-to-all-start.2 = ((bf16[64,16,128]{2,1,0:T(8,128)(2,1)}), bf16[64,16,128]{2,1,0:T(8,128)(2,1)S(1)}, u32[]{:S(2)}, u32[]{:S(2)}) async-start(bf16[64,16,128]{2,1,0:T(8,128)(2,1)} %bitcast.6), calls=%async_computation.2 | async-start | bytes 524288 | tf_op jit(solution)/shard_map/all_to_all | solution.py:451
  82.9 4.5 %collective-permute-start.5 = (bf16[384,384]{1,0:T(8,128)(2,1)S(1)}, bf16[384,384]{1,0:T(8,128)(2,1)S(1)}, u32[]{:S(2)}, u32[]{:S(2)}) collective-permute-start(bf16[384,384]{1,0:T(8,128)(2,1)S(1)} %copy-done.12), channel_id=1, source_target_pairs={{0,1},{1,0},{2,3},{3,2},{4,5},{5,4},{6,7},{7,6},{8,9},{9,8},{10,11... | collective-permute-start | bytes 884744 | tf_op jit(solution)/shard_map/ppermute | solution.py:405
  86.7 0.7 copy-start.15
  87.4 0.7 copy-start.13
  94.4 1.0 copy-start.14
  95.4 0.9 copy-start.16

commit v9 on v8

--- a/solution.py
+++ b/solution.py
@@ -1,3 +1,5 @@
+import functools
+
 import jax
 import jax.numpy as jnp
 from jax import lax
@@ -86,28 +88,34 @@
     )
 
 
-def fan_kernel(own_ref, other_ref, both_ref, sems):
+def fan_kernel(at, part_ref, *refs):
+    both_ref, sems = refs[-2:]
     copies = []
     for peer in range(DP_X):
-        for at, part in enumerate((own_ref, other_ref)):
-            copies.append(
-                pltpu.make_async_copy(part, both_ref.at[peer, at], sems.at[peer * 2 + at])
-            )
-            copies[-1].start()
+        copies.append(pltpu.make_async_copy(part_ref, both_ref.at[peer, at], sems.at[peer]))
+        copies[-1].start()
     for copy in copies:
         copy.wait()
+
+
+def fan_out(at, part, *buffer):
+    return pl.pallas_call(
+        functools.partial(fan_kernel, at),
+        out_shape=shape_of(DP_X, DP_Y, 192, INNER),
+        in_specs=[VMEM] + [ANY] * len(buffer),
+        out_specs=ANY,
+        scratch_shapes=[pltpu.SemaphoreType.DMA((DP_X,))],
+        input_output_aliases={1: 0} if buffer else {},
+        compiler_params=pltpu.CompilerParams(vmem_limit_bytes=24 << 20),
+        interpret=INTERPRET,
+    )(part, *buffer)
 
 
 def gather_weights(core, projection, output_weight):
     packed = pack_weights(core, projection, output_weight)
     other = lax.ppermute(packed, "yh", [(0, 1), (1, 0)])
-    both = call(
-        fan_kernel,
-        shape_of(DP_X, DP_Y, 192, INNER),
-        [VMEM, VMEM],
-        [pltpu.SemaphoreType.DMA((2 * DP_X,))],
-        outs=ANY,
-    )(packed, other)
+    both = fan_out(0, packed)
+    both = fan_out(1, other, both)
     got = lax.all_to_all(both, "x", 0, 0, tiled=True)
     return got.reshape(DP_X * DP_Y, 192, INNER)
 

time: 101 us -> 101 us (level)
  transfers between devices with their start and end apart: 9 -> 9, of which waited for: 5 -> 5; matrix products, arithmetic and copies ran while one was open for 0% -> 0% of each run, Pallas kernels for 17% -> 18%
where the time goes in v9:
time: 101 us; the launch traced here: 99.8 us
  starting transfers between devices  56.2 us (56%)
  Pallas kernels  24.2 us (24%)
  waiting for transfers between devices  13.2 us (13%)
  local copies, waits for them, and re-layouts  5.15 us (5%)
    ppermute x4, starting transfers between devices, core_swap(): return lax.ppermute(block, 'core', [(0, 1), (1, 0)])  14.5 us
    pallas_call x1, Pallas kernels, near_level(): pl.pallas_call(near_kernel, out_shape=[half, half, shape_of(INNER, INNER)...  10.7 us
    ppermute x1, starting transfers between devices, layer(): lax.ppermute(flip_perm, ctx, [(last - r, r) for r in range(2 * POS)])  10.4 us
    all_to_all x1, starting transfers between devices, layer(): far = lax.all_to_all(back.reshape(2 * POS, 16, 128), ctx, 0, 0, tiled=True)  10.3 us
    all_to_all x1, starting transfers between devices, layer(): got = lax.all_to_all(send, 'pos', 0, 0, tiled=True)  9.02 us
    ppermute x1, starting transfers between devices, gather_weights(): other = lax.ppermute(packed, 'yh', [(0, 1), (1, 0)])  8.27 us
    all_to_all x1, waiting for transfers between devices, layer(): far = lax.all_to_all(back.reshape(2 * POS, 16, 128), ctx, 0, 0, tiled=True)  6.3 us
    unnamed x36, local copies, waits for them, and re-layouts  5.15 us
  transfers between devices with their start and end apart: 9, of which 5 were waited for; matrix products, arithmetic and copies ran while one was open for 0% of the time, Pallas kernels for 18%

profile of v9, /device:TPU:1, one launch (start us, length us, event | category | flops | bytes accessed | tf_op | source)
XLA Modules:
  0.0 99.8 jit_solution(9643881958078188986)
XLA Ops:
  0.6 0.0 copy-start.4
  0.6 0.9 copy-done.4
  1.6 0.9 copy-done.5
  2.5 0.1 shard_map.88.part_ref
  2.6 8.3 %collective-permute-start.3 = (bf16[192,384]{1,0:T(8,128)(2,1)S(1)}, bf16[192,384]{1,0:T(8,128)(2,1)S(1)}, u32[]{:S(2)}, u32[]{:S(2)}) collective-permute-start(bf16[192,384]{1,0:T(8,128)(2,1)S(1)} %shard_map.88.part_ref), channel_id=1, source_target_pairs={{0,64},{64,0},{1,65},{65,1},{2,66},{66,2},{3,67},{67,3},{4,68},{68... | collective-permute-start | bytes 442376 | tf_op jit(solution)/shard_map/ppermute | solution.py:116
  10.8 0.9 shard_map.89.refs_0_
  11.7 4.7 %collective-permute-done.3.part_ref = bf16[192,384]{1,0:T(8,128)(2,1)S(1)} collective-permute-done((bf16[192,384]{1,0:T(8,128)(2,1)S(1)}, bf16[192,384]{1,0:T(8,128)(2,1)S(1)}, u32[]{:S(2)}, u32[]{:S(2)}) %collective-permute-start.3) | collective-permute-done | bytes 147488 | tf_op jit(solution)/shard_map/ppermute | solution.py:116
  16.4 0.8 shard_map.90
  17.3 0.0 copy-start.1
  17.3 0.0 copy-start.8
  17.3 3.7 %all-to-all-start = ((bf16[4,2,192,384]{3,2,1,0:T(8,128)(2,1)}), bf16[4,2,192,384]{3,2,1,0:T(8,128)(2,1)S(1)}, u32[]{:S(2)}, u32[]{:S(2)}) async-start(bf16[4,2,192,384]{3,2,1,0:T(8,128)(2,1)} %shard_map.90), calls=%async_computation | async-start | bytes 2359296 | tf_op jit(solution)/shard_map/all_to_all | solution.py:119
  21.0 0.0 copy-start.17
  21.0 0.0 copy-start.10
  21.0 0.0 copy-done.1
  21.0 0.0 copy-done.8
  21.0 0.5 shard_map.86.own_x
  21.5 0.0 copy-start.2
  21.5 7.3 %collective-permute-start = (bf16[512,768]{1,0:T(8,128)(2,1)S(1)}, bf16[512,768]{1,0:T(8,128)(2,1)S(1)}, u32[]{:S(2)}, u32[]{:S(2)}) collective-permute-start(bf16[512,768]{1,0:T(8,128)(2,1)S(1)} %shard_map.86.own_x), channel_id=1, source_target_pairs={{0,1},{1,0},{2,3},{3,2},{4,5},{5,4},{6,7},{7,6},{8,9},{9,8},{10,11... | collective-permute-start | bytes 2359304 | tf_op jit(solution)/shard_map/ppermute | solution.py:413
  28.9 0.0 copy-done.17
  28.9 10.4 %collective-permute-start.1 = (s32[1,512]{1,0:T(1,128)S(1)}, s32[1,512]{1,0:T(1,128)S(1)}, u32[]{:S(2)}, u32[]{:S(2)}) collective-permute-start(s32[1,512]{1,0:T(1,128)S(1)} %copy-done.17), channel_id=1, source_target_pairs={{63,0},{62,1},{61,2},{60,3},{59,4},{58,5},{57,6},{56,7},{55,8},{54... | collective-permute-start | bytes 6152 | tf_op jit(solution)/shard_map/ppermute | solution.py:427
  39.4 1.3 %collective-permute-done.1.own_perm.order_ref = s32[1,512]{1,0:T(1,128)S(1)} collective-permute-done((s32[1,512]{1,0:T(1,128)S(1)}, s32[1,512]{1,0:T(1,128)S(1)}, u32[]{:S(2)}, u32[]{:S(2)}) %collective-permute-start.1) | collective-permute-done | bytes 2080 | tf_op jit(solution)/shard_map/ppermute | solution.py:427
  40.7 2.3 %collective-permute-start.2 = (s32[1,512]{1,0:T(1,128)S(1)}, s32[1,512]{1,0:T(1,128)S(1)}, u32[]{:S(2)}, u32[]{:S(2)}) collective-permute-start(s32[1,512]{1,0:T(1,128)S(1)} %collective-permute-done.1.own_perm.order_ref), channel_id=1, source_target_pairs={{0,1},{1,0},{2,3},{3,2},{4,5},{5,4},{6,7},{7,6},{8,9},{9,8},{10,11... | collective-permute-start | bytes 6152 | tf_op jit(solution)/shard_map/ppermute | solution.py:413
  43.0 0.1 pad_add_fusion.base_ref
  43.1 0.7 collective-permute-done.2.other_perm
  43.8 0.0 collective-permute-done.other_x
  43.8 0.0 copy-done.10
  43.8 1.1 %shard_map.87.picked_ref = bf16[384,768]{1,0:T(8,128)(2,1)S(1)} custom-call(s32[4]{0:T(128)S(1)} %pad_add_fusion.base_ref, s32[6]{0:T(128)S(1)} %copy-done.10, bf16[512,768]{1,0:T(8,128)(2,1)S(1)} %shard_map.86.own_x, bf16[512,768]{1,0:T(8,128)(2,1)S(1)} %collective-permute-done.other_x, s32[1,512]{1,0:T(1,128)S(1)} %collective-permute-done.1.own_perm.order_ref, ...), custom_call_target="tpu_custom_call" | custom-call | flops 603979776 | bytes 3145728 | tf_op jit(solution)/shard_map/pallas_call | solution.py:435
  44.9 0.0 all-to-all-done
  44.9 0.0 copy-start
  45.0 2.0 %shard_map.91 = bf16[32,48,128]{2,1,0:T(8,128)(2,1)} custom-call(s32[4]{0:T(128)S(1)} %pad_add_fusion.base_ref, bf16[384,768]{1,0:T(8,128)(2,1)S(1)} %shard_map.87.picked_ref, bf16[8,192,384]{2,1,0:T(8,128)(2,1)S(1)} %bitcast.9), custom_call_target="tpu_custom_call" | custom-call | flops 150994944 | bytes 2097152 | tf_op jit(solution)/shard_map/pallas_call | solution.py:442
  46.9 0.0 copy-done.6
  47.0 9.0 %all-to-all-start.1 = ((bf16[32,48,128]{2,1,0:T(8,128)(2,1)}), bf16[32,48,128]{2,1,0:T(8,128)(2,1)S(1)}, u32[]{:S(2)}, u32[]{:S(2)}) async-start(bf16[32,48,128]{2,1,0:T(8,128)(2,1)} %shard_map.91), calls=%async_computation.1 | async-start | bytes 786432 | tf_op jit(solution)/shard_map/all_to_all | solution.py:452
  56.0 10.7 %shard_map.93 = (f32[512,384]{1,0:T(8,128)}, f32[512,384]{1,0:T(8,128)}, bf16[384,384]{1,0:T(8,128)(2,1)}) custom-call(s32[4]{0:T(128)} %copy-done.6, bf16[512,768]{1,0:T(8,128)(2,1)} %copy-done.2, bf16[512,768]{1,0:T(8,128)(2,1)} %copy-done.11, bf16[8,192,384]{2,1,0:T(8,128)(2,1)} %bitcast.10), custom_call_target="tpu_custom_call" | custom-call | flops 1610612736 | bytes 5242880 | tf_op jit(solution)/shard_map/pallas_call | solution.py:254
  66.7 0.0 copy-start.9
  66.7 2.5 %collective-permute-start.4 = (f32[512,384]{1,0:T(8,128)}, f32[512,384]{1,0:T(8,128)S(1)}, u32[]{:S(2)}, u32[]{:S(2)}) collective-permute-start(f32[512,384]{1,0:T(8,128)} %get-tuple-element.12), channel_id=1, source_target_pairs={{0,1},{1,0},{2,3},{3,2},{4,5},{5,4},{6,7},{7,6},{8,9},{9,8},{10,11... | collective-permute-start | bytes 2359304 | tf_op jit(solution)/shard_map/ppermute | solution.py:413
  69.2 0.1 all-to-all-done.1.got_ref
  69.4 3.0 %shard_map.92 = bf16[32,2,16,128]{3,2,1,0:T(8,128)(2,1)} custom-call(s32[1]{0:T(128)} %bitcast.core_ref, bf16[32,48,128]{2,1,0:T(8,128)(2,1)S(1)} %all-to-all-done.1.got_ref), custom_call_target="tpu_custom_call" | custom-call | flops 536870912 | bytes 1048576 | tf_op jit(solution)/shard_map/pallas_call | solution.py:455
  72.4 10.3 %all-to-all-start.2 = ((bf16[64,16,128]{2,1,0:T(8,128)(2,1)}), bf16[64,16,128]{2,1,0:T(8,128)(2,1)S(1)}, u32[]{:S(2)}, u32[]{:S(2)}) async-start(bf16[64,16,128]{2,1,0:T(8,128)(2,1)} %bitcast.6), calls=%async_computation.2 | async-start | bytes 524288 | tf_op jit(solution)/shard_map/all_to_all | solution.py:459
  82.6 2.4 %collective-permute-start.5 = (bf16[384,384]{1,0:T(8,128)(2,1)S(1)}, bf16[384,384]{1,0:T(8,128)(2,1)S(1)}, u32[]{:S(2)}, u32[]{:S(2)}) collective-permute-start(bf16[384,384]{1,0:T(8,128)(2,1)S(1)} %copy-done.12), channel_id=1, source_target_pairs={{0,1},{1,0},{2,3},{3,2},{4,5},{5,4},{6,7},{7,6},{8,9},{9,8},{10,11... | collective-permute-start | bytes 884744 | tf_op jit(solution)/shard_map/ppermute | solution.py:413
  85.0 0.0 collective-permute-done.4.got_ref
  85.1 1.4 %shard_map.94 = (f32[512,384]{1,0:T(8,128)S(1)}, f32[384,128]{1,0:T(8,128)S(1)}, bf16[512,384]{1,0:T(8,128)(2,1)S(1)}, f32[1,384]{1,0:T(1,128)S(1)}) custom-call(s32[4]{0:T(128)S(1)} %copy-done.7, s32[6]{0:T(128)S(1)} %copy-done.10, f32[512,384]{1,0:T(8,128)S(1)} %copy-done.3, f32[512,384]{1,0:T(8,128)S(1)} %collective-permute-done.4.got_ref, ...), custom_call_target="tpu_custom_call" | custom-call | flops 268435456 | bytes 4194304 | tf_op jit(solution)/shard_map/pallas_call | solution.py:462
  86.5 0.7 copy-done.15
  87.1 0.0 collective-permute-done.5.other_w
  87.1 0.7 copy-done.13
  87.8 6.3 %all-to-all-done.2.far_ref = bf16[64,16,128]{2,1,0:T(8,128)(2,1)S(1)} async-done(((bf16[64,16,128]{2,1,0:T(8,128)(2,1)}), bf16[64,16,128]{2,1,0:T(8,128)(2,1)S(1)}, u32[]{:S(2)}, u32[]{:S(2)}) %all-to-all-start.2) | async-done | bytes 262176 | tf_op jit(solution)/shard_map/all_to_all | solution.py:459
  94.1 1.0 copy-done.14
  95.1 0.9 copy-done.16
  96.0 3.8 %shard_map.95 = (bf16[512,768]{1,0:T(8,128)(2,1)}, bf16[512,768]{1,0:T(8,128)(2,1)}) custom-call(s32[1]{0:T(128)} %bitcast.core_ref, bf16[64,16,128]{2,1,0:T(8,128)(2,1)S(1)} %all-to-all-done.2.far_ref, f32[512,384]{1,0:T(8,128)S(1)} %get-tuple-element.13.dense_ref, f32[384,128]{1,0:T(8,128)S(1)} %copy-done.16, ...), custom_call_target="tpu_custom_call" | custom-call | flops 1207959552 | bytes 4194304 | tf_op jit(solution)/shard_map/pallas_call | solution.py:476
  (17 shorter events, 0.0 us)
Async XLA Ops:
  0.6 0.9 copy-start.4
  1.6 0.9 copy-start.5
  2.6 13.9 %collective-permute-start.3 = (bf16[192,384]{1,0:T(8,128)(2,1)S(1)}, bf16[192,384]{1,0:T(8,128)(2,1)S(1)}, u32[]{:S(2)}, u32[]{:S(2)}) collective-permute-start(bf16[192,384]{1,0:T(8,128)(2,1)S(1)} %shard_map.88.part_ref), channel_id=1, source_target_pairs={{0,64},{64,0},{1,65},{65,1},{2,66},{66,2},{3,67},{67,3},{4,68},{68... | collective-permute-start | bytes 442376 | tf_op jit(solution)/shard_map/ppermute | solution.py:116
  17.3 3.7 %copy-start.1 = (bf16[1,512,768]{2,1,0:T(8,128)(2,1)S(1)}, bf16[1,512,768]{2,1,0:T(8,128)(2,1)}, u32[]{:S(2)}) copy-start(bf16[1,512,768]{2,1,0:T(8,128)(2,1)} %param.7) | copy-start | bytes 2359300
  17.3 3.7 %copy-start.8 = (f32[768]{0:T(1024)S(1)}, f32[768]{0:T(1024)}, u32[]{:S(2)}) copy-start(f32[768]{0:T(1024)} %gain_ref.2) | copy-start | bytes 9220
  17.3 27.7 %all-to-all-start = ((bf16[4,2,192,384]{3,2,1,0:T(8,128)(2,1)}), bf16[4,2,192,384]{3,2,1,0:T(8,128)(2,1)S(1)}, u32[]{:S(2)}, u32[]{:S(2)}) async-start(bf16[4,2,192,384]{3,2,1,0:T(8,128)(2,1)} %shard_map.90), calls=%async_computation | async-start | bytes 2359296 | tf_op jit(solution)/shard_map/all_to_all | solution.py:119
  21.0 7.9 %copy-start.17 = (s32[1,512]{1,0:T(1,128)S(1)}, s32[1,512]{1,0:T(1,128)}, u32[]{:S(2)}) copy-start(s32[1,512]{1,0:T(1,128)} %param.8) | copy-start | bytes 6148
  21.0 22.9 %copy-start.10 = (s32[6]{0:T(128)S(1)}, s32[6]{0:T(128)}, u32[]{:S(2)}) copy-start(s32[6]{0:T(128)} %offset_ref.3) | copy-start | bytes 76
  21.5 25.4 %copy-start.2 = (bf16[512,768]{1,0:T(8,128)(2,1)}, bf16[512,768]{1,0:T(8,128)(2,1)S(1)}, u32[]{:S(2)}) copy-start(bf16[512,768]{1,0:T(8,128)(2,1)S(1)} %shard_map.86.own_x) | copy-start | bytes 2359300
  21.5 22.3 %collective-permute-start = (bf16[512,768]{1,0:T(8,128)(2,1)S(1)}, bf16[512,768]{1,0:T(8,128)(2,1)S(1)}, u32[]{:S(2)}, u32[]{:S(2)}) collective-permute-start(bf16[512,768]{1,0:T(8,128)(2,1)S(1)} %shard_map.86.own_x), channel_id=1, source_target_pairs={{0,1},{1,0},{2,3},{3,2},{4,5},{5,4},{6,7},{7,6},{8,9},{9,8},{10,11... | collective-permute-start | bytes 2359304 | tf_op jit(solution)/shard_map/ppermute | solution.py:413
  28.9 11.8 %collective-permute-start.1 = (s32[1,512]{1,0:T(1,128)S(1)}, s32[1,512]{1,0:T(1,128)S(1)}, u32[]{:S(2)}, u32[]{:S(2)}) collective-permute-start(s32[1,512]{1,0:T(1,128)S(1)} %copy-done.17), channel_id=1, source_target_pairs={{63,0},{62,1},{61,2},{60,3},{59,4},{58,5},{57,6},{56,7},{55,8},{54... | collective-permute-start | bytes 6152 | tf_op jit(solution)/shard_map/ppermute | solution.py:427
  40.7 3.1 %collective-permute-start.2 = (s32[1,512]{1,0:T(1,128)S(1)}, s32[1,512]{1,0:T(1,128)S(1)}, u32[]{:S(2)}, u32[]{:S(2)}) collective-permute-start(s32[1,512]{1,0:T(1,128)S(1)} %collective-permute-done.1.own_perm.order_ref), channel_id=1, source_target_pairs={{0,1},{1,0},{2,3},{3,2},{4,5},{5,4},{6,7},{7,6},{8,9},{9,8},{10,11... | collective-permute-start | bytes 6152 | tf_op jit(solution)/shard_map/ppermute | solution.py:413
  43.1 3.8 %copy-start.6 = (s32[4]{0:T(128)}, s32[4]{0:T(128)S(1)}, u32[]{:S(2)}) copy-start(s32[4]{0:T(128)S(1)} %pad_add_fusion.base_ref) | copy-start | bytes 52
  43.8 3.1 %copy-start.11 = (bf16[512,768]{1,0:T(8,128)(2,1)}, bf16[512,768]{1,0:T(8,128)(2,1)S(1)}, u32[]{:S(2)}) copy-start(bf16[512,768]{1,0:T(8,128)(2,1)S(1)} %collective-permute-done.other_x) | copy-start | bytes 2359300
  44.9 2.0 %copy-start = (bf16[4,2,192,384]{3,2,1,0:T(8,128)(2,1)}, bf16[4,2,192,384]{3,2,1,0:T(8,128)(2,1)S(1)}, u32[]{:S(2)}) copy-start(bf16[4,2,192,384]{3,2,1,0:T(8,128)(2,1)S(1)} %all-to-all-done) | copy-start | bytes 3538948
  47.0 22.4 %all-to-all-start.1 = ((bf16[32,48,128]{2,1,0:T(8,128)(2,1)}), bf16[32,48,128]{2,1,0:T(8,128)(2,1)S(1)}, u32[]{:S(2)}, u32[]{:S(2)}) async-start(bf16[32,48,128]{2,1,0:T(8,128)(2,1)} %shard_map.91), calls=%async_computation.1 | async-start | bytes 786432 | tf_op jit(solution)/shard_map/all_to_all | solution.py:452
  66.7 15.9 %copy-start.12 = (bf16[384,384]{1,0:T(8,128)(2,1)S(1)}, bf16[384,384]{1,0:T(8,128)(2,1)}, u32[]{:S(2)}) copy-start(bf16[384,384]{1,0:T(8,128)(2,1)} %get-tuple-element.17.own_w) | copy-start | bytes 884740
  66.7 18.3 %copy-start.3 = (f32[512,384]{1,0:T(8,128)S(1)}, f32[512,384]{1,0:T(8,128)}, u32[]{:S(2)}) copy-start(f32[512,384]{1,0:T(8,128)} %get-tuple-element.11.keep_ref) | copy-start | bytes 2359300
  66.7 18.3 %copy-start.7 = (s32[4]{0:T(128)S(1)}, s32[4]{0:T(128)}, u32[]{:S(2)}) copy-start(s32[4]{0:T(128)} %copy-done.6) | copy-start | bytes 52
  66.7 18.3 %copy-start.9 = (f32[384]{0:T(512)S(1)}, f32[384]{0:T(512)}, u32[]{:S(2)}) copy-start(f32[384]{0:T(512)} %gain_ref.3) | copy-start | bytes 4612
  66.7 18.3 %collective-permute-start.4 = (f32[512,384]{1,0:T(8,128)}, f32[512,384]{1,0:T(8,128)S(1)}, u32[]{:S(2)}, u32[]{:S(2)}) collective-permute-start(f32[512,384]{1,0:T(8,128)} %get-tuple-element.12), channel_id=1, source_target_pairs={{0,1},{1,0},{2,3},{3,2},{4,5},{5,4},{6,7},{7,6},{8,9},{9,8},{10,11... | collective-permute-start | bytes 2359304 | tf_op jit(solution)/shard_map/ppermute | solution.py:413
  72.4 21.8 %all-to-all-start.2 = ((bf16[64,16,128]{2,1,0:T(8,128)(2,1)}), bf16[64,16,128]{2,1,0:T(8,128)(2,1)S(1)}, u32[]{:S(2)}, u32[]{:S(2)}) async-start(bf16[64,16,128]{2,1,0:T(8,128)(2,1)} %bitcast.6), calls=%async_computation.2 | async-start | bytes 524288 | tf_op jit(solution)/shard_map/all_to_all | solution.py:459
  82.6 4.5 %collective-permute-start.5 = (bf16[384,384]{1,0:T(8,128)(2,1)S(1)}, bf16[384,384]{1,0:T(8,128)(2,1)S(1)}, u32[]{:S(2)}, u32[]{:S(2)}) collective-permute-start(bf16[384,384]{1,0:T(8,128)(2,1)S(1)} %copy-done.12), channel_id=1, source_target_pairs={{0,1},{1,0},{2,3},{3,2},{4,5},{5,4},{6,7},{7,6},{8,9},{9,8},{10,11... | collective-permute-start | bytes 884744 | tf_op jit(solution)/shard_map/ppermute | solution.py:413
  86.4 0.7 copy-start.15
  87.1 0.7 copy-start.13
  94.1 1.0 copy-start.14
  95.1 0.9 copy-start.16
